TPU v7x, 128 devices: a whole 4x4x4 slice. The times are simulated.
128 devices in a mesh: seq: 8 (over x, core), tensor: 16 (over z, y).
Axes of the slice: x: 4, y: 4, z: 4, core: 2. Of those that a mesh axis runs over, the one named last changes fastest.
Arguments:
- hidden: bfloat16 [1024, 53248], P('seq', 'tensor'), may hold values from -200 to 200, as said below
- down_int: bfloat16 [53248, 16384], P('tensor', 'seq'), may hold values from -8 to 7, as said below
- w_scale: float32 [16384], P('seq'), may hold values from 0.0004 to 0.0025
- had_small: int32 [52, 52], replicated, may hold values from -1 to 1, as said below
Outputs:
- mixed: bfloat16 [1024, 16384], P('tensor', 'seq')
- act_scale: float32 [1024], P('seq')
Inputs may be any that keep to these rules, and one draw needn't show every extreme that they name: `hidden`: activations with unequal token and channel scales. `down_int`: whole numbers. A Hadamard matrix: entries -1 or +1 and had_small had_small^T = 52 I.
All inputs are finite; a program needn't handle non-finite values.
Results may differ from a plain program's by a relative error of at most 0.0011.
Values may be sent and summed in bfloat16 or wider, within the bound.
No kernel may reach another device: no remote copies, remote signals or barrier semaphores. Data moves between devices by JAX's collectives and lax.ppermute only.
A program may use at most 192 MiB of HBM per device.

v0:
```python
import functools
import math

import jax
import jax.numpy as jnp
from jax import lax
from jax.experimental import pallas as pl
from jax.experimental.pallas import tpu as pltpu
from jax.sharding import PartitionSpec as P

FF = 53248
HAD = 52

clip_ratio = 0.9
epsilon = 1e-05

F32, BF16, I16, I32 = jnp.float32, jnp.bfloat16, jnp.int16, jnp.int32
LANES = 128
CODE_TOP = 32767.0
SUM_TOP = 32700.0
BLOCK = 512


def vmem():
    return pl.BlockSpec(memory_space=pltpu.VMEM)


def smem():
    return pl.BlockSpec(memory_space=pltpu.SMEM)


def params(mebibytes=12, **more):
    return pltpu.CompilerParams(vmem_limit_bytes=mebibytes * 1024 * 1024, **more)


def parity_sign(left, right, bits):
    both = left & right
    parity = jnp.zeros(both.shape, I32)
    for shift_bit in range(bits):
        parity = parity ^ (both >> shift_bit & 1)
    return 1 - 2 * parity


def iota(shape, dim):
    return lax.broadcasted_iota(I32, shape, dim)


def block_of(index):
    return jnp.floor((index.astype(F32) + 0.5) * (1.0 / HAD)).astype(I32)


def rotate_kernel(x_ref, had_ref, w_ref, code_ref, held_ref, matrix, mixed, sem):
    fetch = pltpu.make_async_copy(w_ref, held_ref, sem)
    fetch.start()
    width = matrix.shape[0]
    group = 4 * HAD
    row = iota((group, HAD), 0)
    pick_row = (row - HAD * block_of(row) == iota((group, HAD), 1)).astype(BF16)
    lane = iota((HAD, width), 1)
    pick_lane = (lane - HAD * block_of(lane) == iota((HAD, width), 0)).astype(BF16)
    small = had_ref[...].astype(F32).astype(BF16)
    tiled = jnp.dot(small, pick_lane, preferred_element_type=F32).astype(BF16)
    base = jnp.dot(pick_row, tiled, preferred_element_type=F32)
    row_block = block_of(iota((group, width), 0))
    lane_block = block_of(iota((group, width), 1))
    base = base * parity_sign(row_block, lane_block & 3, 2).astype(F32)
    line_block = block_of(iota((8, width), 1)) >> 2
    lines = parity_sign(iota((8, width), 0), line_block, 3).astype(F32)
    for g in range(width // group):
        matrix[g * group : (g + 1) * group, :] = (base * lines[g : g + 1, :]).astype(BF16)
    rows = x_ref.shape[0]
    count = rows // 8
    for half in range(2):
        span = slice(half * width, (half + 1) * width)
        mixed[:, span] = jnp.dot(x_ref[:, span], matrix[...], preferred_element_type=F32)
    norm_factor = jnp.float32(1.0 / math.sqrt(FF))
    top = jnp.zeros((8, LANES), F32)
    for tile in range(width // LANES):
        columns = [slice(half * width + tile * LANES, half * width + (tile + 1) * LANES) for half in range(2)]
        values = [mixed[8 * t : 8 * t + 8, span] for span in columns for t in range(count)]
        step = 1
        while step < len(values):
            for low in range(len(values)):
                if not low & step:
                    a, b = values[low], values[low | step]
                    values[low], values[low | step] = a + b, a - b
            step *= 2
        for index, value in enumerate(values):
            half, t = index // count, index % count
            value = value * norm_factor
            top = jnp.maximum(top, jnp.abs(value))
            mixed[8 * t : 8 * t + 8, columns[half]] = value
    peak = jnp.max(top, axis=1, keepdims=True)
    act_scale = clip_ratio / 7.0 * (peak + epsilon)
    inverse = jnp.broadcast_to(1.0 / act_scale, (8, LANES))
    for t in range(count // 2):
        for tile in range(2 * width // LANES):
            span = slice(tile * LANES, (tile + 1) * LANES)
            halves = []
            for part in range(2):
                start = 16 * t + 8 * part
                quant = jnp.clip(mixed[start : start + 8, span] * inverse, -8.0, 7.0)
                root = jnp.sqrt(jnp.abs(quant)) * (CODE_TOP / math.sqrt(8.0))
                halves.append(jnp.round(jnp.where(quant < 0, -root, root)))
            code_ref[16 * t : 16 * t + 16, span] = jnp.concatenate(halves, 0).astype(I32).astype(I16)
    rest = jnp.broadcast_to(act_scale, (8, LANES)) * 4.0
    lane = iota((8, LANES), 1)
    pieces = jnp.zeros((8, LANES), F32)
    for index in range(4):
        whole = jnp.floor(rest)
        pieces = jnp.where(lane == index, whole, pieces)
        rest = (rest - whole) * 16384.0
    extra = jnp.concatenate([pieces, pieces], 0).astype(I32).astype(I16)
    for t in range(count // 2):
        code_ref[16 * t : 16 * t + 16, 2 * width :] = extra
    fetch.wait()


def scale_of(pieces):
    parts = pieces.astype(I32).astype(F32)
    total = parts[:, 3:4] * 2.0**-42 + parts[:, 2:3] * 2.0**-28
    return (total + parts[:, 1:2] * 2.0**-14 + parts[:, 0:1]) * 0.25


def rotate(x, had_small, weight):
    rows, columns = x.shape
    return pl.pallas_call(
        rotate_kernel,
        out_shape=[
            jax.ShapeDtypeStruct((rows, columns + LANES), I16),
            jax.ShapeDtypeStruct(weight.shape, weight.dtype),
        ],
        in_specs=[vmem(), vmem(), pl.BlockSpec(memory_space=pltpu.HBM)],
        out_specs=[vmem(), vmem()],
        scratch_shapes=[
            pltpu.VMEM((columns // 2, columns // 2), BF16),
            pltpu.VMEM((rows, columns), F32),
            pltpu.SemaphoreType.DMA,
        ],
        compiler_params=params(34),
        name="rotate",
    )(x, had_small, weight)


def product_kernel(at_ref, *refs):
    codes, w_ref = refs[:4], refs[4]
    sends, kept, lhs, total, scale = refs[5:8], refs[8], refs[9], refs[10], refs[11]
    rows = scale.shape[0] // 4
    size = rows // 2
    depth, width = w_ref.shape
    for index, ref in enumerate(codes):
        base = index * rows
        scale[base : base + rows, :] = jnp.broadcast_to(scale_of(ref[:, depth:]), (rows, LANES))
        for tile in range(depth // LANES):
            span = slice(tile * LANES, (tile + 1) * LANES)
            level = ref[:, span].astype(I32).astype(F32)
            quant = level * jnp.abs(level) * (8.0 / CODE_TOP**2)
            high = quant.astype(BF16)
            low = (quant - high.astype(F32)).astype(BF16)
            lhs[base : base + rows, span] = high
            lhs[4 * rows + base : 4 * rows + base + rows, span] = low

    def columns(step, carry):
        start = pl.multiple_of(step * BLOCK, BLOCK)
        both = jnp.dot(lhs[...], w_ref[:, pl.ds(start, BLOCK)], preferred_element_type=F32)
        total[:, pl.ds(start, BLOCK)] = (both[: 4 * rows] + both[4 * rows :]) * scale[:, 0:1]
        return carry

    lax.fori_loop(0, width // BLOCK, columns, 0)
    for d in range(4):
        for group in range(2):
            first = pl.multiple_of(group * 2 * rows + at_ref[4 + d] * size, size)
            value = total[pl.ds(first, size), :]
            span = slice(group * size, (group + 1) * size)
            if d == 0:
                kept[span, :] = value
            else:
                pack(value, sends[d - 1], span)


def product(at, codes, weight):
    rows = codes[0][0].shape[0] if codes[0][1] is None else codes[0][0].shape[0] // 2
    depth, width = weight.shape
    message = jax.ShapeDtypeStruct((rows, width + LANES), I16)
    specs = [
        pl.BlockSpec((rows, depth + LANES), functools.partial(lambda index, n: (index, 0), index or 0))
        for _, index in codes
    ]
    return pl.pallas_call(
        product_kernel,
        grid=(1,),
        out_shape=[message] * 3 + [jax.ShapeDtypeStruct((rows, width), F32)],
        in_specs=[smem()] + specs + [vmem()],
        out_specs=[pl.BlockSpec(message.shape, lambda n: (0, 0))] * 3
        + [pl.BlockSpec((rows, width), lambda n: (0, 0))],
        scratch_shapes=[
            pltpu.VMEM((8 * rows, depth), BF16),
            pltpu.VMEM((4 * rows, width), F32),
            pltpu.VMEM((4 * rows, LANES), F32),
        ],
        compiler_params=params(26),
        cost_estimate=pl.CostEstimate(
            flops=16 * rows * depth * width,
            bytes_accessed=2 * depth * width,
            transcendentals=0,
        ),
    )(at, *[array for array, _ in codes], weight)


def pack(value, out_ref, span=slice(None)):
    width = value.shape[-1]
    top = jnp.max(jnp.abs(value), axis=-1, keepdims=True)
    level = jnp.ceil(jnp.log2(jnp.maximum(top, 1e-30)) * 256.0)
    code = jnp.round(value * (jnp.exp2(level * (-1.0 / 256.0)) * SUM_TOP))
    code = jnp.clip(code, -32767.0, 32767.0)
    out_ref[span, :width] = code.astype(I32).astype(I16)
    out_ref[span, width:] = jnp.broadcast_to(level, (value.shape[0], LANES)).astype(I32).astype(I16)


def unpack(code):
    width = code.shape[-1] - LANES
    level = code[:, width : width + 1].astype(I32).astype(F32)
    factor = jnp.exp2(level * (1.0 / 256.0)) * (1.0 / SUM_TOP)
    return code[:, :width].astype(I32).astype(F32) * factor


def collect_kernel(at_ref, *refs):
    sends, own_ref, held = refs[16:19], refs[19], refs[20]
    half = own_ref.shape[0] // 2
    for chunk in range(4):
        kept, a, b, c = refs[4 * chunk : 4 * chunk + 4]
        value = kept[...] + unpack(a[...]) + unpack(b[...]) + unpack(c[...])
        for group in range(2):
            if chunk in (0, 3):
                held[chunk, group * half : (group + 1) * half, :] = value[group * half : (group + 1) * half]
            else:
                held[1 + group, (chunk - 1) * half : chunk * half, :] = value[group * half : (group + 1) * half]
    for d in range(4):
        value = held[at_ref[d]]
        if d == 0:
            own_ref[...] = value
        else:
            pack(value, sends[d - 1])


def collect(at, parts):
    size, width = parts[0].shape
    message = jax.ShapeDtypeStruct((size, width + LANES), I16)
    return pl.pallas_call(
        collect_kernel,
        out_shape=[message] * 3 + [jax.ShapeDtypeStruct((size, width), F32)],
        in_specs=[smem()] + [vmem()] * 16,
        out_specs=[vmem()] * 4,
        scratch_shapes=[pltpu.VMEM((4, size, width), F32)],
        compiler_params=params(16),
        name="collect",
    )(at, *parts)


def finish_kernel(own_ref, w_ref, a, b, c, out_ref):
    total = own_ref[...] + unpack(a[...]) + unpack(b[...]) + unpack(c[...])
    out_ref[...] = (total * w_ref[...]).astype(BF16)


def finish(own, w_scale, got):
    return pl.pallas_call(
        finish_kernel,
        out_shape=jax.ShapeDtypeStruct(own.shape, BF16),
        in_specs=[vmem()] * 5,
        out_specs=vmem(),
        compiler_params=params(),
        name="finish",
    )(own, w_scale, *got)


def along_x(block, apart):
    return lax.ppermute(block, "seq", [(i, (i + 2 * apart) % 8) for i in range(8)])


def other_core(block):
    return lax.ppermute(block, "seq", [(i, i ^ 1) for i in range(8)])


def along_z(blocks):
    return [
        lax.ppermute(block, "tensor", [(i, (i + 4 * apart) % 16) for i in range(16)])
        for apart, block in enumerate(blocks, 1)
    ]


def along_y(blocks):
    got = []
    for apart, block in enumerate(blocks, 1):
        route = [(i, i // 4 * 4 + (i + apart) % 4) for i in range(16)]
        got.append(lax.ppermute(block, "tensor", route))
    return got


def step(hidden, down_int, w_scale, had_small):
    tokens, columns = hidden.shape
    ranks = lax.axis_size("tensor")
    half, quarter = tokens // 2, tokens // 4
    seq, tensor = lax.axis_index("seq"), lax.axis_index("tensor")
    x, core, z, y = seq // 2, seq % 2, tensor // 4, tensor % 4
    away = jnp.arange(4, dtype=I32)
    slot = (z + away - x) % 4
    slot = jnp.where(slot == 2, 3, jnp.where(slot == 3, 2, slot))
    place = ((y + away) % 4) ^ (2 * core)
    at = jnp.concatenate([slot, place]).astype(I32)
    at, hidden = lax.optimization_barrier((at, hidden))

    ordered = hidden.reshape(2, 2, quarter, columns).swapaxes(0, 1)
    sent = ordered.reshape(ranks, tokens // ranks, columns)
    whole = lax.all_to_all(sent, "tensor", split_axis=0, concat_axis=0, tiled=True)
    code, weight = rotate(whole.reshape(tokens, columns), had_small, down_int)
    code = code.reshape(ranks, tokens // ranks, columns + LANES)
    back = lax.all_to_all(code, "tensor", split_axis=0, concat_axis=0, tiled=True)
    own = back.reshape(tokens, columns + LANES)
    scales = scale_of(own[:, columns : columns + LANES])[:, 0]
    act_scale = scales.reshape(2, 2, quarter).swapaxes(0, 1).reshape(tokens)

    own_c = other_core(own)
    below_0, above_0 = along_x(own[:half], 1), along_x(own[:half], -1)
    below_1, above_1 = along_x(own[half:], 1), along_x(own[half:], -1)
    codes = [(own, 0), (own_c, 0), (own, 1), (own_c, 1)]
    *sends, kept_0 = product(at, codes, weight)
    sends, below_0, above_0 = lax.optimization_barrier((sends, below_0, above_0))
    got_0 = along_y(sends)
    far_0 = along_x(below_0, 1)
    codes = [above_0, other_core(above_0), below_0, other_core(below_0)]
    *sends, kept_1 = product(at, [(code, None) for code in codes], weight)
    sends, below_1, above_1 = lax.optimization_barrier((sends, below_1, above_1))
    got_1 = along_y(sends)
    far_1 = along_x(above_1, -1)
    codes = [above_1, other_core(above_1), below_1, other_core(below_1)]
    *sends, kept_2 = product(at, [(code, None) for code in codes], weight)
    sends, far_0, far_1 = lax.optimization_barrier((sends, far_0, far_1))
    got_2 = along_y(sends)
    codes = [far_0, other_core(far_0), far_1, other_core(far_1)]
    *sends, kept_3 = product(at, [(code, None) for code in codes], weight)
    got_3 = along_y(sends)
    parts = [kept_0, *got_0, kept_1, *got_1, kept_2, *got_2, kept_3, *got_3]
    *sends, own_sum = collect(at, parts)
    mixed = finish(own_sum, w_scale[None, :], along_z(sends))
    return (mixed, act_scale)


def solution(mesh):
    return jax.shard_map(
        step,
        mesh=mesh,
        in_specs=(P("seq", "tensor"), P("tensor", "seq"), P("seq"), P()),
        out_specs=(P("tensor", "seq"), P("seq")),
        check_vma=False,
    )
```

profile of v0, /device:TPU:0, one launch (start us, length us, event | category | flops | bytes accessed | tf_op | source)
XLA Modules:
  0.0 166.3 jit_solution(14004395548986880369)
XLA Ops:
  2.0 23.0 %all_to_all.10 = bf16[16,8,3328]{2,1,0:T(8,128)(2,1)S(1)} all-to-all(bf16[16,8,3328]{2,1,0:T(8,128)(2,1)S(1)} %bitcast.20), channel_id=1, replica_groups=mesh['seq'=8,'tensor'=16] {'tensor'}, dimensions={0} | all-to-all | bytes 1703936 | tf_op jit(solution)/shard_map/all_to_all | solution.py:314
  25.7 4.9 %rotate.1 = (s16[128,3456]{1,0:T(8,128)(2,1)S(1)}, bf16[3328,2048]{1,0:T(8,128)(2,1)S(1)}) custom-call(bf16[128,3328]{1,0:T(8,128)(2,1)S(1)} %bitcast.17, s32[52,52]{1,0:T(8,128)S(1)} %copy-done, bf16[3328,2048]{1,0:T(8,128)(2,1)} %w_ref.1), custom_call_target="tpu_custom_call" | custom-call | tf_op jit(solution)/shard_map/rotate/pallas_call | solution.py:127
  30.6 17.7 %all_to_all.11 = s16[16,8,3456]{2,1,0:T(8,128)(2,1)S(1)} all-to-all(s16[16,8,3456]{2,1,0:T(8,128)(2,1)S(1)} %bitcast.18), channel_id=1, replica_groups=mesh['seq'=8,'tensor'=16] {'tensor'}, dimensions={0} | all-to-all | bytes 1769472 | tf_op jit(solution)/shard_map/all_to_all | solution.py:317
  48.4 2.8 %collective-permute-start.2 = (s16[64,3456]{1,0:T(8,128)(2,1)S(1)}, s16[64,3456]{1,0:T(8,128)(2,1)S(1)}, u32[]{:S(2)}, u32[]{:S(2)}) collective-permute-start(s16[64,3456]{1,0:T(8,128)(2,1)S(1)} %get-tuple-element.81), channel_id=1, source_target_pairs={{0,96},{16,112},{32,0},{48,16},{64,32},{80,48},{96,64},{112,80},{1... | collective-permute-start | bytes 1327112 | tf_op jit(solution)/shard_map/ppermute | solution.py:277
  51.2 9.9 %shard_map.59 = (s16[64,2176]{1,0:T(8,128)(2,1)S(1)}, s16[64,2176]{1,0:T(8,128)(2,1)S(1)}, s16[64,2176]{1,0:T(8,128)(2,1)S(1)}, f32[64,2048]{1,0:T(8,128)S(1)}) custom-call(s32[8]{0:T(128)S(1)} %pad_add_fusion.at_ref, s16[128,3456]{1,0:T(8,128)(2,1)S(1)} %bitcast.14, s16[128,3456]{1,0:T(8,128)(2,1)S(1)} %collective-permute-done.refs_1_.refs_3_, ...), custom_call_target="tpu_custom_call" | custom-call | flops 6979321856 | bytes 13631488 | tf_op jit(solution)/shard_map/pallas_call | solution.py:189
  61.3 3.4 %collective-permute-done.1.refs_2_ = s16[64,3456]{1,0:T(8,128)(2,1)S(1)} collective-permute-done((s16[64,3456]{1,0:T(8,128)(2,1)S(1)}, s16[64,3456]{1,0:T(8,128)(2,1)S(1)}, u32[]{:S(2)}, u32[]{:S(2)}) %collective-permute-start.1) | collective-permute-done | bytes 442400 | tf_op jit(solution)/shard_map/ppermute | solution.py:277
  65.5 1.7 %collective-permute-start.8 = (s16[64,3456]{1,0:T(8,128)(2,1)S(1)}, s16[64,3456]{1,0:T(8,128)(2,1)S(1)}, u32[]{:S(2)}, u32[]{:S(2)}) collective-permute-start(s16[64,3456]{1,0:T(8,128)(2,1)S(1)} %get-tuple-element.80), channel_id=1, source_target_pairs={{0,32},{16,48},{32,64},{48,80},{64,96},{80,112},{96,0},{112,16},{1... | collective-permute-start | bytes 1327112 | tf_op jit(solution)/shard_map/ppermute | solution.py:277
  67.3 9.9 %shard_map.60 = (s16[64,2176]{1,0:T(8,128)(2,1)S(1)}, s16[64,2176]{1,0:T(8,128)(2,1)S(1)}, s16[64,2176]{1,0:T(8,128)(2,1)S(1)}, f32[64,2048]{1,0:T(8,128)S(1)}) custom-call(s32[8]{0:T(128)S(1)} %pad_add_fusion.at_ref, s16[64,3456]{1,0:T(8,128)(2,1)S(1)} %collective-permute-done.2.refs_0_, s16[64,3456]{1,0:T(8,128)(2,1)S(1)} %collective-permute-done.6.refs_1_, ...), custom_call_target="tpu_custom_call" | custom-call | flops 6979321856 | bytes 13631488 | tf_op jit(solution)/shard_map/pallas_call | solution.py:189
  79.6 2.7 %collective-permute-start.16 = (s16[64,3456]{1,0:T(8,128)(2,1)S(1)}, s16[64,3456]{1,0:T(8,128)(2,1)S(1)}, u32[]{:S(2)}, u32[]{:S(2)}) collective-permute-start(s16[64,3456]{1,0:T(8,128)(2,1)S(1)} %collective-permute-done.9.refs_0_), channel_id=1, source_target_pairs={{0,96},{16,112},{32,0},{48,16},{64,32},{80,48},{96,64},{112,80},{1... | collective-permute-start | bytes 1327112 | tf_op jit(solution)/shard_map/ppermute | solution.py:277
  82.3 9.9 %shard_map.61 = (s16[64,2176]{1,0:T(8,128)(2,1)S(1)}, s16[64,2176]{1,0:T(8,128)(2,1)S(1)}, s16[64,2176]{1,0:T(8,128)(2,1)S(1)}, f32[64,2048]{1,0:T(8,128)S(1)}) custom-call(s32[8]{0:T(128)S(1)} %pad_add_fusion.at_ref, s16[64,3456]{1,0:T(8,128)(2,1)S(1)} %collective-permute-done.9.refs_0_, s16[64,3456]{1,0:T(8,128)(2,1)S(1)} %collective-permute-done.13.refs_1_, ...), custom_call_target="tpu_custom_call" | custom-call | flops 6979321856 | bytes 13631488 | tf_op jit(solution)/shard_map/pallas_call | solution.py:189
  94.8 1.5 collective-permute-start.5
  96.3 12.4 %collective-permute-done.3.refs_1_ = s16[64,2176]{1,0:T(8,128)(2,1)S(1)} collective-permute-done((s16[64,2176]{1,0:T(8,128)(2,1)S(1)}, s16[64,2176]{1,0:T(8,128)(2,1)S(1)}, u32[]{:S(2)}, u32[]{:S(2)}) %collective-permute-start.3) | collective-permute-done | bytes 278560 | tf_op jit(solution)/shard_map/ppermute | solution.py:295
  109.7 2.3 %collective-permute-start.12 = (s16[64,2176]{1,0:T(8,128)(2,1)S(1)}, s16[64,2176]{1,0:T(8,128)(2,1)S(1)}, u32[]{:S(2)}, u32[]{:S(2)}) collective-permute-start(s16[64,2176]{1,0:T(8,128)(2,1)S(1)} %get-tuple-element.60), channel_id=1, source_target_pairs={{0,3},{1,0},{2,1},{3,2},{4,7},{5,4},{6,5},{7,6},{8,11},{9,8},{10,9... | collective-permute-start | bytes 835592 | tf_op jit(solution)/shard_map/ppermute | solution.py:295
  112.9 9.9 %shard_map.62 = (s16[64,2176]{1,0:T(8,128)(2,1)S(1)}, s16[64,2176]{1,0:T(8,128)(2,1)S(1)}, s16[64,2176]{1,0:T(8,128)(2,1)S(1)}, f32[64,2048]{1,0:T(8,128)S(1)}) custom-call(s32[8]{0:T(128)S(1)} %pad_add_fusion.at_ref, s16[64,3456]{1,0:T(8,128)(2,1)S(1)} %collective-permute-done.15.refs_0_, s16[64,3456]{1,0:T(8,128)(2,1)S(1)} %collective-permute-done.20.refs_1_, ...), custom_call_target="tpu_custom_call" | custom-call | flops 6979321856 | bytes 13631488 | tf_op jit(solution)/shard_map/pallas_call | solution.py:189
  122.8 2.1 %collective-permute-start.18 = (s16[64,2176]{1,0:T(8,128)(2,1)S(1)}, s16[64,2176]{1,0:T(8,128)(2,1)S(1)}, u32[]{:S(2)}, u32[]{:S(2)}) collective-permute-start(s16[64,2176]{1,0:T(8,128)(2,1)S(1)} %get-tuple-element.68), channel_id=1, source_target_pairs={{0,2},{1,3},{2,0},{3,1},{4,6},{5,7},{6,4},{7,5},{8,10},{9,11},{10,... | collective-permute-start | bytes 835592 | tf_op jit(solution)/shard_map/ppermute | solution.py:295
  124.8 2.6 %collective-permute-start.19 = (s16[64,2176]{1,0:T(8,128)(2,1)S(1)}, s16[64,2176]{1,0:T(8,128)(2,1)S(1)}, u32[]{:S(2)}, u32[]{:S(2)}) collective-permute-start(s16[64,2176]{1,0:T(8,128)(2,1)S(1)} %get-tuple-element.69), channel_id=1, source_target_pairs={{0,3},{1,0},{2,1},{3,2},{4,7},{5,4},{6,5},{7,6},{8,11},{9,8},{10,9... | collective-permute-start | bytes 835592 | tf_op jit(solution)/shard_map/ppermute | solution.py:295
  127.5 1.5 collective-permute-start.23
  129.0 7.3 %collective-permute-done.17.refs_9_ = s16[64,2176]{1,0:T(8,128)(2,1)S(1)} collective-permute-done((s16[64,2176]{1,0:T(8,128)(2,1)S(1)}, s16[64,2176]{1,0:T(8,128)(2,1)S(1)}, u32[]{:S(2)}, u32[]{:S(2)}) %collective-permute-start.17) | collective-permute-done | bytes 278560 | tf_op jit(solution)/shard_map/ppermute | solution.py:295
  136.4 3.6 %collective-permute-done.19.refs_11_ = s16[64,2176]{1,0:T(8,128)(2,1)S(1)} collective-permute-done((s16[64,2176]{1,0:T(8,128)(2,1)S(1)}, s16[64,2176]{1,0:T(8,128)(2,1)S(1)}, u32[]{:S(2)}, u32[]{:S(2)}) %collective-permute-start.19) | collective-permute-done | bytes 278560 | tf_op jit(solution)/shard_map/ppermute | solution.py:295
  140.0 7.0 %collective-permute-done.22.refs_13_ = s16[64,2176]{1,0:T(8,128)(2,1)S(1)} collective-permute-done((s16[64,2176]{1,0:T(8,128)(2,1)S(1)}, s16[64,2176]{1,0:T(8,128)(2,1)S(1)}, u32[]{:S(2)}, u32[]{:S(2)}) %collective-permute-start.22) | collective-permute-done | bytes 278560 | tf_op jit(solution)/shard_map/ppermute | solution.py:295
  147.0 1.4 collective-permute-done.24.refs_15_
  148.4 2.5 %collect.1 = (s16[64,2176]{1,0:T(8,128)(2,1)S(1)}, s16[64,2176]{1,0:T(8,128)(2,1)S(1)}, s16[64,2176]{1,0:T(8,128)(2,1)S(1)}, f32[64,2048]{1,0:T(8,128)S(1)}) custom-call(s32[8]{0:T(128)S(1)} %pad_add_fusion.at_ref, f32[64,2048]{1,0:T(8,128)S(1)} %get-tuple-element.45.refs_0_, s16[64,2176]{1,0:T(8,128)(2,1)S(1)} %collective-permute-done.3.refs_1_, ...), custom_call_target="tpu_custom_call" | custom-call | tf_op jit(solution)/shard_map/collect/pallas_call | solution.py:249
  151.9 2.3 %collective-permute-start.27 = (s16[64,2176]{1,0:T(8,128)(2,1)S(1)}, s16[64,2176]{1,0:T(8,128)(2,1)S(1)}, u32[]{:S(2)}, u32[]{:S(2)}) collective-permute-start(s16[64,2176]{1,0:T(8,128)(2,1)S(1)} %get-tuple-element.79), channel_id=1, source_target_pairs={{0,12},{1,13},{2,14},{3,15},{4,0},{5,1},{6,2},{7,3},{8,4},{9,5},{1... | collective-permute-start | bytes 835592 | tf_op jit(solution)/shard_map/ppermute | solution.py:286
  155.1 9.6 %collective-permute-done.25.a = s16[64,2176]{1,0:T(8,128)(2,1)S(1)} collective-permute-done((s16[64,2176]{1,0:T(8,128)(2,1)S(1)}, s16[64,2176]{1,0:T(8,128)(2,1)S(1)}, u32[]{:S(2)}, u32[]{:S(2)}) %collective-permute-start.25) | collective-permute-done | bytes 278560 | tf_op jit(solution)/shard_map/ppermute | solution.py:286
  (54 shorter events, 13.6 us)
Async XLA Ops:
  48.4 12.9 %collective-permute-start.2 = (s16[64,3456]{1,0:T(8,128)(2,1)S(1)}, s16[64,3456]{1,0:T(8,128)(2,1)S(1)}, u32[]{:S(2)}, u32[]{:S(2)}) collective-permute-start(s16[64,3456]{1,0:T(8,128)(2,1)S(1)} %get-tuple-element.81), channel_id=1, source_target_pairs={{0,96},{16,112},{32,0},{48,16},{64,32},{80,48},{96,64},{112,80},{1... | collective-permute-start | bytes 1327112 | tf_op jit(solution)/shard_map/ppermute | solution.py:277
  51.2 13.5 %collective-permute-start.1 = (s16[64,3456]{1,0:T(8,128)(2,1)S(1)}, s16[64,3456]{1,0:T(8,128)(2,1)S(1)}, u32[]{:S(2)}, u32[]{:S(2)}) collective-permute-start(s16[64,3456]{1,0:T(8,128)(2,1)S(1)} %get-tuple-element.81), channel_id=1, source_target_pairs={{0,32},{16,48},{32,64},{48,80},{64,96},{80,112},{96,0},{112,16},{1... | collective-permute-start | bytes 1327112 | tf_op jit(solution)/shard_map/ppermute | solution.py:277
  65.2 12.1 %collective-permute-start.9 = (s16[64,3456]{1,0:T(8,128)(2,1)S(1)}, s16[64,3456]{1,0:T(8,128)(2,1)S(1)}, u32[]{:S(2)}, u32[]{:S(2)}) collective-permute-start(s16[64,3456]{1,0:T(8,128)(2,1)S(1)} %get-tuple-element.80), channel_id=1, source_target_pairs={{0,96},{16,112},{32,0},{48,16},{64,32},{80,48},{96,64},{112,80},{1... | collective-permute-start | bytes 1327112 | tf_op jit(solution)/shard_map/ppermute | solution.py:277
  65.5 13.0 %collective-permute-start.8 = (s16[64,3456]{1,0:T(8,128)(2,1)S(1)}, s16[64,3456]{1,0:T(8,128)(2,1)S(1)}, u32[]{:S(2)}, u32[]{:S(2)}) collective-permute-start(s16[64,3456]{1,0:T(8,128)(2,1)S(1)} %get-tuple-element.80), channel_id=1, source_target_pairs={{0,32},{16,48},{32,64},{48,80},{64,96},{80,112},{96,0},{112,16},{1... | collective-permute-start | bytes 1327112 | tf_op jit(solution)/shard_map/ppermute | solution.py:277
  78.5 3.8 %collective-permute-start.14 = (s16[64,3456]{1,0:T(8,128)(2,1)S(1)}, s16[64,3456]{1,0:T(8,128)(2,1)S(1)}, u32[]{:S(2)}, u32[]{:S(2)}) collective-permute-start(s16[64,3456]{1,0:T(8,128)(2,1)S(1)} %collective-permute-done.8.refs_2_), channel_id=1, source_target_pairs={{0,16},{16,0},{32,48},{48,32},{64,80},{80,64},{96,112},{112,96},{1... | collective-permute-start | bytes 1327112 | tf_op jit(solution)/shard_map/ppermute | solution.py:281
  79.1 13.3 %collective-permute-start.15 = (s16[64,3456]{1,0:T(8,128)(2,1)S(1)}, s16[64,3456]{1,0:T(8,128)(2,1)S(1)}, u32[]{:S(2)}, u32[]{:S(2)}) collective-permute-start(s16[64,3456]{1,0:T(8,128)(2,1)S(1)} %collective-permute-done.1.refs_2_), channel_id=1, source_target_pairs={{0,32},{16,48},{32,64},{48,80},{64,96},{80,112},{96,0},{112,16},{1... | collective-permute-start | bytes 1327112 | tf_op jit(solution)/shard_map/ppermute | solution.py:277
  79.6 12.8 %collective-permute-start.16 = (s16[64,3456]{1,0:T(8,128)(2,1)S(1)}, s16[64,3456]{1,0:T(8,128)(2,1)S(1)}, u32[]{:S(2)}, u32[]{:S(2)}) collective-permute-start(s16[64,3456]{1,0:T(8,128)(2,1)S(1)} %collective-permute-done.9.refs_0_), channel_id=1, source_target_pairs={{0,96},{16,112},{32,0},{48,16},{64,32},{80,48},{96,64},{112,80},{1... | collective-permute-start | bytes 1327112 | tf_op jit(solution)/shard_map/ppermute | solution.py:277
  92.3 17.4 %collective-permute-start.20 = (s16[64,3456]{1,0:T(8,128)(2,1)S(1)}, s16[64,3456]{1,0:T(8,128)(2,1)S(1)}, u32[]{:S(2)}, u32[]{:S(2)}) collective-permute-start(s16[64,3456]{1,0:T(8,128)(2,1)S(1)} %collective-permute-done.15.refs_0_), channel_id=1, source_target_pairs={{0,16},{16,0},{32,48},{48,32},{64,80},{80,64},{96,112},{112,96},{1... | collective-permute-start | bytes 1327112 | tf_op jit(solution)/shard_map/ppermute | solution.py:281
  92.4 19.7 %collective-permute-start.21 = (s16[64,3456]{1,0:T(8,128)(2,1)S(1)}, s16[64,3456]{1,0:T(8,128)(2,1)S(1)}, u32[]{:S(2)}, u32[]{:S(2)}) collective-permute-start(s16[64,3456]{1,0:T(8,128)(2,1)S(1)} %collective-permute-done.16.refs_2_), channel_id=1, source_target_pairs={{0,16},{16,0},{32,48},{48,32},{64,80},{80,64},{96,112},{112,96},{1... | collective-permute-start | bytes 1327112 | tf_op jit(solution)/shard_map/ppermute | solution.py:281
  92.9 15.8 %collective-permute-start.3 = (s16[64,2176]{1,0:T(8,128)(2,1)S(1)}, s16[64,2176]{1,0:T(8,128)(2,1)S(1)}, u32[]{:S(2)}, u32[]{:S(2)}) collective-permute-start(s16[64,2176]{1,0:T(8,128)(2,1)S(1)} %get-tuple-element.49), channel_id=1, source_target_pairs={{0,1},{1,2},{2,3},{3,0},{4,5},{5,6},{6,7},{7,4},{8,9},{9,10},{10,1... | collective-permute-start | bytes 835592 | tf_op jit(solution)/shard_map/ppermute | solution.py:295
  93.5 15.2 %collective-permute-start.4 = (s16[64,2176]{1,0:T(8,128)(2,1)S(1)}, s16[64,2176]{1,0:T(8,128)(2,1)S(1)}, u32[]{:S(2)}, u32[]{:S(2)}) collective-permute-start(s16[64,2176]{1,0:T(8,128)(2,1)S(1)} %get-tuple-element.50), channel_id=1, source_target_pairs={{0,2},{1,3},{2,0},{3,1},{4,6},{5,7},{6,4},{7,5},{8,10},{9,11},{10,... | collective-permute-start | bytes 835592 | tf_op jit(solution)/shard_map/ppermute | solution.py:295
  94.8 28.0 %collective-permute-start.5 = (s16[64,2176]{1,0:T(8,128)(2,1)S(1)}, s16[64,2176]{1,0:T(8,128)(2,1)S(1)}, u32[]{:S(2)}, u32[]{:S(2)}) collective-permute-start(s16[64,2176]{1,0:T(8,128)(2,1)S(1)} %get-tuple-element.51), channel_id=1, source_target_pairs={{0,3},{1,0},{2,1},{3,2},{4,7},{5,4},{6,5},{7,6},{8,11},{9,8},{10,9... | collective-permute-start | bytes 835592 | tf_op jit(solution)/shard_map/ppermute | solution.py:295
  108.7 16.2 %collective-permute-start.10 = (s16[64,2176]{1,0:T(8,128)(2,1)S(1)}, s16[64,2176]{1,0:T(8,128)(2,1)S(1)}, u32[]{:S(2)}, u32[]{:S(2)}) collective-permute-start(s16[64,2176]{1,0:T(8,128)(2,1)S(1)} %get-tuple-element.58), channel_id=1, source_target_pairs={{0,1},{1,2},{2,3},{3,0},{4,5},{5,6},{6,7},{7,4},{8,9},{9,10},{10,1... | collective-permute-start | bytes 835592 | tf_op jit(solution)/shard_map/ppermute | solution.py:295
  108.7 18.8 %collective-permute-start.11 = (s16[64,2176]{1,0:T(8,128)(2,1)S(1)}, s16[64,2176]{1,0:T(8,128)(2,1)S(1)}, u32[]{:S(2)}, u32[]{:S(2)}) collective-permute-start(s16[64,2176]{1,0:T(8,128)(2,1)S(1)} %get-tuple-element.59), channel_id=1, source_target_pairs={{0,2},{1,3},{2,0},{3,1},{4,6},{5,7},{6,4},{7,5},{8,10},{9,11},{10,... | collective-permute-start | bytes 835592 | tf_op jit(solution)/shard_map/ppermute | solution.py:295
  109.7 17.8 %collective-permute-start.12 = (s16[64,2176]{1,0:T(8,128)(2,1)S(1)}, s16[64,2176]{1,0:T(8,128)(2,1)S(1)}, u32[]{:S(2)}, u32[]{:S(2)}) collective-permute-start(s16[64,2176]{1,0:T(8,128)(2,1)S(1)} %get-tuple-element.60), channel_id=1, source_target_pairs={{0,3},{1,0},{2,1},{3,2},{4,7},{5,4},{6,5},{7,6},{8,11},{9,8},{10,9... | collective-permute-start | bytes 835592 | tf_op jit(solution)/shard_map/ppermute | solution.py:295
  112.0 24.3 %collective-permute-start.17 = (s16[64,2176]{1,0:T(8,128)(2,1)S(1)}, s16[64,2176]{1,0:T(8,128)(2,1)S(1)}, u32[]{:S(2)}, u32[]{:S(2)}) collective-permute-start(s16[64,2176]{1,0:T(8,128)(2,1)S(1)} %get-tuple-element.67), channel_id=1, source_target_pairs={{0,1},{1,2},{2,3},{3,0},{4,5},{5,6},{6,7},{7,4},{8,9},{9,10},{10,1... | collective-permute-start | bytes 835592 | tf_op jit(solution)/shard_map/ppermute | solution.py:295
  122.8 13.6 %collective-permute-start.18 = (s16[64,2176]{1,0:T(8,128)(2,1)S(1)}, s16[64,2176]{1,0:T(8,128)(2,1)S(1)}, u32[]{:S(2)}, u32[]{:S(2)}) collective-permute-start(s16[64,2176]{1,0:T(8,128)(2,1)S(1)} %get-tuple-element.68), channel_id=1, source_target_pairs={{0,2},{1,3},{2,0},{3,1},{4,6},{5,7},{6,4},{7,5},{8,10},{9,11},{10,... | collective-permute-start | bytes 835592 | tf_op jit(solution)/shard_map/ppermute | solution.py:295
  124.8 15.1 %collective-permute-start.19 = (s16[64,2176]{1,0:T(8,128)(2,1)S(1)}, s16[64,2176]{1,0:T(8,128)(2,1)S(1)}, u32[]{:S(2)}, u32[]{:S(2)}) collective-permute-start(s16[64,2176]{1,0:T(8,128)(2,1)S(1)} %get-tuple-element.69), channel_id=1, source_target_pairs={{0,3},{1,0},{2,1},{3,2},{4,7},{5,4},{6,5},{7,6},{8,11},{9,8},{10,9... | collective-permute-start | bytes 835592 | tf_op jit(solution)/shard_map/ppermute | solution.py:295
  127.5 19.5 %collective-permute-start.22 = (s16[64,2176]{1,0:T(8,128)(2,1)S(1)}, s16[64,2176]{1,0:T(8,128)(2,1)S(1)}, u32[]{:S(2)}, u32[]{:S(2)}) collective-permute-start(s16[64,2176]{1,0:T(8,128)(2,1)S(1)} %get-tuple-element.73), channel_id=1, source_target_pairs={{0,1},{1,2},{2,3},{3,0},{4,5},{5,6},{6,7},{7,4},{8,9},{9,10},{10,1... | collective-permute-start | bytes 835592 | tf_op jit(solution)/shard_map/ppermute | solution.py:295
  127.5 19.5 %collective-permute-start.23 = (s16[64,2176]{1,0:T(8,128)(2,1)S(1)}, s16[64,2176]{1,0:T(8,128)(2,1)S(1)}, u32[]{:S(2)}, u32[]{:S(2)}) collective-permute-start(s16[64,2176]{1,0:T(8,128)(2,1)S(1)} %get-tuple-element.74), channel_id=1, source_target_pairs={{0,2},{1,3},{2,0},{3,1},{4,6},{5,7},{6,4},{7,5},{8,10},{9,11},{10,... | collective-permute-start | bytes 835592 | tf_op jit(solution)/shard_map/ppermute | solution.py:295
  136.3 12.1 %collective-permute-start.24 = (s16[64,2176]{1,0:T(8,128)(2,1)S(1)}, s16[64,2176]{1,0:T(8,128)(2,1)S(1)}, u32[]{:S(2)}, u32[]{:S(2)}) collective-permute-start(s16[64,2176]{1,0:T(8,128)(2,1)S(1)} %get-tuple-element.75), channel_id=1, source_target_pairs={{0,3},{1,0},{2,1},{3,2},{4,7},{5,4},{6,5},{7,6},{8,11},{9,8},{10,9... | collective-permute-start | bytes 835592 | tf_op jit(solution)/shard_map/ppermute | solution.py:295
  150.9 13.8 %collective-permute-start.25 = (s16[64,2176]{1,0:T(8,128)(2,1)S(1)}, s16[64,2176]{1,0:T(8,128)(2,1)S(1)}, u32[]{:S(2)}, u32[]{:S(2)}) collective-permute-start(s16[64,2176]{1,0:T(8,128)(2,1)S(1)} %get-tuple-element.77), channel_id=1, source_target_pairs={{0,4},{1,5},{2,6},{3,7},{4,8},{5,9},{6,10},{7,11},{8,12},{9,13},{1... | collective-permute-start | bytes 835592 | tf_op jit(solution)/shard_map/ppermute | solution.py:286
  151.0 13.7 %collective-permute-start.26 = (s16[64,2176]{1,0:T(8,128)(2,1)S(1)}, s16[64,2176]{1,0:T(8,128)(2,1)S(1)}, u32[]{:S(2)}, u32[]{:S(2)}) collective-permute-start(s16[64,2176]{1,0:T(8,128)(2,1)S(1)} %get-tuple-element.78), channel_id=1, source_target_pairs={{0,8},{1,9},{2,10},{3,11},{4,12},{5,13},{6,14},{7,15},{8,0},{9,1},... | collective-permute-start | bytes 835592 | tf_op jit(solution)/shard_map/ppermute | solution.py:286
  151.9 13.4 %collective-permute-start.27 = (s16[64,2176]{1,0:T(8,128)(2,1)S(1)}, s16[64,2176]{1,0:T(8,128)(2,1)S(1)}, u32[]{:S(2)}, u32[]{:S(2)}) collective-permute-start(s16[64,2176]{1,0:T(8,128)(2,1)S(1)} %get-tuple-element.79), channel_id=1, source_target_pairs={{0,12},{1,13},{2,14},{3,15},{4,0},{5,1},{6,2},{7,3},{8,4},{9,5},{1... | collective-permute-start | bytes 835592 | tf_op jit(solution)/shard_map/ppermute | solution.py:286
  (6 other events, 85.4 us)
where the time goes:
time: 168 us; the launch traced here: 166 us
  Pallas kernels  47.9 us (29%)
  waiting for transfers between devices  47.1 us (28%)
  blocking collectives  40.7 us (24%)
  starting transfers between devices  26.8 us (16%)
  local copies, waits for them, and re-layouts  2.72 us (2%)
    pallas_call x4, Pallas kernels, product(): pl.pallas_call(product_kernel, grid=(1,), out_shape=[message] * 3 + [jax....  39.6 us
    ppermute x12, waiting for transfers between devices, along_y(): got.append(lax.ppermute(block, 'tensor', route))  31.8 us
    all_to_all x1, blocking collectives, step(): lax.all_to_all(sent, 'tensor', split_axis=0, concat_axis=0, tiled=True)  23 us
    all_to_all x1, blocking collectives, step(): lax.all_to_all(code, 'tensor', split_axis=0, concat_axis=0, tiled=True)  17.7 us
    ppermute x12, starting transfers between devices, along_y(): got.append(lax.ppermute(block, 'tensor', route))  13.8 us
    ppermute x3, waiting for transfers between devices, along_z(): lax.ppermute(block, 'tensor', [(i, (i + 4 * apart) % 16) for i in range(1...  10.2 us
    ppermute x6, starting transfers between devices, along_x(): lax.ppermute(block, 'seq', [(i, (i + 2 * apart) % 8) for i in range(8)])  8.09 us
    ppermute x6, waiting for transfers between devices, along_x(): lax.ppermute(block, 'seq', [(i, (i + 2 * apart) % 8) for i in range(8)])  5.12 us
  transfers between devices with their start and end apart: 28, of which 12 were waited for; matrix products, arithmetic and copies ran while one was open for 1% of the time, Pallas kernels for 24%

commit v1 on v0

--- a/solution.py
+++ b/solution.py
@@ -19,18 +19,24 @@
 CODE_TOP = 32767.0
 SUM_TOP = 32700.0
 BLOCK = 512
+ROWS = 64
 
 
 def vmem():
     return pl.BlockSpec(memory_space=pltpu.VMEM)
 
 
-def smem():
-    return pl.BlockSpec(memory_space=pltpu.SMEM)
-
-
 def params(mebibytes=12, **more):
     return pltpu.CompilerParams(vmem_limit_bytes=mebibytes * 1024 * 1024, **more)
+
+
+def slot_of(apart):
+    ahead = ((lax.axis_index("tensor") >> 2) + apart - (lax.axis_index("seq") >> 1)) & 3
+    return ahead ^ (ahead >> 1)
+
+
+def place_of(apart):
+    return ((lax.axis_index("tensor") + apart) & 3) ^ ((lax.axis_index("seq") & 1) * 2)
 
 
 def parity_sign(left, right, bits):
@@ -58,7 +64,7 @@
     pick_row = (row - HAD * block_of(row) == iota((group, HAD), 1)).astype(BF16)
     lane = iota((HAD, width), 1)
     pick_lane = (lane - HAD * block_of(lane) == iota((HAD, width), 0)).astype(BF16)
-    small = had_ref[...].astype(F32).astype(BF16)
+    small = had_ref[...]
     tiled = jnp.dot(small, pick_lane, preferred_element_type=F32).astype(BF16)
     base = jnp.dot(pick_row, tiled, preferred_element_type=F32)
     row_block = block_of(iota((group, width), 0))
@@ -142,9 +148,9 @@
     )(x, had_small, weight)
 
 
-def product_kernel(at_ref, *refs):
+def product_kernel(strides, parts, *refs):
     codes, w_ref = refs[:4], refs[4]
-    sends, kept, lhs, total, scale = refs[5:8], refs[8], refs[9], refs[10], refs[11]
+    outs, (lhs, total, scale) = refs[5:-3], refs[-3:]
     rows = scale.shape[0] // 4
     size = rows // 2
     depth, width = w_ref.shape
@@ -167,32 +173,34 @@
         return carry
 
     lax.fori_loop(0, width // BLOCK, columns, 0)
-    for d in range(4):
-        for group in range(2):
-            first = pl.multiple_of(group * 2 * rows + at_ref[4 + d] * size, size)
+    for group in range(2):
+        chosen = outs if parts == 1 else outs[4 * group : 4 * group + 4]
+        span = slice(group * size, (group + 1) * size) if parts == 1 else slice(None)
+        for d in range(4):
+            first = pl.multiple_of(group * strides[0] + place_of(d) * strides[1], size)
             value = total[pl.ds(first, size), :]
-            span = slice(group * size, (group + 1) * size)
             if d == 0:
-                kept[span, :] = value
+                chosen[3][span, :] = value
             else:
-                pack(value, sends[d - 1], span)
-
-
-def product(at, codes, weight):
-    rows = codes[0][0].shape[0] if codes[0][1] is None else codes[0][0].shape[0] // 2
+                pack(value, chosen[d - 1], span)
+
+
+def product(codes, weight, strides, parts=1):
+    rows = ROWS
     depth, width = weight.shape
-    message = jax.ShapeDtypeStruct((rows, width + LANES), I16)
+    size = rows // parts
+    outs = [jax.ShapeDtypeStruct((size, width + LANES), I16)] * 3 + [jax.ShapeDtypeStruct((size, width), F32)]
+    outs = outs * parts
     specs = [
-        pl.BlockSpec((rows, depth + LANES), functools.partial(lambda index, n: (index, 0), index or 0))
+        pl.BlockSpec((rows, depth + LANES), functools.partial(lambda index, n: (index, 0), index))
         for _, index in codes
     ]
     return pl.pallas_call(
-        product_kernel,
+        functools.partial(product_kernel, strides, parts),
         grid=(1,),
-        out_shape=[message] * 3 + [jax.ShapeDtypeStruct((rows, width), F32)],
-        in_specs=[smem()] + specs + [vmem()],
-        out_specs=[pl.BlockSpec(message.shape, lambda n: (0, 0))] * 3
-        + [pl.BlockSpec((rows, width), lambda n: (0, 0))],
+        out_shape=outs,
+        in_specs=specs + [vmem()],
+        out_specs=[pl.BlockSpec(out.shape, lambda n: (0, 0)) for out in outs],
         scratch_shapes=[
             pltpu.VMEM((8 * rows, depth), BF16),
             pltpu.VMEM((4 * rows, width), F32),
@@ -204,7 +212,7 @@
             bytes_accessed=2 * depth * width,
             transcendentals=0,
         ),
-    )(at, *[array for array, _ in codes], weight)
+    )(*[array for array, _ in codes], weight)
 
 
 def pack(value, out_ref, span=slice(None)):
@@ -224,53 +232,61 @@
     return code[:, :width].astype(I32).astype(F32) * factor
 
 
-def collect_kernel(at_ref, *refs):
-    sends, own_ref, held = refs[16:19], refs[19], refs[20]
-    half = own_ref.shape[0] // 2
-    for chunk in range(4):
-        kept, a, b, c = refs[4 * chunk : 4 * chunk + 4]
-        value = kept[...] + unpack(a[...]) + unpack(b[...]) + unpack(c[...])
-        for group in range(2):
-            if chunk in (0, 3):
-                held[chunk, group * half : (group + 1) * half, :] = value[group * half : (group + 1) * half]
-            else:
-                held[1 + group, (chunk - 1) * half : chunk * half, :] = value[group * half : (group + 1) * half]
+def collect_kernel(part, *refs):
+    first, middle, last = refs[:4], refs[4:8], refs[8:12]
+    sends, own_ref, held = refs[12:15], refs[15], refs[16]
+    size = own_ref.shape[0]
+
+    def joined(blocks, span):
+        total = blocks[0][span, :]
+        for got in blocks[1:]:
+            total = total + unpack(got[span, :])
+        return total
+
+    held[0] = joined(first, slice(part * size, (part + 1) * size))
+    held[1] = joined(middle, slice(0, size))
+    held[2] = joined(middle, slice(size, 2 * size))
+    held[3] = joined(last, slice(0, size))
     for d in range(4):
-        value = held[at_ref[d]]
+        value = held[slot_of(d)]
         if d == 0:
             own_ref[...] = value
         else:
             pack(value, sends[d - 1])
 
 
-def collect(at, parts):
-    size, width = parts[0].shape
+def collect(part, first, middle, last):
+    size, width = last[0].shape
     message = jax.ShapeDtypeStruct((size, width + LANES), I16)
     return pl.pallas_call(
-        collect_kernel,
+        functools.partial(collect_kernel, part),
         out_shape=[message] * 3 + [jax.ShapeDtypeStruct((size, width), F32)],
-        in_specs=[smem()] + [vmem()] * 16,
+        in_specs=[vmem()] * 12,
         out_specs=[vmem()] * 4,
         scratch_shapes=[pltpu.VMEM((4, size, width), F32)],
-        compiler_params=params(16),
-        name="collect",
-    )(at, *parts)
-
-
-def finish_kernel(own_ref, w_ref, a, b, c, out_ref):
-    total = own_ref[...] + unpack(a[...]) + unpack(b[...]) + unpack(c[...])
-    out_ref[...] = (total * w_ref[...]).astype(BF16)
-
-
-def finish(own, w_scale, got):
+        compiler_params=params(12),
+    )(*first, *middle, *last)
+
+
+def finish_kernel(w_ref, *refs):
+    out_ref = refs[-1]
+    for part in range(2):
+        own, a, b, c = refs[4 * part : 4 * part + 4]
+        size = own.shape[0]
+        total = own[...] + unpack(a[...]) + unpack(b[...]) + unpack(c[...])
+        out_ref[part * size : (part + 1) * size, :] = (total * w_ref[...]).astype(BF16)
+
+
+def finish(w_scale, parts):
+    size, width = parts[0].shape
     return pl.pallas_call(
         finish_kernel,
-        out_shape=jax.ShapeDtypeStruct(own.shape, BF16),
-        in_specs=[vmem()] * 5,
+        out_shape=jax.ShapeDtypeStruct((2 * size, width), BF16),
+        in_specs=[vmem()] * 9,
         out_specs=vmem(),
         compiler_params=params(),
         name="finish",
-    )(own, w_scale, *got)
+    )(w_scale, *parts)
 
 
 def along_x(block, apart):
@@ -282,10 +298,10 @@
 
 
 def along_z(blocks):
-    return [
-        lax.ppermute(block, "tensor", [(i, (i + 4 * apart) % 16) for i in range(16)])
-        for apart, block in enumerate(blocks, 1)
-    ]
+    got = []
+    for apart, block in enumerate(blocks, 1):
+        got.append(lax.ppermute(block, "tensor", [(i, (i + 4 * apart) % 16) for i in range(16)]))
+    return got
 
 
 def along_y(blocks):
@@ -299,49 +315,45 @@
 def step(hidden, down_int, w_scale, had_small):
     tokens, columns = hidden.shape
     ranks = lax.axis_size("tensor")
-    half, quarter = tokens // 2, tokens // 4
-    seq, tensor = lax.axis_index("seq"), lax.axis_index("tensor")
-    x, core, z, y = seq // 2, seq % 2, tensor // 4, tensor % 4
-    away = jnp.arange(4, dtype=I32)
-    slot = (z + away - x) % 4
-    slot = jnp.where(slot == 2, 3, jnp.where(slot == 3, 2, slot))
-    place = ((y + away) % 4) ^ (2 * core)
-    at = jnp.concatenate([slot, place]).astype(I32)
-    at, hidden = lax.optimization_barrier((at, hidden))
-
-    ordered = hidden.reshape(2, 2, quarter, columns).swapaxes(0, 1)
-    sent = ordered.reshape(ranks, tokens // ranks, columns)
+    small = had_small.astype(BF16)
+    small, hidden = lax.optimization_barrier((small, hidden))
+    sent = hidden.reshape(ranks, tokens // ranks, columns)
     whole = lax.all_to_all(sent, "tensor", split_axis=0, concat_axis=0, tiled=True)
-    code, weight = rotate(whole.reshape(tokens, columns), had_small, down_int)
+    code, weight = rotate(whole.reshape(tokens, columns), small, down_int)
     code = code.reshape(ranks, tokens // ranks, columns + LANES)
     back = lax.all_to_all(code, "tensor", split_axis=0, concat_axis=0, tiled=True)
     own = back.reshape(tokens, columns + LANES)
-    scales = scale_of(own[:, columns : columns + LANES])[:, 0]
-    act_scale = scales.reshape(2, 2, quarter).swapaxes(0, 1).reshape(tokens)
+    act_scale = scale_of(own[:, columns : columns + LANES])[:, 0]
 
     own_c = other_core(own)
-    below_0, above_0 = along_x(own[:half], 1), along_x(own[:half], -1)
-    below_1, above_1 = along_x(own[half:], 1), along_x(own[half:], -1)
-    codes = [(own, 0), (own_c, 0), (own, 1), (own_c, 1)]
-    *sends, kept_0 = product(at, codes, weight)
+    halves = own.reshape(2, 2, ROWS // 2, columns + LANES)
+    own_0 = halves[:, 0].reshape(ROWS, columns + LANES)
+    own_1 = halves[:, 1].reshape(ROWS, columns + LANES)
+    below_0, above_0 = along_x(own_0, 1), along_x(own_0, -1)
+    below_1, above_1 = along_x(own_1, 1), along_x(own_1, -1)
+    natural, grouped = (ROWS // 2, ROWS), (2 * ROWS, ROWS // 2)
+    codes = [(own, 0), (own, 1), (own_c, 0), (own_c, 1)]
+    *sends, kept_0 = product(codes, weight, natural)
     sends, below_0, above_0 = lax.optimization_barrier((sends, below_0, above_0))
     got_0 = along_y(sends)
     far_0 = along_x(below_0, 1)
     codes = [above_0, other_core(above_0), below_0, other_core(below_0)]
-    *sends, kept_1 = product(at, [(code, None) for code in codes], weight)
+    *sends, kept_1 = product([(code, 0) for code in codes], weight, grouped)
     sends, below_1, above_1 = lax.optimization_barrier((sends, below_1, above_1))
     got_1 = along_y(sends)
     far_1 = along_x(above_1, -1)
     codes = [above_1, other_core(above_1), below_1, other_core(below_1)]
-    *sends, kept_2 = product(at, [(code, None) for code in codes], weight)
+    *sends, kept_2 = product([(code, 0) for code in codes], weight, grouped)
     sends, far_0, far_1 = lax.optimization_barrier((sends, far_0, far_1))
     got_2 = along_y(sends)
     codes = [far_0, other_core(far_0), far_1, other_core(far_1)]
-    *sends, kept_3 = product(at, [(code, None) for code in codes], weight)
-    got_3 = along_y(sends)
-    parts = [kept_0, *got_0, kept_1, *got_1, kept_2, *got_2, kept_3, *got_3]
-    *sends, own_sum = collect(at, parts)
-    mixed = finish(own_sum, w_scale[None, :], along_z(sends))
+    outs = product([(code, 0) for code in codes], weight, grouped, 2)
+    got_a, got_b = along_y(outs[:3]), along_y(outs[4:7])
+    *sends, own_a = collect(0, [kept_0, *got_0], [kept_1, *got_1], [outs[3], *got_a])
+    end_a = along_z(sends)
+    *sends, own_b = collect(1, [kept_0, *got_0], [kept_2, *got_2], [outs[7], *got_b])
+    end_b = along_z(sends)
+    mixed = finish(w_scale[None, :], [own_a, *end_a, own_b, *end_b])
     return (mixed, act_scale)
 
 

time: 168 us -> 163 us (0.970)
  Pallas kernels: 47.9 us -> 44.9 us
  waiting for transfers between devices: 47.1 us -> 44.3 us
  local copies, waits for them, and re-layouts: 2.72 us -> 0.06 us
  starting transfers between devices: 26.8 us -> 29.1 us
    ppermute x3 -> x6, waiting for transfers between devices: 10.2 us -> 5.68 us  [along_z(): lax.ppermute(block, 'tensor', [(i, (i + 4 * apart) % 16) for i in range(1...]
    pallas_call x6 -> x7, Pallas kernels: 43 us -> 40 us  [the longest x4 37.3 us: product(): pl.pallas_call(functools.partial(product_kernel, strides, parts), grid=(1...]
    ppermute x12 -> x15, starting transfers between devices: 13.8 us -> 15 us  [along_y(): got.append(lax.ppermute(block, 'tensor', route))]
    ppermute x3 -> x6, starting transfers between devices: 3.3 us -> 4.39 us  [along_z(): lax.ppermute(block, 'tensor', [(i, (i + 4 * apart) % 16) for i in range(1...]
    ppermute x12 -> x15, waiting for transfers between devices: 31.8 us -> 31.8 us  [along_y(): got.append(lax.ppermute(block, 'tensor', route))]
  transfers between devices with their start and end apart: 28 -> 34, of which waited for: 12 -> 16; matrix products, arithmetic and copies ran while one was open for 1% -> 0% of each run, Pallas kernels for 24% -> 24%
where the time goes in v1:
time: 163 us; the launch traced here: 161 us
  Pallas kernels  44.9 us (28%)
  waiting for transfers between devices  44.3 us (27%)
  blocking collectives  40.9 us (25%)
  starting transfers between devices  29.1 us (18%)
    pallas_call x4, Pallas kernels, product(): pl.pallas_call(functools.partial(product_kernel, strides, parts), grid=(1...  37.3 us
    ppermute x15, waiting for transfers between devices, along_y(): got.append(lax.ppermute(block, 'tensor', route))  31.8 us
    all_to_all x1, blocking collectives, step(): lax.all_to_all(sent, 'tensor', split_axis=0, concat_axis=0, tiled=True)  23.2 us
    all_to_all x1, blocking collectives, step(): lax.all_to_all(code, 'tensor', split_axis=0, concat_axis=0, tiled=True)  17.7 us
    ppermute x15, starting transfers between devices, along_y(): got.append(lax.ppermute(block, 'tensor', route))  15 us
    ppermute x6, starting transfers between devices, along_x(): lax.ppermute(block, 'seq', [(i, (i + 2 * apart) % 8) for i in range(8)])  8.09 us
    ppermute x6, waiting for transfers between devices, along_x(): lax.ppermute(block, 'seq', [(i, (i + 2 * apart) % 8) for i in range(8)])  6.8 us
    ppermute x6, waiting for transfers between devices, along_z(): lax.ppermute(block, 'tensor', [(i, (i + 4 * apart) % 16) for i in range(1...  5.68 us
  transfers between devices with their start and end apart: 34, of which 16 were waited for; matrix products, arithmetic and copies ran while one was open for 0% of the time, Pallas kernels for 24%

profile of v1, /device:TPU:0, one launch (start us, length us, event | category | flops | bytes accessed | tf_op | source)
XLA Modules:
  0.0 161.5 jit_solution(11327800213764763280)
XLA Ops:
  1.4 23.2 %all_to_all.10 = bf16[16,8,3328]{2,1,0:T(8,128)(2,1)S(1)} all-to-all(bf16[16,8,3328]{2,1,0:T(8,128)(2,1)} %bitcast.16), channel_id=1, replica_groups=mesh['seq'=8,'tensor'=16] {'tensor'}, dimensions={0} | all-to-all | bytes 1703936 | tf_op jit(solution)/shard_map/all_to_all | solution.py:321
  24.6 4.9 %rotate.1 = (s16[128,3456]{1,0:T(8,128)(2,1)S(1)}, bf16[3328,2048]{1,0:T(8,128)(2,1)S(1)}) custom-call(bf16[128,3328]{1,0:T(8,128)(2,1)S(1)} %bitcast.13, bf16[52,52]{1,0:T(8,128)(2,1)S(1)} %convert_element_type.9.had_ref, bf16[3328,2048]{1,0:T(8,128)(2,1)} %w_ref.1), custom_call_target="tpu_custom_call" | custom-call | tf_op jit(solution)/shard_map/rotate/pallas_call | solution.py:133
  29.5 17.7 %all_to_all.11 = s16[16,8,3456]{2,1,0:T(8,128)(2,1)S(1)} all-to-all(s16[16,8,3456]{2,1,0:T(8,128)(2,1)S(1)} %bitcast.14), channel_id=1, replica_groups=mesh['seq'=8,'tensor'=16] {'tensor'}, dimensions={0} | all-to-all | bytes 1769472 | tf_op jit(solution)/shard_map/all_to_all | solution.py:324
  47.3 2.8 %collective-permute-start.2 = (s16[64,3456]{1,0:T(8,128)(2,1)S(1)}, s16[64,3456]{1,0:T(8,128)(2,1)S(1)}, u32[]{:S(2)}, u32[]{:S(2)}) collective-permute-start(s16[64,3456]{1,0:T(8,128)(2,1)S(1)} %bitcast.19), channel_id=1, source_target_pairs={{0,96},{16,112},{32,0},{48,16},{64,32},{80,48},{96,64},{112,80},{1... | collective-permute-start | bytes 1327112 | tf_op jit(solution)/shard_map/ppermute | solution.py:293
  50.1 9.3 %shard_map.59 = (s16[64,2176]{1,0:T(8,128)(2,1)S(1)}, s16[64,2176]{1,0:T(8,128)(2,1)S(1)}, s16[64,2176]{1,0:T(8,128)(2,1)S(1)}, f32[64,2048]{1,0:T(8,128)S(1)}) custom-call(s16[128,3456]{1,0:T(8,128)(2,1)S(1)} %bitcast.10, s16[128,3456]{1,0:T(8,128)(2,1)S(1)} %bitcast.11, s16[128,3456]{1,0:T(8,128)(2,1)S(1)} %collective-permute-done.refs_2_.refs_3_, ...), custom_call_target="tpu_custom_call" | custom-call | flops 6979321856 | bytes 13631488 | tf_op jit(solution)/shard_map/pallas_call | solution.py:198
  60.2 3.4 %collective-permute-done.1.refs_2_ = s16[64,3456]{1,0:T(8,128)(2,1)S(1)} collective-permute-done((s16[64,3456]{1,0:T(8,128)(2,1)S(1)}, s16[64,3456]{1,0:T(8,128)(2,1)S(1)}, u32[]{:S(2)}, u32[]{:S(2)}) %collective-permute-start.1) | collective-permute-done | bytes 442400 | tf_op jit(solution)/shard_map/ppermute | solution.py:293
  64.4 1.7 %collective-permute-start.8 = (s16[64,3456]{1,0:T(8,128)(2,1)S(1)}, s16[64,3456]{1,0:T(8,128)(2,1)S(1)}, u32[]{:S(2)}, u32[]{:S(2)}) collective-permute-start(s16[64,3456]{1,0:T(8,128)(2,1)S(1)} %bitcast.18), channel_id=1, source_target_pairs={{0,32},{16,48},{32,64},{48,80},{64,96},{80,112},{96,0},{112,16},{1... | collective-permute-start | bytes 1327112 | tf_op jit(solution)/shard_map/ppermute | solution.py:293
  66.1 9.3 %shard_map.60 = (s16[64,2176]{1,0:T(8,128)(2,1)S(1)}, s16[64,2176]{1,0:T(8,128)(2,1)S(1)}, s16[64,2176]{1,0:T(8,128)(2,1)S(1)}, f32[64,2048]{1,0:T(8,128)S(1)}) custom-call(s16[64,3456]{1,0:T(8,128)(2,1)S(1)} %collective-permute-done.2.refs_0_, s16[64,3456]{1,0:T(8,128)(2,1)S(1)} %collective-permute-done.6.refs_1_, ...), custom_call_target="tpu_custom_call" | custom-call | flops 6979321856 | bytes 13631488 | tf_op jit(solution)/shard_map/pallas_call | solution.py:198
  78.4 2.7 %collective-permute-start.16 = (s16[64,3456]{1,0:T(8,128)(2,1)S(1)}, s16[64,3456]{1,0:T(8,128)(2,1)S(1)}, u32[]{:S(2)}, u32[]{:S(2)}) collective-permute-start(s16[64,3456]{1,0:T(8,128)(2,1)S(1)} %collective-permute-done.9.refs_0_), channel_id=1, source_target_pairs={{0,96},{16,112},{32,0},{48,16},{64,32},{80,48},{96,64},{112,80},{1... | collective-permute-start | bytes 1327112 | tf_op jit(solution)/shard_map/ppermute | solution.py:293
  81.2 9.3 %shard_map.61 = (s16[64,2176]{1,0:T(8,128)(2,1)S(1)}, s16[64,2176]{1,0:T(8,128)(2,1)S(1)}, s16[64,2176]{1,0:T(8,128)(2,1)S(1)}, f32[64,2048]{1,0:T(8,128)S(1)}) custom-call(s16[64,3456]{1,0:T(8,128)(2,1)S(1)} %collective-permute-done.9.refs_0_, s16[64,3456]{1,0:T(8,128)(2,1)S(1)} %collective-permute-done.13.refs_1_, ...), custom_call_target="tpu_custom_call" | custom-call | flops 6979321856 | bytes 13631488 | tf_op jit(solution)/shard_map/pallas_call | solution.py:198
  93.7 1.5 collective-permute-start.5
  95.1 12.4 %collective-permute-done.3.refs_1_ = s16[64,2176]{1,0:T(8,128)(2,1)S(1)} collective-permute-done((s16[64,2176]{1,0:T(8,128)(2,1)S(1)}, s16[64,2176]{1,0:T(8,128)(2,1)S(1)}, u32[]{:S(2)}, u32[]{:S(2)}) %collective-permute-start.3) | collective-permute-done | bytes 278560 | tf_op jit(solution)/shard_map/ppermute | solution.py:311
  108.6 2.3 %collective-permute-start.12 = (s16[64,2176]{1,0:T(8,128)(2,1)S(1)}, s16[64,2176]{1,0:T(8,128)(2,1)S(1)}, u32[]{:S(2)}, u32[]{:S(2)}) collective-permute-start(s16[64,2176]{1,0:T(8,128)(2,1)S(1)} %get-tuple-element.68), channel_id=1, source_target_pairs={{0,3},{1,0},{2,1},{3,2},{4,7},{5,4},{6,5},{7,6},{8,11},{9,8},{10,9... | collective-permute-start | bytes 835592 | tf_op jit(solution)/shard_map/ppermute | solution.py:311
  111.7 2.1 %collective-permute-start.26 = (s16[64,2176]{1,0:T(8,128)(2,1)S(1)}, s16[64,2176]{1,0:T(8,128)(2,1)S(1)}, u32[]{:S(2)}, u32[]{:S(2)}) collective-permute-start(s16[64,2176]{1,0:T(8,128)(2,1)S(1)} %get-tuple-element.86), channel_id=1, source_target_pairs={{0,2},{1,3},{2,0},{3,1},{4,6},{5,7},{6,4},{7,5},{8,10},{9,11},{10,... | collective-permute-start | bytes 835592 | tf_op jit(solution)/shard_map/ppermute | solution.py:311
  113.8 9.3 %shard_map.62 = (s16[32,2176]{1,0:T(8,128)(2,1)S(1)}, s16[32,2176]{1,0:T(8,128)(2,1)S(1)}, s16[32,2176]{1,0:T(8,128)(2,1)S(1)}, f32[32,2048]{1,0:T(8,128)S(1)}, ...) custom-call(s16[64,3456]{1,0:T(8,128)(2,1)S(1)} %collective-permute-, ...), custom_call_target="tpu_custom_call" | custom-call | flops 6979321856 | bytes 13631488 | tf_op jit(solution)/shard_map/pallas_call | solution.py:198
  124.2 1.7 %collective-permute-start.27 = (s16[64,2176]{1,0:T(8,128)(2,1)S(1)}, s16[64,2176]{1,0:T(8,128)(2,1)S(1)}, u32[]{:S(2)}, u32[]{:S(2)}) collective-permute-start(s16[64,2176]{1,0:T(8,128)(2,1)S(1)} %get-tuple-element.87), channel_id=1, source_target_pairs={{0,3},{1,0},{2,1},{3,2},{4,7},{5,4},{6,5},{7,6},{8,11},{9,8},{10,9... | collective-permute-start | bytes 835592 | tf_op jit(solution)/shard_map/ppermute | solution.py:311
  127.6 10.6 %collective-permute-done.25.refs_5_ = s16[64,2176]{1,0:T(8,128)(2,1)S(1)} collective-permute-done((s16[64,2176]{1,0:T(8,128)(2,1)S(1)}, s16[64,2176]{1,0:T(8,128)(2,1)S(1)}, u32[]{:S(2)}, u32[]{:S(2)}) %collective-permute-start.25) | collective-permute-done | bytes 278560 | tf_op jit(solution)/shard_map/ppermute | solution.py:311
  138.2 1.7 %collective-permute-done.19.refs_9_ = s16[32,2176]{1,0:T(8,128)(2,1)S(1)} collective-permute-done((s16[32,2176]{1,0:T(8,128)(2,1)S(1)}, s16[32,2176]{1,0:T(8,128)(2,1)S(1)}, u32[]{:S(2)}, u32[]{:S(2)}) %collective-permute-start.19) | collective-permute-done | bytes 139296 | tf_op jit(solution)/shard_map/ppermute | solution.py:311
  140.9 2.5 %collective-permute-done.21.refs_11_ = s16[32,2176]{1,0:T(8,128)(2,1)S(1)} collective-permute-done((s16[32,2176]{1,0:T(8,128)(2,1)S(1)}, s16[32,2176]{1,0:T(8,128)(2,1)S(1)}, u32[]{:S(2)}, u32[]{:S(2)}) %collective-permute-start.21) | collective-permute-done | bytes 139296 | tf_op jit(solution)/shard_map/ppermute | solution.py:311
  145.6 2.9 %collective-permute-done.28.refs_9_ = s16[32,2176]{1,0:T(8,128)(2,1)S(1)} collective-permute-done((s16[32,2176]{1,0:T(8,128)(2,1)S(1)}, s16[32,2176]{1,0:T(8,128)(2,1)S(1)}, u32[]{:S(2)}, u32[]{:S(2)}) %collective-permute-start.28) | collective-permute-done | bytes 139296 | tf_op jit(solution)/shard_map/ppermute | solution.py:311
  150.1 1.3 collective-permute-start.31
  153.6 1.5 collective-permute-start.33
  156.3 2.8 %collective-permute-done.31.refs_5_ = s16[32,2176]{1,0:T(8,128)(2,1)S(1)} collective-permute-done((s16[32,2176]{1,0:T(8,128)(2,1)S(1)}, s16[32,2176]{1,0:T(8,128)(2,1)S(1)}, u32[]{:S(2)}, u32[]{:S(2)}) %collective-permute-start.31) | collective-permute-done | bytes 139296 | tf_op jit(solution)/shard_map/ppermute | solution.py:303
  159.1 1.4 collective-permute-done.33.refs_7_
  (60 shorter events, 22.1 us)
Async XLA Ops:
  47.3 12.9 %collective-permute-start.2 = (s16[64,3456]{1,0:T(8,128)(2,1)S(1)}, s16[64,3456]{1,0:T(8,128)(2,1)S(1)}, u32[]{:S(2)}, u32[]{:S(2)}) collective-permute-start(s16[64,3456]{1,0:T(8,128)(2,1)S(1)} %bitcast.19), channel_id=1, source_target_pairs={{0,96},{16,112},{32,0},{48,16},{64,32},{80,48},{96,64},{112,80},{1... | collective-permute-start | bytes 1327112 | tf_op jit(solution)/shard_map/ppermute | solution.py:293
  50.1 13.5 %collective-permute-start.1 = (s16[64,3456]{1,0:T(8,128)(2,1)S(1)}, s16[64,3456]{1,0:T(8,128)(2,1)S(1)}, u32[]{:S(2)}, u32[]{:S(2)}) collective-permute-start(s16[64,3456]{1,0:T(8,128)(2,1)S(1)} %bitcast.20), channel_id=1, source_target_pairs={{0,32},{16,48},{32,64},{48,80},{64,96},{80,112},{96,0},{112,16},{1... | collective-permute-start | bytes 1327112 | tf_op jit(solution)/shard_map/ppermute | solution.py:293
  64.1 12.1 %collective-permute-start.9 = (s16[64,3456]{1,0:T(8,128)(2,1)S(1)}, s16[64,3456]{1,0:T(8,128)(2,1)S(1)}, u32[]{:S(2)}, u32[]{:S(2)}) collective-permute-start(s16[64,3456]{1,0:T(8,128)(2,1)S(1)} %bitcast.17), channel_id=1, source_target_pairs={{0,96},{16,112},{32,0},{48,16},{64,32},{80,48},{96,64},{112,80},{1... | collective-permute-start | bytes 1327112 | tf_op jit(solution)/shard_map/ppermute | solution.py:293
  64.4 13.0 %collective-permute-start.8 = (s16[64,3456]{1,0:T(8,128)(2,1)S(1)}, s16[64,3456]{1,0:T(8,128)(2,1)S(1)}, u32[]{:S(2)}, u32[]{:S(2)}) collective-permute-start(s16[64,3456]{1,0:T(8,128)(2,1)S(1)} %bitcast.18), channel_id=1, source_target_pairs={{0,32},{16,48},{32,64},{48,80},{64,96},{80,112},{96,0},{112,16},{1... | collective-permute-start | bytes 1327112 | tf_op jit(solution)/shard_map/ppermute | solution.py:293
  77.9 13.3 %collective-permute-start.15 = (s16[64,3456]{1,0:T(8,128)(2,1)S(1)}, s16[64,3456]{1,0:T(8,128)(2,1)S(1)}, u32[]{:S(2)}, u32[]{:S(2)}) collective-permute-start(s16[64,3456]{1,0:T(8,128)(2,1)S(1)} %collective-permute-done.1.refs_2_), channel_id=1, source_target_pairs={{0,32},{16,48},{32,64},{48,80},{64,96},{80,112},{96,0},{112,16},{1... | collective-permute-start | bytes 1327112 | tf_op jit(solution)/shard_map/ppermute | solution.py:293
  78.4 12.8 %collective-permute-start.16 = (s16[64,3456]{1,0:T(8,128)(2,1)S(1)}, s16[64,3456]{1,0:T(8,128)(2,1)S(1)}, u32[]{:S(2)}, u32[]{:S(2)}) collective-permute-start(s16[64,3456]{1,0:T(8,128)(2,1)S(1)} %collective-permute-done.9.refs_0_), channel_id=1, source_target_pairs={{0,96},{16,112},{32,0},{48,16},{64,32},{80,48},{96,64},{112,80},{1... | collective-permute-start | bytes 1327112 | tf_op jit(solution)/shard_map/ppermute | solution.py:293
  91.2 19.7 %collective-permute-start.17 = (s16[64,3456]{1,0:T(8,128)(2,1)S(1)}, s16[64,3456]{1,0:T(8,128)(2,1)S(1)}, u32[]{:S(2)}, u32[]{:S(2)}) collective-permute-start(s16[64,3456]{1,0:T(8,128)(2,1)S(1)} %collective-permute-done.15.refs_0_), channel_id=1, source_target_pairs={{0,16},{16,0},{32,48},{48,32},{64,80},{80,64},{96,112},{112,96},{1... | collective-permute-start | bytes 1327112 | tf_op jit(solution)/shard_map/ppermute | solution.py:297
  91.2 20.5 %collective-permute-start.18 = (s16[64,3456]{1,0:T(8,128)(2,1)S(1)}, s16[64,3456]{1,0:T(8,128)(2,1)S(1)}, u32[]{:S(2)}, u32[]{:S(2)}) collective-permute-start(s16[64,3456]{1,0:T(8,128)(2,1)S(1)} %collective-permute-done.16.refs_2_), channel_id=1, source_target_pairs={{0,16},{16,0},{32,48},{48,32},{64,80},{80,64},{96,112},{112,96},{1... | collective-permute-start | bytes 1327112 | tf_op jit(solution)/shard_map/ppermute | solution.py:297
  91.7 15.8 %collective-permute-start.3 = (s16[64,2176]{1,0:T(8,128)(2,1)S(1)}, s16[64,2176]{1,0:T(8,128)(2,1)S(1)}, u32[]{:S(2)}, u32[]{:S(2)}) collective-permute-start(s16[64,2176]{1,0:T(8,128)(2,1)S(1)} %get-tuple-element.57), channel_id=1, source_target_pairs={{0,1},{1,2},{2,3},{3,0},{4,5},{5,6},{6,7},{7,4},{8,9},{9,10},{10,1... | collective-permute-start | bytes 835592 | tf_op jit(solution)/shard_map/ppermute | solution.py:311
  92.3 15.2 %collective-permute-start.4 = (s16[64,2176]{1,0:T(8,128)(2,1)S(1)}, s16[64,2176]{1,0:T(8,128)(2,1)S(1)}, u32[]{:S(2)}, u32[]{:S(2)}) collective-permute-start(s16[64,2176]{1,0:T(8,128)(2,1)S(1)} %get-tuple-element.58), channel_id=1, source_target_pairs={{0,2},{1,3},{2,0},{3,1},{4,6},{5,7},{6,4},{7,5},{8,10},{9,11},{10,... | collective-permute-start | bytes 835592 | tf_op jit(solution)/shard_map/ppermute | solution.py:311
  93.7 14.9 %collective-permute-start.5 = (s16[64,2176]{1,0:T(8,128)(2,1)S(1)}, s16[64,2176]{1,0:T(8,128)(2,1)S(1)}, u32[]{:S(2)}, u32[]{:S(2)}) collective-permute-start(s16[64,2176]{1,0:T(8,128)(2,1)S(1)} %get-tuple-element.59), channel_id=1, source_target_pairs={{0,3},{1,0},{2,1},{3,2},{4,7},{5,4},{6,5},{7,6},{8,11},{9,8},{10,9... | collective-permute-start | bytes 835592 | tf_op jit(solution)/shard_map/ppermute | solution.py:311
  107.5 16.7 %collective-permute-start.10 = (s16[64,2176]{1,0:T(8,128)(2,1)S(1)}, s16[64,2176]{1,0:T(8,128)(2,1)S(1)}, u32[]{:S(2)}, u32[]{:S(2)}) collective-permute-start(s16[64,2176]{1,0:T(8,128)(2,1)S(1)} %get-tuple-element.66), channel_id=1, source_target_pairs={{0,1},{1,2},{2,3},{3,0},{4,5},{5,6},{6,7},{7,4},{8,9},{9,10},{10,1... | collective-permute-start | bytes 835592 | tf_op jit(solution)/shard_map/ppermute | solution.py:311
  107.5 18.4 %collective-permute-start.11 = (s16[64,2176]{1,0:T(8,128)(2,1)S(1)}, s16[64,2176]{1,0:T(8,128)(2,1)S(1)}, u32[]{:S(2)}, u32[]{:S(2)}) collective-permute-start(s16[64,2176]{1,0:T(8,128)(2,1)S(1)} %get-tuple-element.67), channel_id=1, source_target_pairs={{0,2},{1,3},{2,0},{3,1},{4,6},{5,7},{6,4},{7,5},{8,10},{9,11},{10,... | collective-permute-start | bytes 835592 | tf_op jit(solution)/shard_map/ppermute | solution.py:311
  108.6 17.7 %collective-permute-start.12 = (s16[64,2176]{1,0:T(8,128)(2,1)S(1)}, s16[64,2176]{1,0:T(8,128)(2,1)S(1)}, u32[]{:S(2)}, u32[]{:S(2)}) collective-permute-start(s16[64,2176]{1,0:T(8,128)(2,1)S(1)} %get-tuple-element.68), channel_id=1, source_target_pairs={{0,3},{1,0},{2,1},{3,2},{4,7},{5,4},{6,5},{7,6},{8,11},{9,8},{10,9... | collective-permute-start | bytes 835592 | tf_op jit(solution)/shard_map/ppermute | solution.py:311
  110.9 27.3 %collective-permute-start.25 = (s16[64,2176]{1,0:T(8,128)(2,1)S(1)}, s16[64,2176]{1,0:T(8,128)(2,1)S(1)}, u32[]{:S(2)}, u32[]{:S(2)}) collective-permute-start(s16[64,2176]{1,0:T(8,128)(2,1)S(1)} %get-tuple-element.85), channel_id=1, source_target_pairs={{0,1},{1,2},{2,3},{3,0},{4,5},{5,6},{6,7},{7,4},{8,9},{9,10},{10,1... | collective-permute-start | bytes 835592 | tf_op jit(solution)/shard_map/ppermute | solution.py:311
  111.7 33.6 %collective-permute-start.26 = (s16[64,2176]{1,0:T(8,128)(2,1)S(1)}, s16[64,2176]{1,0:T(8,128)(2,1)S(1)}, u32[]{:S(2)}, u32[]{:S(2)}) collective-permute-start(s16[64,2176]{1,0:T(8,128)(2,1)S(1)} %get-tuple-element.86), channel_id=1, source_target_pairs={{0,2},{1,3},{2,0},{3,1},{4,6},{5,7},{6,4},{7,5},{8,10},{9,11},{10,... | collective-permute-start | bytes 835592 | tf_op jit(solution)/shard_map/ppermute | solution.py:311
  124.2 21.1 %collective-permute-start.27 = (s16[64,2176]{1,0:T(8,128)(2,1)S(1)}, s16[64,2176]{1,0:T(8,128)(2,1)S(1)}, u32[]{:S(2)}, u32[]{:S(2)}) collective-permute-start(s16[64,2176]{1,0:T(8,128)(2,1)S(1)} %get-tuple-element.87), channel_id=1, source_target_pairs={{0,3},{1,0},{2,1},{3,2},{4,7},{5,4},{6,5},{7,6},{8,11},{9,8},{10,9... | collective-permute-start | bytes 835592 | tf_op jit(solution)/shard_map/ppermute | solution.py:311
  126.0 13.9 %collective-permute-start.19 = (s16[32,2176]{1,0:T(8,128)(2,1)S(1)}, s16[32,2176]{1,0:T(8,128)(2,1)S(1)}, u32[]{:S(2)}, u32[]{:S(2)}) collective-permute-start(s16[32,2176]{1,0:T(8,128)(2,1)S(1)} %get-tuple-element.77), channel_id=1, source_target_pairs={{0,1},{1,2},{2,3},{3,0},{4,5},{5,6},{6,7},{7,4},{8,9},{9,10},{10,1... | collective-permute-start | bytes 417800 | tf_op jit(solution)/shard_map/ppermute | solution.py:311
  126.3 13.9 %collective-permute-start.20 = (s16[32,2176]{1,0:T(8,128)(2,1)S(1)}, s16[32,2176]{1,0:T(8,128)(2,1)S(1)}, u32[]{:S(2)}, u32[]{:S(2)}) collective-permute-start(s16[32,2176]{1,0:T(8,128)(2,1)S(1)} %get-tuple-element.78), channel_id=1, source_target_pairs={{0,2},{1,3},{2,0},{3,1},{4,6},{5,7},{6,4},{7,5},{8,10},{9,11},{10,... | collective-permute-start | bytes 417800 | tf_op jit(solution)/shard_map/ppermute | solution.py:311
  139.9 8.6 %collective-permute-start.28 = (s16[32,2176]{1,0:T(8,128)(2,1)S(1)}, s16[32,2176]{1,0:T(8,128)(2,1)S(1)}, u32[]{:S(2)}, u32[]{:S(2)}) collective-permute-start(s16[32,2176]{1,0:T(8,128)(2,1)S(1)} %get-tuple-element.89), channel_id=1, source_target_pairs={{0,1},{1,2},{2,3},{3,0},{4,5},{5,6},{6,7},{7,4},{8,9},{9,10},{10,1... | collective-permute-start | bytes 417800 | tf_op jit(solution)/shard_map/ppermute | solution.py:311
  140.2 8.5 %collective-permute-start.29 = (s16[32,2176]{1,0:T(8,128)(2,1)S(1)}, s16[32,2176]{1,0:T(8,128)(2,1)S(1)}, u32[]{:S(2)}, u32[]{:S(2)}) collective-permute-start(s16[32,2176]{1,0:T(8,128)(2,1)S(1)} %get-tuple-element.90), channel_id=1, source_target_pairs={{0,2},{1,3},{2,0},{3,1},{4,6},{5,7},{6,4},{7,5},{8,10},{9,11},{10,... | collective-permute-start | bytes 417800 | tf_op jit(solution)/shard_map/ppermute | solution.py:311
  145.3 8.3 %collective-permute-start.22 = (s16[32,2176]{1,0:T(8,128)(2,1)S(1)}, s16[32,2176]{1,0:T(8,128)(2,1)S(1)}, u32[]{:S(2)}, u32[]{:S(2)}) collective-permute-start(s16[32,2176]{1,0:T(8,128)(2,1)S(1)} %get-tuple-element.81), channel_id=1, source_target_pairs={{0,4},{1,5},{2,6},{3,7},{4,8},{5,9},{6,10},{7,11},{8,12},{9,13},{1... | collective-permute-start | bytes 417800 | tf_op jit(solution)/shard_map/ppermute | solution.py:303
  145.4 10.4 %collective-permute-start.23 = (s16[32,2176]{1,0:T(8,128)(2,1)S(1)}, s16[32,2176]{1,0:T(8,128)(2,1)S(1)}, u32[]{:S(2)}, u32[]{:S(2)}) collective-permute-start(s16[32,2176]{1,0:T(8,128)(2,1)S(1)} %get-tuple-element.82), channel_id=1, source_target_pairs={{0,8},{1,9},{2,10},{3,11},{4,12},{5,13},{6,14},{7,15},{8,0},{9,1},... | collective-permute-start | bytes 417800 | tf_op jit(solution)/shard_map/ppermute | solution.py:303
  150.1 9.0 %collective-permute-start.31 = (s16[32,2176]{1,0:T(8,128)(2,1)S(1)}, s16[32,2176]{1,0:T(8,128)(2,1)S(1)}, u32[]{:S(2)}, u32[]{:S(2)}) collective-permute-start(s16[32,2176]{1,0:T(8,128)(2,1)S(1)} %get-tuple-element.93), channel_id=1, source_target_pairs={{0,4},{1,5},{2,6},{3,7},{4,8},{5,9},{6,10},{7,11},{8,12},{9,13},{1... | collective-permute-start | bytes 417800 | tf_op jit(solution)/shard_map/ppermute | solution.py:303
  (11 other events, 118.1 us)

commit v2 on v1

--- a/solution.py
+++ b/solution.py
@@ -55,7 +55,7 @@
     return jnp.floor((index.astype(F32) + 0.5) * (1.0 / HAD)).astype(I32)
 
 
-def rotate_kernel(x_ref, had_ref, w_ref, code_ref, held_ref, matrix, mixed, sem):
+def rotate_kernel(x_ref, had_ref, w_ref, code_ref, held_ref, matrix, stacked, mixed, sem):
     fetch = pltpu.make_async_copy(w_ref, held_ref, sem)
     fetch.start()
     width = matrix.shape[0]
@@ -77,13 +77,13 @@
     rows = x_ref.shape[0]
     count = rows // 8
     for half in range(2):
-        span = slice(half * width, (half + 1) * width)
-        mixed[:, span] = jnp.dot(x_ref[:, span], matrix[...], preferred_element_type=F32)
+        stacked[half * rows : (half + 1) * rows, :] = x_ref[:, half * width : (half + 1) * width]
+    mixed[...] = jnp.dot(stacked[...], matrix[...], preferred_element_type=F32)
     norm_factor = jnp.float32(1.0 / math.sqrt(FF))
     top = jnp.zeros((8, LANES), F32)
     for tile in range(width // LANES):
-        columns = [slice(half * width + tile * LANES, half * width + (tile + 1) * LANES) for half in range(2)]
-        values = [mixed[8 * t : 8 * t + 8, span] for span in columns for t in range(count)]
+        span = slice(tile * LANES, (tile + 1) * LANES)
+        values = [mixed[8 * t : 8 * t + 8, span] for t in range(2 * count)]
         step = 1
         while step < len(values):
             for low in range(len(values)):
@@ -92,20 +92,21 @@
                     values[low], values[low | step] = a + b, a - b
             step *= 2
         for index, value in enumerate(values):
-            half, t = index // count, index % count
             value = value * norm_factor
             top = jnp.maximum(top, jnp.abs(value))
-            mixed[8 * t : 8 * t + 8, columns[half]] = value
+            mixed[8 * index : 8 * index + 8, span] = value
     peak = jnp.max(top, axis=1, keepdims=True)
     act_scale = clip_ratio / 7.0 * (peak + epsilon)
     inverse = jnp.broadcast_to(1.0 / act_scale, (8, LANES))
     for t in range(count // 2):
         for tile in range(2 * width // LANES):
             span = slice(tile * LANES, (tile + 1) * LANES)
+            half, place = divmod(tile, width // LANES)
             halves = []
             for part in range(2):
-                start = 16 * t + 8 * part
-                quant = jnp.clip(mixed[start : start + 8, span] * inverse, -8.0, 7.0)
+                start = half * rows + 16 * t + 8 * part
+                value = mixed[start : start + 8, place * LANES : (place + 1) * LANES]
+                quant = jnp.clip(value * inverse, -8.0, 7.0)
                 root = jnp.sqrt(jnp.abs(quant)) * (CODE_TOP / math.sqrt(8.0))
                 halves.append(jnp.round(jnp.where(quant < 0, -root, root)))
             code_ref[16 * t : 16 * t + 16, span] = jnp.concatenate(halves, 0).astype(I32).astype(I16)
@@ -140,7 +141,8 @@
         out_specs=[vmem(), vmem()],
         scratch_shapes=[
             pltpu.VMEM((columns // 2, columns // 2), BF16),
-            pltpu.VMEM((rows, columns), F32),
+            pltpu.VMEM((2 * rows, columns // 2), BF16),
+            pltpu.VMEM((2 * rows, columns // 2), F32),
             pltpu.SemaphoreType.DMA,
         ],
         compiler_params=params(34),
@@ -148,11 +150,12 @@
     )(x, had_small, weight)
 
 
-def product_kernel(strides, parts, *refs):
-    codes, w_ref = refs[:4], refs[4]
-    outs, (lhs, total, scale) = refs[5:-3], refs[-3:]
-    rows = scale.shape[0] // 4
-    size = rows // 2
+def product_kernel(strides, groups, *refs):
+    count = 2 * groups
+    codes, w_ref = refs[:count], refs[count]
+    sends, kept, (lhs, total, scale) = refs[count + 1 : count + 4], refs[count + 4], refs[-3:]
+    rows = scale.shape[0] // count
+    size = kept.shape[0] // groups
     depth, width = w_ref.shape
     for index, ref in enumerate(codes):
         base = index * rows
@@ -164,51 +167,50 @@
             high = quant.astype(BF16)
             low = (quant - high.astype(F32)).astype(BF16)
             lhs[base : base + rows, span] = high
-            lhs[4 * rows + base : 4 * rows + base + rows, span] = low
+            lhs[count * rows + base : count * rows + base + rows, span] = low
 
     def columns(step, carry):
         start = pl.multiple_of(step * BLOCK, BLOCK)
         both = jnp.dot(lhs[...], w_ref[:, pl.ds(start, BLOCK)], preferred_element_type=F32)
-        total[:, pl.ds(start, BLOCK)] = (both[: 4 * rows] + both[4 * rows :]) * scale[:, 0:1]
+        total[:, pl.ds(start, BLOCK)] = (both[: count * rows] + both[count * rows :]) * scale[:, 0:1]
         return carry
 
     lax.fori_loop(0, width // BLOCK, columns, 0)
-    for group in range(2):
-        chosen = outs if parts == 1 else outs[4 * group : 4 * group + 4]
-        span = slice(group * size, (group + 1) * size) if parts == 1 else slice(None)
+    for group in range(groups):
+        span = slice(group * size, (group + 1) * size)
         for d in range(4):
             first = pl.multiple_of(group * strides[0] + place_of(d) * strides[1], size)
             value = total[pl.ds(first, size), :]
             if d == 0:
-                chosen[3][span, :] = value
+                kept[span, :] = value
             else:
-                pack(value, chosen[d - 1], span)
-
-
-def product(codes, weight, strides, parts=1):
-    rows = ROWS
-    depth, width = weight.shape
-    size = rows // parts
-    outs = [jax.ShapeDtypeStruct((size, width + LANES), I16)] * 3 + [jax.ShapeDtypeStruct((size, width), F32)]
-    outs = outs * parts
+                pack(value, sends[d - 1], span)
+
+
+def product(codes, weight, strides):
+    rows, depth, width = ROWS, *weight.shape
+    groups = len(codes) // 2
+    size = groups * rows // 2
+    message = jax.ShapeDtypeStruct((size, width + LANES), I16)
+    outs = [message] * 3 + [jax.ShapeDtypeStruct((size, width), F32)]
     specs = [
         pl.BlockSpec((rows, depth + LANES), functools.partial(lambda index, n: (index, 0), index))
         for _, index in codes
     ]
     return pl.pallas_call(
-        functools.partial(product_kernel, strides, parts),
+        functools.partial(product_kernel, strides, groups),
         grid=(1,),
         out_shape=outs,
         in_specs=specs + [vmem()],
         out_specs=[pl.BlockSpec(out.shape, lambda n: (0, 0)) for out in outs],
         scratch_shapes=[
-            pltpu.VMEM((8 * rows, depth), BF16),
-            pltpu.VMEM((4 * rows, width), F32),
-            pltpu.VMEM((4 * rows, LANES), F32),
+            pltpu.VMEM((4 * groups * rows, depth), BF16),
+            pltpu.VMEM((2 * groups * rows, width), F32),
+            pltpu.VMEM((2 * groups * rows, LANES), F32),
         ],
         compiler_params=params(26),
         cost_estimate=pl.CostEstimate(
-            flops=16 * rows * depth * width,
+            flops=8 * groups * rows * depth * width,
             bytes_accessed=2 * depth * width,
             transcendentals=0,
         ),
@@ -336,22 +338,23 @@
     *sends, kept_0 = product(codes, weight, natural)
     sends, below_0, above_0 = lax.optimization_barrier((sends, below_0, above_0))
     got_0 = along_y(sends)
-    far_0 = along_x(below_0, 1)
+    far_0, far_1 = along_x(own_0, 2), along_x(own_1, 2)
     codes = [above_0, other_core(above_0), below_0, other_core(below_0)]
     *sends, kept_1 = product([(code, 0) for code in codes], weight, grouped)
     sends, below_1, above_1 = lax.optimization_barrier((sends, below_1, above_1))
     got_1 = along_y(sends)
-    far_1 = along_x(above_1, -1)
     codes = [above_1, other_core(above_1), below_1, other_core(below_1)]
     *sends, kept_2 = product([(code, 0) for code in codes], weight, grouped)
-    sends, far_0, far_1 = lax.optimization_barrier((sends, far_0, far_1))
+    sends, far_0 = lax.optimization_barrier((sends, far_0))
     got_2 = along_y(sends)
-    codes = [far_0, other_core(far_0), far_1, other_core(far_1)]
-    outs = product([(code, 0) for code in codes], weight, grouped, 2)
-    got_a, got_b = along_y(outs[:3]), along_y(outs[4:7])
-    *sends, own_a = collect(0, [kept_0, *got_0], [kept_1, *got_1], [outs[3], *got_a])
+    *sends, kept_a = product([(far_0, 0), (other_core(far_0), 0)], weight, grouped)
+    sends, far_1 = lax.optimization_barrier((sends, far_1))
+    got_a = along_y(sends)
+    *sends, kept_b = product([(far_1, 0), (other_core(far_1), 0)], weight, grouped)
+    got_b = along_y(sends)
+    *sends, own_a = collect(0, [kept_0, *got_0], [kept_1, *got_1], [kept_a, *got_a])
     end_a = along_z(sends)
-    *sends, own_b = collect(1, [kept_0, *got_0], [kept_2, *got_2], [outs[7], *got_b])
+    *sends, own_b = collect(1, [kept_0, *got_0], [kept_2, *got_2], [kept_b, *got_b])
     end_b = along_z(sends)
     mixed = finish(w_scale[None, :], [own_a, *end_a, own_b, *end_b])
     return (mixed, act_scale)

time: 163 us -> 163 us (level)
    ppermute x15, waiting for transfers between devices: 31.8 us -> 24.4 us  [along_y(): got.append(lax.ppermute(block, 'tensor', route))]
    ppermute x6, waiting for transfers between devices: 6.8 us -> 13 us  [along_x(): lax.ppermute(block, 'seq', [(i, (i + 2 * apart) % 8) for i in range(8)])]
    ppermute x6, starting transfers between devices: 4.39 us -> 8.01 us  [along_z(): lax.ppermute(block, 'tensor', [(i, (i + 4 * apart) % 16) for i in range(1...]
    pallas_call x4 -> x5, Pallas kernels: 37.3 us -> 38.4 us  [product(): pl.pallas_call(functools.partial(product_kernel, strides, groups), grid=(...]
  transfers between devices with their start and end apart: 34 -> 34, of which waited for: 16 -> 17; matrix products, arithmetic and copies ran while one was open for 0% -> 0% of each run, Pallas kernels for 24% -> 25%
where the time goes in v2:
time: 163 us; the launch traced here: 162 us
  Pallas kernels  46 us (28%)
  waiting for transfers between devices  43.5 us (27%)
  blocking collectives  40.9 us (25%)
  starting transfers between devices  29.6 us (18%)
    pallas_call x5, Pallas kernels, product(): pl.pallas_call(functools.partial(product_kernel, strides, groups), grid=(...  38.4 us
    ppermute x15, waiting for transfers between devices, along_y(): got.append(lax.ppermute(block, 'tensor', route))  24.4 us
    all_to_all x1, blocking collectives, step(): lax.all_to_all(sent, 'tensor', split_axis=0, concat_axis=0, tiled=True)  23.2 us
    all_to_all x1, blocking collectives, step(): lax.all_to_all(code, 'tensor', split_axis=0, concat_axis=0, tiled=True)  17.7 us
    ppermute x15, starting transfers between devices, along_y(): got.append(lax.ppermute(block, 'tensor', route))  14 us
    ppermute x6, waiting for transfers between devices, along_x(): lax.ppermute(block, 'seq', [(i, (i + 2 * apart) % 8) for i in range(8)])  13 us
    ppermute x6, starting transfers between devices, along_z(): lax.ppermute(block, 'tensor', [(i, (i + 4 * apart) % 16) for i in range(1...  8.01 us
    ppermute x6, starting transfers between devices, along_x(): lax.ppermute(block, 'seq', [(i, (i + 2 * apart) % 8) for i in range(8)])  6.57 us
  transfers between devices with their start and end apart: 34, of which 17 were waited for; matrix products, arithmetic and copies ran while one was open for 0% of the time, Pallas kernels for 25%

profile of v2, /device:TPU:0, one launch (start us, length us, event | category | flops | bytes accessed | tf_op | source)
XLA Modules:
  0.0 162.2 jit_solution(30564325646801462)
XLA Ops:
  1.4 23.2 %all_to_all.10 = bf16[16,8,3328]{2,1,0:T(8,128)(2,1)S(1)} all-to-all(bf16[16,8,3328]{2,1,0:T(8,128)(2,1)} %bitcast.16), channel_id=1, replica_groups=mesh['seq'=8,'tensor'=16] {'tensor'}, dimensions={0} | all-to-all | bytes 1703936 | tf_op jit(solution)/shard_map/all_to_all | solution.py:323
  24.6 4.9 %rotate.1 = (s16[128,3456]{1,0:T(8,128)(2,1)S(1)}, bf16[3328,2048]{1,0:T(8,128)(2,1)S(1)}) custom-call(bf16[128,3328]{1,0:T(8,128)(2,1)S(1)} %bitcast.13, bf16[52,52]{1,0:T(8,128)(2,1)S(1)} %convert_element_type.9.had_ref, bf16[3328,2048]{1,0:T(8,128)(2,1)} %w_ref.1), custom_call_target="tpu_custom_call" | custom-call | tf_op jit(solution)/shard_map/rotate/pallas_call | solution.py:134
  29.5 17.7 %all_to_all.11 = s16[16,8,3456]{2,1,0:T(8,128)(2,1)S(1)} all-to-all(s16[16,8,3456]{2,1,0:T(8,128)(2,1)S(1)} %bitcast.14), channel_id=1, replica_groups=mesh['seq'=8,'tensor'=16] {'tensor'}, dimensions={0} | all-to-all | bytes 1769472 | tf_op jit(solution)/shard_map/all_to_all | solution.py:326
  47.3 2.8 %collective-permute-start.2 = (s16[64,3456]{1,0:T(8,128)(2,1)S(1)}, s16[64,3456]{1,0:T(8,128)(2,1)S(1)}, u32[]{:S(2)}, u32[]{:S(2)}) collective-permute-start(s16[64,3456]{1,0:T(8,128)(2,1)S(1)} %bitcast.20), channel_id=1, source_target_pairs={{0,96},{16,112},{32,0},{48,16},{64,32},{80,48},{96,64},{112,80},{1... | collective-permute-start | bytes 1327112 | tf_op jit(solution)/shard_map/ppermute | solution.py:295
  50.1 9.3 %shard_map.59 = (s16[64,2176]{1,0:T(8,128)(2,1)S(1)}, s16[64,2176]{1,0:T(8,128)(2,1)S(1)}, s16[64,2176]{1,0:T(8,128)(2,1)S(1)}, f32[64,2048]{1,0:T(8,128)S(1)}) custom-call(s16[128,3456]{1,0:T(8,128)(2,1)S(1)} %bitcast.10, s16[128,3456]{1,0:T(8,128)(2,1)S(1)} %bitcast.11, s16[128,3456]{1,0:T(8,128)(2,1)S(1)} %collective-permute-done.refs_2_.refs_3_, ...), custom_call_target="tpu_custom_call" | custom-call | flops 6979321856 | bytes 13631488 | tf_op jit(solution)/shard_map/pallas_call | solution.py:200
  60.2 3.4 %collective-permute-done.1.refs_2_ = s16[64,3456]{1,0:T(8,128)(2,1)S(1)} collective-permute-done((s16[64,3456]{1,0:T(8,128)(2,1)S(1)}, s16[64,3456]{1,0:T(8,128)(2,1)S(1)}, u32[]{:S(2)}, u32[]{:S(2)}) %collective-permute-start.1) | collective-permute-done | bytes 442400 | tf_op jit(solution)/shard_map/ppermute | solution.py:295
  64.4 1.7 %collective-permute-start.8 = (s16[64,3456]{1,0:T(8,128)(2,1)S(1)}, s16[64,3456]{1,0:T(8,128)(2,1)S(1)}, u32[]{:S(2)}, u32[]{:S(2)}) collective-permute-start(s16[64,3456]{1,0:T(8,128)(2,1)S(1)} %bitcast.18), channel_id=1, source_target_pairs={{0,32},{16,48},{32,64},{48,80},{64,96},{80,112},{96,0},{112,16},{1... | collective-permute-start | bytes 1327112 | tf_op jit(solution)/shard_map/ppermute | solution.py:295
  66.1 9.3 %shard_map.60 = (s16[64,2176]{1,0:T(8,128)(2,1)S(1)}, s16[64,2176]{1,0:T(8,128)(2,1)S(1)}, s16[64,2176]{1,0:T(8,128)(2,1)S(1)}, f32[64,2048]{1,0:T(8,128)S(1)}) custom-call(s16[64,3456]{1,0:T(8,128)(2,1)S(1)} %collective-permute-done.2.refs_0_, s16[64,3456]{1,0:T(8,128)(2,1)S(1)} %collective-permute-done.6.refs_1_, ...), custom_call_target="tpu_custom_call" | custom-call | flops 6979321856 | bytes 13631488 | tf_op jit(solution)/shard_map/pallas_call | solution.py:200
  79.8 9.3 %shard_map.61 = (s16[64,2176]{1,0:T(8,128)(2,1)S(1)}, s16[64,2176]{1,0:T(8,128)(2,1)S(1)}, s16[64,2176]{1,0:T(8,128)(2,1)S(1)}, f32[64,2048]{1,0:T(8,128)S(1)}) custom-call(s16[64,3456]{1,0:T(8,128)(2,1)S(1)} %collective-permute-done.9.refs_0_, s16[64,3456]{1,0:T(8,128)(2,1)S(1)} %collective-permute-done.13.refs_1_, ...), custom_call_target="tpu_custom_call" | custom-call | flops 6979321856 | bytes 13631488 | tf_op jit(solution)/shard_map/pallas_call | solution.py:200
  89.2 2.3 %collective-permute-done.15.refs_0_ = s16[64,3456]{1,0:T(8,128)(2,1)S(1)} collective-permute-done((s16[64,3456]{1,0:T(8,128)(2,1)S(1)}, s16[64,3456]{1,0:T(8,128)(2,1)S(1)}, u32[]{:S(2)}, u32[]{:S(2)}) %collective-permute-start.15) | collective-permute-done | bytes 442400 | tf_op jit(solution)/shard_map/ppermute | solution.py:295
  94.3 1.5 collective-permute-start.5
  95.8 5.2 %shard_map.62 = (s16[32,2176]{1,0:T(8,128)(2,1)S(1)}, s16[32,2176]{1,0:T(8,128)(2,1)S(1)}, s16[32,2176]{1,0:T(8,128)(2,1)S(1)}, f32[32,2048]{1,0:T(8,128)S(1)}) custom-call(s16[64,3456]{1,0:T(8,128)(2,1)S(1)} %collective-permute-done.15.refs_0_, s16[64,3456]{1,0:T(8,128)(2,1)S(1)} %collective-permute-done.16.refs_1_, ...), custom_call_target="tpu_custom_call" | custom-call | flops 3489660928 | bytes 13631488 | tf_op jit(solution)/shard_map/pallas_call | solution.py:200
  101.0 4.6 %collective-permute-done.17.refs_0_ = s16[64,3456]{1,0:T(8,128)(2,1)S(1)} collective-permute-done((s16[64,3456]{1,0:T(8,128)(2,1)S(1)}, s16[64,3456]{1,0:T(8,128)(2,1)S(1)}, u32[]{:S(2)}, u32[]{:S(2)}) %collective-permute-start.17) | collective-permute-done | bytes 442400 | tf_op jit(solution)/shard_map/ppermute | solution.py:295
  106.2 2.1 %collective-permute-done.3.refs_1_ = s16[64,2176]{1,0:T(8,128)(2,1)S(1)} collective-permute-done((s16[64,2176]{1,0:T(8,128)(2,1)S(1)}, s16[64,2176]{1,0:T(8,128)(2,1)S(1)}, u32[]{:S(2)}, u32[]{:S(2)}) %collective-permute-start.3) | collective-permute-done | bytes 278560 | tf_op jit(solution)/shard_map/ppermute | solution.py:313
  110.4 11.9 %collective-permute-done.10.refs_5_ = s16[64,2176]{1,0:T(8,128)(2,1)S(1)} collective-permute-done((s16[64,2176]{1,0:T(8,128)(2,1)S(1)}, s16[64,2176]{1,0:T(8,128)(2,1)S(1)}, u32[]{:S(2)}, u32[]{:S(2)}) %collective-permute-start.10) | collective-permute-done | bytes 278560 | tf_op jit(solution)/shard_map/ppermute | solution.py:313
  122.6 1.7 %collective-permute-start.18 = (s16[32,2176]{1,0:T(8,128)(2,1)S(1)}, s16[32,2176]{1,0:T(8,128)(2,1)S(1)}, u32[]{:S(2)}, u32[]{:S(2)}) collective-permute-start(s16[32,2176]{1,0:T(8,128)(2,1)S(1)} %get-tuple-element.82), channel_id=1, source_target_pairs={{0,1},{1,2},{2,3},{3,0},{4,5},{5,6},{6,7},{7,4},{8,9},{9,10},{10,1... | collective-permute-start | bytes 417800 | tf_op jit(solution)/shard_map/ppermute | solution.py:313
  124.3 9.9 %collective-permute-done.24.refs_5_ = s16[64,2176]{1,0:T(8,128)(2,1)S(1)} collective-permute-done((s16[64,2176]{1,0:T(8,128)(2,1)S(1)}, s16[64,2176]{1,0:T(8,128)(2,1)S(1)}, u32[]{:S(2)}, u32[]{:S(2)}) %collective-permute-start.24) | collective-permute-done | bytes 278560 | tf_op jit(solution)/shard_map/ppermute | solution.py:313
  134.2 5.2 %shard_map.64 = (s16[32,2176]{1,0:T(8,128)(2,1)S(1)}, s16[32,2176]{1,0:T(8,128)(2,1)S(1)}, s16[32,2176]{1,0:T(8,128)(2,1)S(1)}, f32[32,2048]{1,0:T(8,128)S(1)}) custom-call(s16[64,3456]{1,0:T(8,128)(2,1)S(1)} %collective-permute-done.17.refs_0_, s16[64,3456]{1,0:T(8,128)(2,1)S(1)} %collective-permute-done.27.refs_1_, ...), custom_call_target="tpu_custom_call" | custom-call | flops 3489660928 | bytes 13631488 | tf_op jit(solution)/shard_map/pallas_call | solution.py:200
  139.5 2.1 %collective-permute-start.28 = (s16[32,2176]{1,0:T(8,128)(2,1)S(1)}, s16[32,2176]{1,0:T(8,128)(2,1)S(1)}, u32[]{:S(2)}, u32[]{:S(2)}) collective-permute-start(s16[32,2176]{1,0:T(8,128)(2,1)S(1)} %get-tuple-element.95), channel_id=1, source_target_pairs={{0,1},{1,2},{2,3},{3,0},{4,5},{5,6},{6,7},{7,4},{8,9},{9,10},{10,1... | collective-permute-start | bytes 417800 | tf_op jit(solution)/shard_map/ppermute | solution.py:313
  141.6 3.5 %collective-permute-start.29 = (s16[32,2176]{1,0:T(8,128)(2,1)S(1)}, s16[32,2176]{1,0:T(8,128)(2,1)S(1)}, u32[]{:S(2)}, u32[]{:S(2)}) collective-permute-start(s16[32,2176]{1,0:T(8,128)(2,1)S(1)} %get-tuple-element.96), channel_id=1, source_target_pairs={{0,2},{1,3},{2,0},{3,1},{4,6},{5,7},{6,4},{7,5},{8,10},{9,11},{10,... | collective-permute-start | bytes 417800 | tf_op jit(solution)/shard_map/ppermute | solution.py:313
  146.7 2.3 %collective-permute-start.22 = (s16[32,2176]{1,0:T(8,128)(2,1)S(1)}, s16[32,2176]{1,0:T(8,128)(2,1)S(1)}, u32[]{:S(2)}, u32[]{:S(2)}) collective-permute-start(s16[32,2176]{1,0:T(8,128)(2,1)S(1)} %get-tuple-element.87), channel_id=1, source_target_pairs={{0,8},{1,9},{2,10},{3,11},{4,12},{5,13},{6,14},{7,15},{8,0},{9,1},... | collective-permute-start | bytes 417800 | tf_op jit(solution)/shard_map/ppermute | solution.py:305
  151.9 1.9 %collective-permute-start.32 = (s16[32,2176]{1,0:T(8,128)(2,1)S(1)}, s16[32,2176]{1,0:T(8,128)(2,1)S(1)}, u32[]{:S(2)}, u32[]{:S(2)}) collective-permute-start(s16[32,2176]{1,0:T(8,128)(2,1)S(1)} %get-tuple-element.100), channel_id=1, source_target_pairs={{0,8},{1,9},{2,10},{3,11},{4,12},{5,13},{6,14},{7,15},{8,0},{9,1},... | collective-permute-start | bytes 417800 | tf_op jit(solution)/shard_map/ppermute | solution.py:305
  154.7 1.7 %collective-permute-start.33 = (s16[32,2176]{1,0:T(8,128)(2,1)S(1)}, s16[32,2176]{1,0:T(8,128)(2,1)S(1)}, u32[]{:S(2)}, u32[]{:S(2)}) collective-permute-start(s16[32,2176]{1,0:T(8,128)(2,1)S(1)} %get-tuple-element.101), channel_id=1, source_target_pairs={{0,12},{1,13},{2,14},{3,15},{4,0},{5,1},{6,2},{7,3},{8,4},{9,5},{1... | collective-permute-start | bytes 417800 | tf_op jit(solution)/shard_map/ppermute | solution.py:305
  157.6 2.8 %collective-permute-done.31.refs_5_ = s16[32,2176]{1,0:T(8,128)(2,1)S(1)} collective-permute-done((s16[32,2176]{1,0:T(8,128)(2,1)S(1)}, s16[32,2176]{1,0:T(8,128)(2,1)S(1)}, u32[]{:S(2)}, u32[]{:S(2)}) %collective-permute-start.31) | collective-permute-done | bytes 139296 | tf_op jit(solution)/shard_map/ppermute | solution.py:305
  (61 shorter events, 20.9 us)
Async XLA Ops:
  47.3 12.9 %collective-permute-start.2 = (s16[64,3456]{1,0:T(8,128)(2,1)S(1)}, s16[64,3456]{1,0:T(8,128)(2,1)S(1)}, u32[]{:S(2)}, u32[]{:S(2)}) collective-permute-start(s16[64,3456]{1,0:T(8,128)(2,1)S(1)} %bitcast.20), channel_id=1, source_target_pairs={{0,96},{16,112},{32,0},{48,16},{64,32},{80,48},{96,64},{112,80},{1... | collective-permute-start | bytes 1327112 | tf_op jit(solution)/shard_map/ppermute | solution.py:295
  50.1 13.5 %collective-permute-start.1 = (s16[64,3456]{1,0:T(8,128)(2,1)S(1)}, s16[64,3456]{1,0:T(8,128)(2,1)S(1)}, u32[]{:S(2)}, u32[]{:S(2)}) collective-permute-start(s16[64,3456]{1,0:T(8,128)(2,1)S(1)} %bitcast.21), channel_id=1, source_target_pairs={{0,32},{16,48},{32,64},{48,80},{64,96},{80,112},{96,0},{112,16},{1... | collective-permute-start | bytes 1327112 | tf_op jit(solution)/shard_map/ppermute | solution.py:295
  64.1 12.1 %collective-permute-start.9 = (s16[64,3456]{1,0:T(8,128)(2,1)S(1)}, s16[64,3456]{1,0:T(8,128)(2,1)S(1)}, u32[]{:S(2)}, u32[]{:S(2)}) collective-permute-start(s16[64,3456]{1,0:T(8,128)(2,1)S(1)} %bitcast.17), channel_id=1, source_target_pairs={{0,96},{16,112},{32,0},{48,16},{64,32},{80,48},{96,64},{112,80},{1... | collective-permute-start | bytes 1327112 | tf_op jit(solution)/shard_map/ppermute | solution.py:295
  64.4 13.0 %collective-permute-start.8 = (s16[64,3456]{1,0:T(8,128)(2,1)S(1)}, s16[64,3456]{1,0:T(8,128)(2,1)S(1)}, u32[]{:S(2)}, u32[]{:S(2)}) collective-permute-start(s16[64,3456]{1,0:T(8,128)(2,1)S(1)} %bitcast.18), channel_id=1, source_target_pairs={{0,32},{16,48},{32,64},{48,80},{64,96},{80,112},{96,0},{112,16},{1... | collective-permute-start | bytes 1327112 | tf_op jit(solution)/shard_map/ppermute | solution.py:295
  77.9 13.6 %collective-permute-start.15 = (s16[64,3456]{1,0:T(8,128)(2,1)S(1)}, s16[64,3456]{1,0:T(8,128)(2,1)S(1)}, u32[]{:S(2)}, u32[]{:S(2)}) collective-permute-start(s16[64,3456]{1,0:T(8,128)(2,1)S(1)} %bitcast.22), channel_id=1, source_target_pairs={{0,64},{16,80},{32,96},{48,112},{64,0},{80,16},{96,32},{112,48},{1... | collective-permute-start | bytes 1327112 | tf_op jit(solution)/shard_map/ppermute | solution.py:295
  91.5 14.1 %collective-permute-start.17 = (s16[64,3456]{1,0:T(8,128)(2,1)S(1)}, s16[64,3456]{1,0:T(8,128)(2,1)S(1)}, u32[]{:S(2)}, u32[]{:S(2)}) collective-permute-start(s16[64,3456]{1,0:T(8,128)(2,1)S(1)} %bitcast.19), channel_id=1, source_target_pairs={{0,64},{16,80},{32,96},{48,112},{64,0},{80,16},{96,32},{112,48},{1... | collective-permute-start | bytes 1327112 | tf_op jit(solution)/shard_map/ppermute | solution.py:295
  92.4 16.0 %collective-permute-start.3 = (s16[64,2176]{1,0:T(8,128)(2,1)S(1)}, s16[64,2176]{1,0:T(8,128)(2,1)S(1)}, u32[]{:S(2)}, u32[]{:S(2)}) collective-permute-start(s16[64,2176]{1,0:T(8,128)(2,1)S(1)} %get-tuple-element.60), channel_id=1, source_target_pairs={{0,1},{1,2},{2,3},{3,0},{4,5},{5,6},{6,7},{7,4},{8,9},{9,10},{10,1... | collective-permute-start | bytes 835592 | tf_op jit(solution)/shard_map/ppermute | solution.py:313
  93.0 15.4 %collective-permute-start.4 = (s16[64,2176]{1,0:T(8,128)(2,1)S(1)}, s16[64,2176]{1,0:T(8,128)(2,1)S(1)}, u32[]{:S(2)}, u32[]{:S(2)}) collective-permute-start(s16[64,2176]{1,0:T(8,128)(2,1)S(1)} %get-tuple-element.61), channel_id=1, source_target_pairs={{0,2},{1,3},{2,0},{3,1},{4,6},{5,7},{6,4},{7,5},{8,10},{9,11},{10,... | collective-permute-start | bytes 835592 | tf_op jit(solution)/shard_map/ppermute | solution.py:313
  94.3 14.7 %collective-permute-start.5 = (s16[64,2176]{1,0:T(8,128)(2,1)S(1)}, s16[64,2176]{1,0:T(8,128)(2,1)S(1)}, u32[]{:S(2)}, u32[]{:S(2)}) collective-permute-start(s16[64,2176]{1,0:T(8,128)(2,1)S(1)} %get-tuple-element.62), channel_id=1, source_target_pairs={{0,3},{1,0},{2,1},{3,2},{4,7},{5,4},{6,5},{7,6},{8,11},{9,8},{10,9... | collective-permute-start | bytes 835592 | tf_op jit(solution)/shard_map/ppermute | solution.py:313
  105.6 28.7 %collective-permute-start.27 = (s16[64,3456]{1,0:T(8,128)(2,1)S(1)}, s16[64,3456]{1,0:T(8,128)(2,1)S(1)}, u32[]{:S(2)}, u32[]{:S(2)}) collective-permute-start(s16[64,3456]{1,0:T(8,128)(2,1)S(1)} %collective-permute-done.17.refs_0_), channel_id=1, source_target_pairs={{0,16},{16,0},{32,48},{48,32},{64,80},{80,64},{96,112},{112,96},{1... | collective-permute-start | bytes 1327112 | tf_op jit(solution)/shard_map/ppermute | solution.py:299
  105.6 16.7 %collective-permute-start.10 = (s16[64,2176]{1,0:T(8,128)(2,1)S(1)}, s16[64,2176]{1,0:T(8,128)(2,1)S(1)}, u32[]{:S(2)}, u32[]{:S(2)}) collective-permute-start(s16[64,2176]{1,0:T(8,128)(2,1)S(1)} %get-tuple-element.69), channel_id=1, source_target_pairs={{0,1},{1,2},{2,3},{3,0},{4,5},{5,6},{6,7},{7,4},{8,9},{9,10},{10,1... | collective-permute-start | bytes 835592 | tf_op jit(solution)/shard_map/ppermute | solution.py:313
  108.3 14.0 %collective-permute-start.11 = (s16[64,2176]{1,0:T(8,128)(2,1)S(1)}, s16[64,2176]{1,0:T(8,128)(2,1)S(1)}, u32[]{:S(2)}, u32[]{:S(2)}) collective-permute-start(s16[64,2176]{1,0:T(8,128)(2,1)S(1)} %get-tuple-element.70), channel_id=1, source_target_pairs={{0,2},{1,3},{2,0},{3,1},{4,6},{5,7},{6,4},{7,5},{8,10},{9,11},{10,... | collective-permute-start | bytes 835592 | tf_op jit(solution)/shard_map/ppermute | solution.py:313
  108.3 14.3 %collective-permute-start.12 = (s16[64,2176]{1,0:T(8,128)(2,1)S(1)}, s16[64,2176]{1,0:T(8,128)(2,1)S(1)}, u32[]{:S(2)}, u32[]{:S(2)}) collective-permute-start(s16[64,2176]{1,0:T(8,128)(2,1)S(1)} %get-tuple-element.71), channel_id=1, source_target_pairs={{0,3},{1,0},{2,1},{3,2},{4,7},{5,4},{6,5},{7,6},{8,11},{9,8},{10,9... | collective-permute-start | bytes 835592 | tf_op jit(solution)/shard_map/ppermute | solution.py:313
  109.0 25.2 %collective-permute-start.24 = (s16[64,2176]{1,0:T(8,128)(2,1)S(1)}, s16[64,2176]{1,0:T(8,128)(2,1)S(1)}, u32[]{:S(2)}, u32[]{:S(2)}) collective-permute-start(s16[64,2176]{1,0:T(8,128)(2,1)S(1)} %get-tuple-element.90), channel_id=1, source_target_pairs={{0,1},{1,2},{2,3},{3,0},{4,5},{5,6},{6,7},{7,4},{8,9},{9,10},{10,1... | collective-permute-start | bytes 835592 | tf_op jit(solution)/shard_map/ppermute | solution.py:313
  122.3 24.3 %collective-permute-start.25 = (s16[64,2176]{1,0:T(8,128)(2,1)S(1)}, s16[64,2176]{1,0:T(8,128)(2,1)S(1)}, u32[]{:S(2)}, u32[]{:S(2)}) collective-permute-start(s16[64,2176]{1,0:T(8,128)(2,1)S(1)} %get-tuple-element.91), channel_id=1, source_target_pairs={{0,2},{1,3},{2,0},{3,1},{4,6},{5,7},{6,4},{7,5},{8,10},{9,11},{10,... | collective-permute-start | bytes 835592 | tf_op jit(solution)/shard_map/ppermute | solution.py:313
  122.3 24.3 %collective-permute-start.26 = (s16[64,2176]{1,0:T(8,128)(2,1)S(1)}, s16[64,2176]{1,0:T(8,128)(2,1)S(1)}, u32[]{:S(2)}, u32[]{:S(2)}) collective-permute-start(s16[64,2176]{1,0:T(8,128)(2,1)S(1)} %get-tuple-element.92), channel_id=1, source_target_pairs={{0,3},{1,0},{2,1},{3,2},{4,7},{5,4},{6,5},{7,6},{8,11},{9,8},{10,9... | collective-permute-start | bytes 835592 | tf_op jit(solution)/shard_map/ppermute | solution.py:313
  122.6 16.8 %collective-permute-start.18 = (s16[32,2176]{1,0:T(8,128)(2,1)S(1)}, s16[32,2176]{1,0:T(8,128)(2,1)S(1)}, u32[]{:S(2)}, u32[]{:S(2)}) collective-permute-start(s16[32,2176]{1,0:T(8,128)(2,1)S(1)} %get-tuple-element.82), channel_id=1, source_target_pairs={{0,1},{1,2},{2,3},{3,0},{4,5},{5,6},{6,7},{7,4},{8,9},{9,10},{10,1... | collective-permute-start | bytes 417800 | tf_op jit(solution)/shard_map/ppermute | solution.py:313
  134.2 10.9 %collective-permute-start.20 = (s16[32,2176]{1,0:T(8,128)(2,1)S(1)}, s16[32,2176]{1,0:T(8,128)(2,1)S(1)}, u32[]{:S(2)}, u32[]{:S(2)}) collective-permute-start(s16[32,2176]{1,0:T(8,128)(2,1)S(1)} %get-tuple-element.84), channel_id=1, source_target_pairs={{0,3},{1,0},{2,1},{3,2},{4,7},{5,4},{6,5},{7,6},{8,11},{9,8},{10,9... | collective-permute-start | bytes 417800 | tf_op jit(solution)/shard_map/ppermute | solution.py:313
  139.5 9.5 %collective-permute-start.28 = (s16[32,2176]{1,0:T(8,128)(2,1)S(1)}, s16[32,2176]{1,0:T(8,128)(2,1)S(1)}, u32[]{:S(2)}, u32[]{:S(2)}) collective-permute-start(s16[32,2176]{1,0:T(8,128)(2,1)S(1)} %get-tuple-element.95), channel_id=1, source_target_pairs={{0,1},{1,2},{2,3},{3,0},{4,5},{5,6},{6,7},{7,4},{8,9},{9,10},{10,1... | collective-permute-start | bytes 417800 | tf_op jit(solution)/shard_map/ppermute | solution.py:313
  141.6 8.6 %collective-permute-start.29 = (s16[32,2176]{1,0:T(8,128)(2,1)S(1)}, s16[32,2176]{1,0:T(8,128)(2,1)S(1)}, u32[]{:S(2)}, u32[]{:S(2)}) collective-permute-start(s16[32,2176]{1,0:T(8,128)(2,1)S(1)} %get-tuple-element.96), channel_id=1, source_target_pairs={{0,2},{1,3},{2,0},{3,1},{4,6},{5,7},{6,4},{7,5},{8,10},{9,11},{10,... | collective-permute-start | bytes 417800 | tf_op jit(solution)/shard_map/ppermute | solution.py:313
  146.7 10.4 %collective-permute-start.22 = (s16[32,2176]{1,0:T(8,128)(2,1)S(1)}, s16[32,2176]{1,0:T(8,128)(2,1)S(1)}, u32[]{:S(2)}, u32[]{:S(2)}) collective-permute-start(s16[32,2176]{1,0:T(8,128)(2,1)S(1)} %get-tuple-element.87), channel_id=1, source_target_pairs={{0,8},{1,9},{2,10},{3,11},{4,12},{5,13},{6,14},{7,15},{8,0},{9,1},... | collective-permute-start | bytes 417800 | tf_op jit(solution)/shard_map/ppermute | solution.py:305
  149.0 8.7 %collective-permute-start.23 = (s16[32,2176]{1,0:T(8,128)(2,1)S(1)}, s16[32,2176]{1,0:T(8,128)(2,1)S(1)}, u32[]{:S(2)}, u32[]{:S(2)}) collective-permute-start(s16[32,2176]{1,0:T(8,128)(2,1)S(1)} %get-tuple-element.88), channel_id=1, source_target_pairs={{0,12},{1,13},{2,14},{3,15},{4,0},{5,1},{6,2},{7,3},{8,4},{9,5},{1... | collective-permute-start | bytes 417800 | tf_op jit(solution)/shard_map/ppermute | solution.py:305
  151.0 9.3 %collective-permute-start.31 = (s16[32,2176]{1,0:T(8,128)(2,1)S(1)}, s16[32,2176]{1,0:T(8,128)(2,1)S(1)}, u32[]{:S(2)}, u32[]{:S(2)}) collective-permute-start(s16[32,2176]{1,0:T(8,128)(2,1)S(1)} %get-tuple-element.99), channel_id=1, source_target_pairs={{0,4},{1,5},{2,6},{3,7},{4,8},{5,9},{6,10},{7,11},{8,12},{9,13},{1... | collective-permute-start | bytes 417800 | tf_op jit(solution)/shard_map/ppermute | solution.py:305
  151.9 8.5 %collective-permute-start.32 = (s16[32,2176]{1,0:T(8,128)(2,1)S(1)}, s16[32,2176]{1,0:T(8,128)(2,1)S(1)}, u32[]{:S(2)}, u32[]{:S(2)}) collective-permute-start(s16[32,2176]{1,0:T(8,128)(2,1)S(1)} %get-tuple-element.100), channel_id=1, source_target_pairs={{0,8},{1,9},{2,10},{3,11},{4,12},{5,13},{6,14},{7,15},{8,0},{9,1},... | collective-permute-start | bytes 417800 | tf_op jit(solution)/shard_map/ppermute | solution.py:305
  (11 other events, 103.9 us)

commit v3 on v2

--- a/solution.py
+++ b/solution.py
@@ -19,6 +19,7 @@
 CODE_TOP = 32767.0
 SUM_TOP = 32700.0
 BLOCK = 512
+FETCH_ROOM = 28
 ROWS = 64
 
 
@@ -55,9 +56,7 @@
     return jnp.floor((index.astype(F32) + 0.5) * (1.0 / HAD)).astype(I32)
 
 
-def rotate_kernel(x_ref, had_ref, w_ref, code_ref, held_ref, matrix, stacked, mixed, sem):
-    fetch = pltpu.make_async_copy(w_ref, held_ref, sem)
-    fetch.start()
+def rotate_kernel(x_ref, had_ref, code_ref, matrix, stacked, mixed):
     width = matrix.shape[0]
     group = 4 * HAD
     row = iota((group, HAD), 0)
@@ -120,7 +119,6 @@
     extra = jnp.concatenate([pieces, pieces], 0).astype(I32).astype(I16)
     for t in range(count // 2):
         code_ref[16 * t : 16 * t + 16, 2 * width :] = extra
-    fetch.wait()
 
 
 def scale_of(pieces):
@@ -129,34 +127,39 @@
     return (total + parts[:, 1:2] * 2.0**-14 + parts[:, 0:1]) * 0.25
 
 
-def rotate(x, had_small, weight):
+def rotate(x, had_small):
     rows, columns = x.shape
     return pl.pallas_call(
         rotate_kernel,
-        out_shape=[
-            jax.ShapeDtypeStruct((rows, columns + LANES), I16),
-            jax.ShapeDtypeStruct(weight.shape, weight.dtype),
-        ],
-        in_specs=[vmem(), vmem(), pl.BlockSpec(memory_space=pltpu.HBM)],
-        out_specs=[vmem(), vmem()],
+        out_shape=jax.ShapeDtypeStruct((rows, columns + LANES), I16),
+        in_specs=[vmem(), vmem()],
+        out_specs=vmem(),
         scratch_shapes=[
             pltpu.VMEM((columns // 2, columns // 2), BF16),
             pltpu.VMEM((2 * rows, columns // 2), BF16),
             pltpu.VMEM((2 * rows, columns // 2), F32),
-            pltpu.SemaphoreType.DMA,
         ],
-        compiler_params=params(34),
+        compiler_params=params(24),
         name="rotate",
-    )(x, had_small, weight)
-
-
-def product_kernel(strides, groups, *refs):
+    )(x, had_small)
+
+
+def product_kernel(strides, groups, fetched, parts, *refs):
     count = 2 * groups
     codes, w_ref = refs[:count], refs[count]
-    sends, kept, (lhs, total, scale) = refs[count + 1 : count + 4], refs[count + 4], refs[-3:]
+    last = count + 1 + 4 * parts
+    outs = refs[count + 1 : last]
+    lhs, total, scale = refs[last + fetched : last + 3 + fetched]
     rows = scale.shape[0] // count
-    size = kept.shape[0] // groups
+    size = rows // 2
     depth, width = w_ref.shape
+    fetches = []
+    if fetched:
+        far_ref, w_ref, sem = w_ref, refs[last], refs[-1]
+        for step in range(width // BLOCK):
+            span = slice(step * BLOCK, (step + 1) * BLOCK)
+            fetches.append(pltpu.make_async_copy(far_ref.at[:, span], w_ref.at[:, span], sem.at[step]))
+            fetches[-1].start()
     for index, ref in enumerate(codes):
         base = index * rows
         scale[base : base + rows, :] = jnp.broadcast_to(scale_of(ref[:, depth:]), (rows, LANES))
@@ -170,45 +173,59 @@
             lhs[count * rows + base : count * rows + base + rows, span] = low
 
     def columns(step, carry):
-        start = pl.multiple_of(step * BLOCK, BLOCK)
+        if fetched:
+            start = step * BLOCK
+            fetches[step].wait()
+        else:
+            start = pl.multiple_of(step * BLOCK, BLOCK)
         both = jnp.dot(lhs[...], w_ref[:, pl.ds(start, BLOCK)], preferred_element_type=F32)
         total[:, pl.ds(start, BLOCK)] = (both[: count * rows] + both[count * rows :]) * scale[:, 0:1]
         return carry
 
-    lax.fori_loop(0, width // BLOCK, columns, 0)
+    if fetched:
+        for step in range(width // BLOCK):
+            columns(step, 0)
+    else:
+        lax.fori_loop(0, width // BLOCK, columns, 0)
     for group in range(groups):
-        span = slice(group * size, (group + 1) * size)
+        span = slice(group * size, (group + 1) * size) if parts == 1 else slice(None)
+        chosen = outs if parts == 1 else outs[4 * group : 4 * group + 4]
         for d in range(4):
             first = pl.multiple_of(group * strides[0] + place_of(d) * strides[1], size)
             value = total[pl.ds(first, size), :]
             if d == 0:
-                kept[span, :] = value
+                chosen[3][span, :] = value
             else:
-                pack(value, sends[d - 1], span)
-
-
-def product(codes, weight, strides):
+                pack(value, chosen[d - 1], span)
+
+
+def product(codes, weight, strides, fetched=False, parts=1):
     rows, depth, width = ROWS, *weight.shape
     groups = len(codes) // 2
-    size = groups * rows // 2
+    size = groups * rows // 2 // parts
     message = jax.ShapeDtypeStruct((size, width + LANES), I16)
-    outs = [message] * 3 + [jax.ShapeDtypeStruct((size, width), F32)]
+    outs = ([message] * 3 + [jax.ShapeDtypeStruct((size, width), F32)]) * parts
     specs = [
         pl.BlockSpec((rows, depth + LANES), functools.partial(lambda index, n: (index, 0), index))
         for _, index in codes
     ]
+    out_specs = [pl.BlockSpec(out.shape, lambda n: (0, 0)) for out in outs]
+    if fetched:
+        outs = outs + [jax.ShapeDtypeStruct(weight.shape, weight.dtype)]
+        out_specs = out_specs + [vmem()]
     return pl.pallas_call(
-        functools.partial(product_kernel, strides, groups),
+        functools.partial(product_kernel, strides, groups, int(fetched), parts),
         grid=(1,),
         out_shape=outs,
-        in_specs=specs + [vmem()],
-        out_specs=[pl.BlockSpec(out.shape, lambda n: (0, 0)) for out in outs],
+        in_specs=specs + [pl.BlockSpec(memory_space=pltpu.HBM) if fetched else vmem()],
+        out_specs=out_specs,
         scratch_shapes=[
             pltpu.VMEM((4 * groups * rows, depth), BF16),
             pltpu.VMEM((2 * groups * rows, width), F32),
             pltpu.VMEM((2 * groups * rows, LANES), F32),
-        ],
-        compiler_params=params(26),
+        ]
+        + [pltpu.SemaphoreType.DMA((width // BLOCK,))] * fetched,
+        compiler_params=params(FETCH_ROOM if fetched else 26),
         cost_estimate=pl.CostEstimate(
             flops=8 * groups * rows * depth * width,
             bytes_accessed=2 * depth * width,
@@ -321,7 +338,7 @@
     small, hidden = lax.optimization_barrier((small, hidden))
     sent = hidden.reshape(ranks, tokens // ranks, columns)
     whole = lax.all_to_all(sent, "tensor", split_axis=0, concat_axis=0, tiled=True)
-    code, weight = rotate(whole.reshape(tokens, columns), small, down_int)
+    code = rotate(whole.reshape(tokens, columns), small)
     code = code.reshape(ranks, tokens // ranks, columns + LANES)
     back = lax.all_to_all(code, "tensor", split_axis=0, concat_axis=0, tiled=True)
     own = back.reshape(tokens, columns + LANES)
@@ -335,23 +352,22 @@
     below_1, above_1 = along_x(own_1, 1), along_x(own_1, -1)
     natural, grouped = (ROWS // 2, ROWS), (2 * ROWS, ROWS // 2)
     codes = [(own, 0), (own, 1), (own_c, 0), (own_c, 1)]
-    *sends, kept_0 = product(codes, weight, natural)
+    *sends, kept_0, weight = product(codes, down_int, natural, True)
     sends, below_0, above_0 = lax.optimization_barrier((sends, below_0, above_0))
     got_0 = along_y(sends)
-    far_0, far_1 = along_x(own_0, 2), along_x(own_1, 2)
     codes = [above_0, other_core(above_0), below_0, other_core(below_0)]
     *sends, kept_1 = product([(code, 0) for code in codes], weight, grouped)
-    sends, below_1, above_1 = lax.optimization_barrier((sends, below_1, above_1))
+    sends, below_0, below_1, above_1 = lax.optimization_barrier((sends, below_0, below_1, above_1))
     got_1 = along_y(sends)
+    far_0, far_1 = along_x(below_0, 1), along_x(above_1, -1)
     codes = [above_1, other_core(above_1), below_1, other_core(below_1)]
     *sends, kept_2 = product([(code, 0) for code in codes], weight, grouped)
-    sends, far_0 = lax.optimization_barrier((sends, far_0))
+    sends, far_0, far_1 = lax.optimization_barrier((sends, far_0, far_1))
     got_2 = along_y(sends)
-    *sends, kept_a = product([(far_0, 0), (other_core(far_0), 0)], weight, grouped)
-    sends, far_1 = lax.optimization_barrier((sends, far_1))
-    got_a = along_y(sends)
-    *sends, kept_b = product([(far_1, 0), (other_core(far_1), 0)], weight, grouped)
-    got_b = along_y(sends)
+    codes = [far_0, other_core(far_0), far_1, other_core(far_1)]
+    outs = product([(code, 0) for code in codes], weight, grouped, parts=2)
+    got_a, got_b = along_y(outs[:3]), along_y(outs[4:7])
+    kept_a, kept_b = outs[3], outs[7]
     *sends, own_a = collect(0, [kept_0, *got_0], [kept_1, *got_1], [kept_a, *got_a])
     end_a = along_z(sends)
     *sends, own_b = collect(1, [kept_0, *got_0], [kept_2, *got_2], [kept_b, *got_b])

time: 163 us -> 161 us (0.988)
  starting transfers between devices: 29.6 us -> 27.9 us
    ppermute x15, waiting for transfers between devices: 24.4 us -> 31.8 us  [along_y(): got.append(lax.ppermute(block, 'tensor', route))]
    ppermute x6, waiting for transfers between devices: 13 us -> 6.96 us  [along_x(): lax.ppermute(block, 'seq', [(i, (i + 2 * apart) % 8) for i in range(8)])]
    ppermute x6, starting transfers between devices: 8.01 us -> 4.42 us  [along_z(): lax.ppermute(block, 'tensor', [(i, (i + 4 * apart) % 16) for i in range(1...]
    pallas_call x6 -> x5, Pallas kernels: 43.3 us -> 42.8 us  [the longest x4 39.2 us: product(): pl.pallas_call(functools.partial(product_kernel, strides, groups, int(fet...]
  transfers between devices with their start and end apart: 34 -> 34, of which waited for: 17 -> 15; matrix products, arithmetic and copies ran while one was open for 0% -> 0% of each run, Pallas kernels for 25% -> 25%
where the time goes in v3:
time: 161 us
  Pallas kernels  45.5 us (28%)
  waiting for transfers between devices  44.5 us (28%)
  blocking collectives  40.9 us (25%)
  starting transfers between devices  27.9 us (17%)
    pallas_call x4, Pallas kernels, product(): pl.pallas_call(functools.partial(product_kernel, strides, groups, int(fet...  39.2 us
    ppermute x15, waiting for transfers between devices, along_y(): got.append(lax.ppermute(block, 'tensor', route))  31.8 us
    all_to_all x1, blocking collectives, step(): lax.all_to_all(sent, 'tensor', split_axis=0, concat_axis=0, tiled=True)  23.2 us
    all_to_all x1, blocking collectives, step(): lax.all_to_all(code, 'tensor', split_axis=0, concat_axis=0, tiled=True)  17.7 us
    ppermute x15, starting transfers between devices, along_y(): got.append(lax.ppermute(block, 'tensor', route))  15 us
    ppermute x6, waiting for transfers between devices, along_x(): lax.ppermute(block, 'seq', [(i, (i + 2 * apart) % 8) for i in range(8)])  6.96 us
    ppermute x6, starting transfers between devices, along_x(): lax.ppermute(block, 'seq', [(i, (i + 2 * apart) % 8) for i in range(8)])  6.88 us
    ppermute x6, waiting for transfers between devices, along_z(): lax.ppermute(block, 'tensor', [(i, (i + 4 * apart) % 16) for i in range(1...  5.69 us
  transfers between devices with their start and end apart: 34, of which 15 were waited for; matrix products, arithmetic and copies ran while one was open for 0% of the time, Pallas kernels for 25%

profile of v3, /device:TPU:0, one launch (start us, length us, event | category | flops | bytes accessed | tf_op | source)
XLA Modules:
  0.0 161.0 jit_solution(16284412147949814791)
XLA Ops:
  1.4 23.2 %all_to_all.10 = bf16[16,8,3328]{2,1,0:T(8,128)(2,1)S(1)} all-to-all(bf16[16,8,3328]{2,1,0:T(8,128)(2,1)} %bitcast.16), channel_id=1, replica_groups=mesh['seq'=8,'tensor'=16] {'tensor'}, dimensions={0} | all-to-all | bytes 1703936 | tf_op jit(solution)/shard_map/all_to_all | solution.py:340
  24.6 3.7 %rotate.1 = s16[128,3456]{1,0:T(8,128)(2,1)S(1)} custom-call(bf16[128,3328]{1,0:T(8,128)(2,1)S(1)} %bitcast.14, bf16[52,52]{1,0:T(8,128)(2,1)S(1)} %convert_element_type.9.had_ref), custom_call_target="tpu_custom_call" | custom-call | tf_op jit(solution)/shard_map/rotate/pallas_call | solution.py:132
  28.3 17.7 %all_to_all.11 = s16[16,8,3456]{2,1,0:T(8,128)(2,1)S(1)} all-to-all(s16[16,8,3456]{2,1,0:T(8,128)(2,1)S(1)} %bitcast.13), channel_id=1, replica_groups=mesh['seq'=8,'tensor'=16] {'tensor'}, dimensions={0} | all-to-all | bytes 1769472 | tf_op jit(solution)/shard_map/all_to_all | solution.py:343
  46.0 2.8 %collective-permute-start.2 = (s16[64,3456]{1,0:T(8,128)(2,1)S(1)}, s16[64,3456]{1,0:T(8,128)(2,1)S(1)}, u32[]{:S(2)}, u32[]{:S(2)}) collective-permute-start(s16[64,3456]{1,0:T(8,128)(2,1)S(1)} %bitcast.19), channel_id=1, source_target_pairs={{0,96},{16,112},{32,0},{48,16},{64,32},{80,48},{96,64},{112,80},{1... | collective-permute-start | bytes 1327112 | tf_op jit(solution)/shard_map/ppermute | solution.py:312
  48.9 11.2 %shard_map.59 = (s16[64,2176]{1,0:T(8,128)(2,1)S(1)}, s16[64,2176]{1,0:T(8,128)(2,1)S(1)}, s16[64,2176]{1,0:T(8,128)(2,1)S(1)}, f32[64,2048]{1,0:T(8,128)S(1)}, bf16[3328,2048]{1,0:T(8,128)(2,1)S(1)}) custom-call(s16[128,3456]{1,0:T(8,128)(2,1)S(1)} %bitcast.10, s16[128,3456]{1,0:T(8,128)(2,1)S(1)} %bitcast.11, ...), custom_call_target="tpu_custom_call" | custom-call | flops 6979321856 | bytes 13631488 | tf_op jit(solution)/shard_map/pallas_call | solution.py:216
  60.1 2.3 %collective-permute-done.1.refs_2_ = s16[64,3456]{1,0:T(8,128)(2,1)S(1)} collective-permute-done((s16[64,3456]{1,0:T(8,128)(2,1)S(1)}, s16[64,3456]{1,0:T(8,128)(2,1)S(1)}, u32[]{:S(2)}, u32[]{:S(2)}) %collective-permute-start.1) | collective-permute-done | bytes 442400 | tf_op jit(solution)/shard_map/ppermute | solution.py:312
  64.9 9.3 %shard_map.60 = (s16[64,2176]{1,0:T(8,128)(2,1)S(1)}, s16[64,2176]{1,0:T(8,128)(2,1)S(1)}, s16[64,2176]{1,0:T(8,128)(2,1)S(1)}, f32[64,2048]{1,0:T(8,128)S(1)}) custom-call(s16[64,3456]{1,0:T(8,128)(2,1)S(1)} %collective-permute-done.2.refs_0_, s16[64,3456]{1,0:T(8,128)(2,1)S(1)} %collective-permute-done.6.refs_1_, ...), custom_call_target="tpu_custom_call" | custom-call | flops 6979321856 | bytes 13631488 | tf_op jit(solution)/shard_map/pallas_call | solution.py:216
  75.0 2.0 %collective-permute-done.8.refs_2_ = s16[64,3456]{1,0:T(8,128)(2,1)S(1)} collective-permute-done((s16[64,3456]{1,0:T(8,128)(2,1)S(1)}, s16[64,3456]{1,0:T(8,128)(2,1)S(1)}, u32[]{:S(2)}, u32[]{:S(2)}) %collective-permute-start.8) | collective-permute-done | bytes 442400 | tf_op jit(solution)/shard_map/ppermute | solution.py:312
  77.8 1.7 %collective-permute-start.15 = (s16[64,3456]{1,0:T(8,128)(2,1)S(1)}, s16[64,3456]{1,0:T(8,128)(2,1)S(1)}, u32[]{:S(2)}, u32[]{:S(2)}) collective-permute-start(s16[64,3456]{1,0:T(8,128)(2,1)S(1)} %collective-permute-done.1.refs_2_), channel_id=1, source_target_pairs={{0,32},{16,48},{32,64},{48,80},{64,96},{80,112},{96,0},{112,16},{1... | collective-permute-start | bytes 1327112 | tf_op jit(solution)/shard_map/ppermute | solution.py:312
  79.5 9.3 %shard_map.61 = (s16[64,2176]{1,0:T(8,128)(2,1)S(1)}, s16[64,2176]{1,0:T(8,128)(2,1)S(1)}, s16[64,2176]{1,0:T(8,128)(2,1)S(1)}, f32[64,2048]{1,0:T(8,128)S(1)}) custom-call(s16[64,3456]{1,0:T(8,128)(2,1)S(1)} %collective-permute-done.9.refs_0_, s16[64,3456]{1,0:T(8,128)(2,1)S(1)} %collective-permute-done.13.refs_1_, ...), custom_call_target="tpu_custom_call" | custom-call | flops 6979321856 | bytes 13631488 | tf_op jit(solution)/shard_map/pallas_call | solution.py:216
  88.9 1.9 %collective-permute-done.15.refs_0_ = s16[64,3456]{1,0:T(8,128)(2,1)S(1)} collective-permute-done((s16[64,3456]{1,0:T(8,128)(2,1)S(1)}, s16[64,3456]{1,0:T(8,128)(2,1)S(1)}, u32[]{:S(2)}, u32[]{:S(2)}) %collective-permute-start.15) | collective-permute-done | bytes 442400 | tf_op jit(solution)/shard_map/ppermute | solution.py:312
  93.3 1.5 collective-permute-start.5
  94.7 12.4 %collective-permute-done.3.refs_1_ = s16[64,2176]{1,0:T(8,128)(2,1)S(1)} collective-permute-done((s16[64,2176]{1,0:T(8,128)(2,1)S(1)}, s16[64,2176]{1,0:T(8,128)(2,1)S(1)}, u32[]{:S(2)}, u32[]{:S(2)}) %collective-permute-start.3) | collective-permute-done | bytes 278560 | tf_op jit(solution)/shard_map/ppermute | solution.py:330
  108.2 2.3 %collective-permute-start.12 = (s16[64,2176]{1,0:T(8,128)(2,1)S(1)}, s16[64,2176]{1,0:T(8,128)(2,1)S(1)}, u32[]{:S(2)}, u32[]{:S(2)}) collective-permute-start(s16[64,2176]{1,0:T(8,128)(2,1)S(1)} %get-tuple-element.67), channel_id=1, source_target_pairs={{0,3},{1,0},{2,1},{3,2},{4,7},{5,4},{6,5},{7,6},{8,11},{9,8},{10,9... | collective-permute-start | bytes 835592 | tf_op jit(solution)/shard_map/ppermute | solution.py:330
  111.3 2.1 %collective-permute-start.26 = (s16[64,2176]{1,0:T(8,128)(2,1)S(1)}, s16[64,2176]{1,0:T(8,128)(2,1)S(1)}, u32[]{:S(2)}, u32[]{:S(2)}) collective-permute-start(s16[64,2176]{1,0:T(8,128)(2,1)S(1)} %get-tuple-element.86), channel_id=1, source_target_pairs={{0,2},{1,3},{2,0},{3,1},{4,6},{5,7},{6,4},{7,5},{8,10},{9,11},{10,... | collective-permute-start | bytes 835592 | tf_op jit(solution)/shard_map/ppermute | solution.py:330
  113.4 9.3 %shard_map.62 = (s16[32,2176]{1,0:T(8,128)(2,1)S(1)}, s16[32,2176]{1,0:T(8,128)(2,1)S(1)}, s16[32,2176]{1,0:T(8,128)(2,1)S(1)}, f32[32,2048]{1,0:T(8,128)S(1)}, ...) custom-call(s16[64,3456]{1,0:T(8,128)(2,1)S(1)} %collective-permute-, ...), custom_call_target="tpu_custom_call" | custom-call | flops 6979321856 | bytes 13631488 | tf_op jit(solution)/shard_map/pallas_call | solution.py:216
  123.8 1.7 %collective-permute-start.27 = (s16[64,2176]{1,0:T(8,128)(2,1)S(1)}, s16[64,2176]{1,0:T(8,128)(2,1)S(1)}, u32[]{:S(2)}, u32[]{:S(2)}) collective-permute-start(s16[64,2176]{1,0:T(8,128)(2,1)S(1)} %get-tuple-element.87), channel_id=1, source_target_pairs={{0,3},{1,0},{2,1},{3,2},{4,7},{5,4},{6,5},{7,6},{8,11},{9,8},{10,9... | collective-permute-start | bytes 835592 | tf_op jit(solution)/shard_map/ppermute | solution.py:330
  127.1 10.6 %collective-permute-done.25.refs_5_ = s16[64,2176]{1,0:T(8,128)(2,1)S(1)} collective-permute-done((s16[64,2176]{1,0:T(8,128)(2,1)S(1)}, s16[64,2176]{1,0:T(8,128)(2,1)S(1)}, u32[]{:S(2)}, u32[]{:S(2)}) %collective-permute-start.25) | collective-permute-done | bytes 278560 | tf_op jit(solution)/shard_map/ppermute | solution.py:330
  137.8 1.7 %collective-permute-done.19.refs_9_ = s16[32,2176]{1,0:T(8,128)(2,1)S(1)} collective-permute-done((s16[32,2176]{1,0:T(8,128)(2,1)S(1)}, s16[32,2176]{1,0:T(8,128)(2,1)S(1)}, u32[]{:S(2)}, u32[]{:S(2)}) %collective-permute-start.19) | collective-permute-done | bytes 139296 | tf_op jit(solution)/shard_map/ppermute | solution.py:330
  140.5 2.5 %collective-permute-done.21.refs_11_ = s16[32,2176]{1,0:T(8,128)(2,1)S(1)} collective-permute-done((s16[32,2176]{1,0:T(8,128)(2,1)S(1)}, s16[32,2176]{1,0:T(8,128)(2,1)S(1)}, u32[]{:S(2)}, u32[]{:S(2)}) %collective-permute-start.21) | collective-permute-done | bytes 139296 | tf_op jit(solution)/shard_map/ppermute | solution.py:330
  145.2 2.9 %collective-permute-done.28.refs_9_ = s16[32,2176]{1,0:T(8,128)(2,1)S(1)} collective-permute-done((s16[32,2176]{1,0:T(8,128)(2,1)S(1)}, s16[32,2176]{1,0:T(8,128)(2,1)S(1)}, u32[]{:S(2)}, u32[]{:S(2)}) %collective-permute-start.28) | collective-permute-done | bytes 139296 | tf_op jit(solution)/shard_map/ppermute | solution.py:330
  153.2 1.5 collective-permute-start.33
  155.8 2.8 %collective-permute-done.31.refs_5_ = s16[32,2176]{1,0:T(8,128)(2,1)S(1)} collective-permute-done((s16[32,2176]{1,0:T(8,128)(2,1)S(1)}, s16[32,2176]{1,0:T(8,128)(2,1)S(1)}, u32[]{:S(2)}, u32[]{:S(2)}) %collective-permute-start.31) | collective-permute-done | bytes 139296 | tf_op jit(solution)/shard_map/ppermute | solution.py:322
  158.7 1.4 collective-permute-done.33.refs_7_
  (60 shorter events, 22.3 us)
Async XLA Ops:
  46.0 14.0 %collective-permute-start.2 = (s16[64,3456]{1,0:T(8,128)(2,1)S(1)}, s16[64,3456]{1,0:T(8,128)(2,1)S(1)}, u32[]{:S(2)}, u32[]{:S(2)}) collective-permute-start(s16[64,3456]{1,0:T(8,128)(2,1)S(1)} %bitcast.19), channel_id=1, source_target_pairs={{0,96},{16,112},{32,0},{48,16},{64,32},{80,48},{96,64},{112,80},{1... | collective-permute-start | bytes 1327112 | tf_op jit(solution)/shard_map/ppermute | solution.py:312
  48.9 13.5 %collective-permute-start.1 = (s16[64,3456]{1,0:T(8,128)(2,1)S(1)}, s16[64,3456]{1,0:T(8,128)(2,1)S(1)}, u32[]{:S(2)}, u32[]{:S(2)}) collective-permute-start(s16[64,3456]{1,0:T(8,128)(2,1)S(1)} %bitcast.20), channel_id=1, source_target_pairs={{0,32},{16,48},{32,64},{48,80},{64,96},{80,112},{96,0},{112,16},{1... | collective-permute-start | bytes 1327112 | tf_op jit(solution)/shard_map/ppermute | solution.py:312
  62.9 12.1 %collective-permute-start.9 = (s16[64,3456]{1,0:T(8,128)(2,1)S(1)}, s16[64,3456]{1,0:T(8,128)(2,1)S(1)}, u32[]{:S(2)}, u32[]{:S(2)}) collective-permute-start(s16[64,3456]{1,0:T(8,128)(2,1)S(1)} %bitcast.17), channel_id=1, source_target_pairs={{0,96},{16,112},{32,0},{48,16},{64,32},{80,48},{96,64},{112,80},{1... | collective-permute-start | bytes 1327112 | tf_op jit(solution)/shard_map/ppermute | solution.py:312
  63.9 13.1 %collective-permute-start.8 = (s16[64,3456]{1,0:T(8,128)(2,1)S(1)}, s16[64,3456]{1,0:T(8,128)(2,1)S(1)}, u32[]{:S(2)}, u32[]{:S(2)}) collective-permute-start(s16[64,3456]{1,0:T(8,128)(2,1)S(1)} %bitcast.18), channel_id=1, source_target_pairs={{0,32},{16,48},{32,64},{48,80},{64,96},{80,112},{96,0},{112,16},{1... | collective-permute-start | bytes 1327112 | tf_op jit(solution)/shard_map/ppermute | solution.py:312
  77.5 13.3 %collective-permute-start.16 = (s16[64,3456]{1,0:T(8,128)(2,1)S(1)}, s16[64,3456]{1,0:T(8,128)(2,1)S(1)}, u32[]{:S(2)}, u32[]{:S(2)}) collective-permute-start(s16[64,3456]{1,0:T(8,128)(2,1)S(1)} %collective-permute-done.9.refs_0_), channel_id=1, source_target_pairs={{0,96},{16,112},{32,0},{48,16},{64,32},{80,48},{96,64},{112,80},{1... | collective-permute-start | bytes 1327112 | tf_op jit(solution)/shard_map/ppermute | solution.py:312
  77.8 13.0 %collective-permute-start.15 = (s16[64,3456]{1,0:T(8,128)(2,1)S(1)}, s16[64,3456]{1,0:T(8,128)(2,1)S(1)}, u32[]{:S(2)}, u32[]{:S(2)}) collective-permute-start(s16[64,3456]{1,0:T(8,128)(2,1)S(1)} %collective-permute-done.1.refs_2_), channel_id=1, source_target_pairs={{0,32},{16,48},{32,64},{48,80},{64,96},{80,112},{96,0},{112,16},{1... | collective-permute-start | bytes 1327112 | tf_op jit(solution)/shard_map/ppermute | solution.py:312
  90.8 19.7 %collective-permute-start.17 = (s16[64,3456]{1,0:T(8,128)(2,1)S(1)}, s16[64,3456]{1,0:T(8,128)(2,1)S(1)}, u32[]{:S(2)}, u32[]{:S(2)}) collective-permute-start(s16[64,3456]{1,0:T(8,128)(2,1)S(1)} %collective-permute-done.15.refs_0_), channel_id=1, source_target_pairs={{0,16},{16,0},{32,48},{48,32},{64,80},{80,64},{96,112},{112,96},{1... | collective-permute-start | bytes 1327112 | tf_op jit(solution)/shard_map/ppermute | solution.py:316
  90.8 20.5 %collective-permute-start.18 = (s16[64,3456]{1,0:T(8,128)(2,1)S(1)}, s16[64,3456]{1,0:T(8,128)(2,1)S(1)}, u32[]{:S(2)}, u32[]{:S(2)}) collective-permute-start(s16[64,3456]{1,0:T(8,128)(2,1)S(1)} %collective-permute-done.16.refs_2_), channel_id=1, source_target_pairs={{0,16},{16,0},{32,48},{48,32},{64,80},{80,64},{96,112},{112,96},{1... | collective-permute-start | bytes 1327112 | tf_op jit(solution)/shard_map/ppermute | solution.py:316
  91.3 15.8 %collective-permute-start.3 = (s16[64,2176]{1,0:T(8,128)(2,1)S(1)}, s16[64,2176]{1,0:T(8,128)(2,1)S(1)}, u32[]{:S(2)}, u32[]{:S(2)}) collective-permute-start(s16[64,2176]{1,0:T(8,128)(2,1)S(1)} %get-tuple-element.55), channel_id=1, source_target_pairs={{0,1},{1,2},{2,3},{3,0},{4,5},{5,6},{6,7},{7,4},{8,9},{9,10},{10,1... | collective-permute-start | bytes 835592 | tf_op jit(solution)/shard_map/ppermute | solution.py:330
  91.9 15.2 %collective-permute-start.4 = (s16[64,2176]{1,0:T(8,128)(2,1)S(1)}, s16[64,2176]{1,0:T(8,128)(2,1)S(1)}, u32[]{:S(2)}, u32[]{:S(2)}) collective-permute-start(s16[64,2176]{1,0:T(8,128)(2,1)S(1)} %get-tuple-element.56), channel_id=1, source_target_pairs={{0,2},{1,3},{2,0},{3,1},{4,6},{5,7},{6,4},{7,5},{8,10},{9,11},{10,... | collective-permute-start | bytes 835592 | tf_op jit(solution)/shard_map/ppermute | solution.py:330
  93.3 14.9 %collective-permute-start.5 = (s16[64,2176]{1,0:T(8,128)(2,1)S(1)}, s16[64,2176]{1,0:T(8,128)(2,1)S(1)}, u32[]{:S(2)}, u32[]{:S(2)}) collective-permute-start(s16[64,2176]{1,0:T(8,128)(2,1)S(1)} %get-tuple-element.57), channel_id=1, source_target_pairs={{0,3},{1,0},{2,1},{3,2},{4,7},{5,4},{6,5},{7,6},{8,11},{9,8},{10,9... | collective-permute-start | bytes 835592 | tf_op jit(solution)/shard_map/ppermute | solution.py:330
  107.1 16.7 %collective-permute-start.10 = (s16[64,2176]{1,0:T(8,128)(2,1)S(1)}, s16[64,2176]{1,0:T(8,128)(2,1)S(1)}, u32[]{:S(2)}, u32[]{:S(2)}) collective-permute-start(s16[64,2176]{1,0:T(8,128)(2,1)S(1)} %get-tuple-element.65), channel_id=1, source_target_pairs={{0,1},{1,2},{2,3},{3,0},{4,5},{5,6},{6,7},{7,4},{8,9},{9,10},{10,1... | collective-permute-start | bytes 835592 | tf_op jit(solution)/shard_map/ppermute | solution.py:330
  107.1 18.4 %collective-permute-start.11 = (s16[64,2176]{1,0:T(8,128)(2,1)S(1)}, s16[64,2176]{1,0:T(8,128)(2,1)S(1)}, u32[]{:S(2)}, u32[]{:S(2)}) collective-permute-start(s16[64,2176]{1,0:T(8,128)(2,1)S(1)} %get-tuple-element.66), channel_id=1, source_target_pairs={{0,2},{1,3},{2,0},{3,1},{4,6},{5,7},{6,4},{7,5},{8,10},{9,11},{10,... | collective-permute-start | bytes 835592 | tf_op jit(solution)/shard_map/ppermute | solution.py:330
  108.2 17.7 %collective-permute-start.12 = (s16[64,2176]{1,0:T(8,128)(2,1)S(1)}, s16[64,2176]{1,0:T(8,128)(2,1)S(1)}, u32[]{:S(2)}, u32[]{:S(2)}) collective-permute-start(s16[64,2176]{1,0:T(8,128)(2,1)S(1)} %get-tuple-element.67), channel_id=1, source_target_pairs={{0,3},{1,0},{2,1},{3,2},{4,7},{5,4},{6,5},{7,6},{8,11},{9,8},{10,9... | collective-permute-start | bytes 835592 | tf_op jit(solution)/shard_map/ppermute | solution.py:330
  110.5 27.3 %collective-permute-start.25 = (s16[64,2176]{1,0:T(8,128)(2,1)S(1)}, s16[64,2176]{1,0:T(8,128)(2,1)S(1)}, u32[]{:S(2)}, u32[]{:S(2)}) collective-permute-start(s16[64,2176]{1,0:T(8,128)(2,1)S(1)} %get-tuple-element.85), channel_id=1, source_target_pairs={{0,1},{1,2},{2,3},{3,0},{4,5},{5,6},{6,7},{7,4},{8,9},{9,10},{10,1... | collective-permute-start | bytes 835592 | tf_op jit(solution)/shard_map/ppermute | solution.py:330
  111.3 33.6 %collective-permute-start.26 = (s16[64,2176]{1,0:T(8,128)(2,1)S(1)}, s16[64,2176]{1,0:T(8,128)(2,1)S(1)}, u32[]{:S(2)}, u32[]{:S(2)}) collective-permute-start(s16[64,2176]{1,0:T(8,128)(2,1)S(1)} %get-tuple-element.86), channel_id=1, source_target_pairs={{0,2},{1,3},{2,0},{3,1},{4,6},{5,7},{6,4},{7,5},{8,10},{9,11},{10,... | collective-permute-start | bytes 835592 | tf_op jit(solution)/shard_map/ppermute | solution.py:330
  123.8 21.2 %collective-permute-start.27 = (s16[64,2176]{1,0:T(8,128)(2,1)S(1)}, s16[64,2176]{1,0:T(8,128)(2,1)S(1)}, u32[]{:S(2)}, u32[]{:S(2)}) collective-permute-start(s16[64,2176]{1,0:T(8,128)(2,1)S(1)} %get-tuple-element.87), channel_id=1, source_target_pairs={{0,3},{1,0},{2,1},{3,2},{4,7},{5,4},{6,5},{7,6},{8,11},{9,8},{10,9... | collective-permute-start | bytes 835592 | tf_op jit(solution)/shard_map/ppermute | solution.py:330
  125.6 13.9 %collective-permute-start.19 = (s16[32,2176]{1,0:T(8,128)(2,1)S(1)}, s16[32,2176]{1,0:T(8,128)(2,1)S(1)}, u32[]{:S(2)}, u32[]{:S(2)}) collective-permute-start(s16[32,2176]{1,0:T(8,128)(2,1)S(1)} %get-tuple-element.77), channel_id=1, source_target_pairs={{0,1},{1,2},{2,3},{3,0},{4,5},{5,6},{6,7},{7,4},{8,9},{9,10},{10,1... | collective-permute-start | bytes 417800 | tf_op jit(solution)/shard_map/ppermute | solution.py:330
  125.9 13.9 %collective-permute-start.20 = (s16[32,2176]{1,0:T(8,128)(2,1)S(1)}, s16[32,2176]{1,0:T(8,128)(2,1)S(1)}, u32[]{:S(2)}, u32[]{:S(2)}) collective-permute-start(s16[32,2176]{1,0:T(8,128)(2,1)S(1)} %get-tuple-element.78), channel_id=1, source_target_pairs={{0,2},{1,3},{2,0},{3,1},{4,6},{5,7},{6,4},{7,5},{8,10},{9,11},{10,... | collective-permute-start | bytes 417800 | tf_op jit(solution)/shard_map/ppermute | solution.py:330
  139.5 8.6 %collective-permute-start.28 = (s16[32,2176]{1,0:T(8,128)(2,1)S(1)}, s16[32,2176]{1,0:T(8,128)(2,1)S(1)}, u32[]{:S(2)}, u32[]{:S(2)}) collective-permute-start(s16[32,2176]{1,0:T(8,128)(2,1)S(1)} %get-tuple-element.89), channel_id=1, source_target_pairs={{0,1},{1,2},{2,3},{3,0},{4,5},{5,6},{6,7},{7,4},{8,9},{9,10},{10,1... | collective-permute-start | bytes 417800 | tf_op jit(solution)/shard_map/ppermute | solution.py:330
  139.8 8.5 %collective-permute-start.29 = (s16[32,2176]{1,0:T(8,128)(2,1)S(1)}, s16[32,2176]{1,0:T(8,128)(2,1)S(1)}, u32[]{:S(2)}, u32[]{:S(2)}) collective-permute-start(s16[32,2176]{1,0:T(8,128)(2,1)S(1)} %get-tuple-element.90), channel_id=1, source_target_pairs={{0,2},{1,3},{2,0},{3,1},{4,6},{5,7},{6,4},{7,5},{8,10},{9,11},{10,... | collective-permute-start | bytes 417800 | tf_op jit(solution)/shard_map/ppermute | solution.py:330
  144.9 8.3 %collective-permute-start.22 = (s16[32,2176]{1,0:T(8,128)(2,1)S(1)}, s16[32,2176]{1,0:T(8,128)(2,1)S(1)}, u32[]{:S(2)}, u32[]{:S(2)}) collective-permute-start(s16[32,2176]{1,0:T(8,128)(2,1)S(1)} %get-tuple-element.81), channel_id=1, source_target_pairs={{0,4},{1,5},{2,6},{3,7},{4,8},{5,9},{6,10},{7,11},{8,12},{9,13},{1... | collective-permute-start | bytes 417800 | tf_op jit(solution)/shard_map/ppermute | solution.py:322
  145.0 10.4 %collective-permute-start.23 = (s16[32,2176]{1,0:T(8,128)(2,1)S(1)}, s16[32,2176]{1,0:T(8,128)(2,1)S(1)}, u32[]{:S(2)}, u32[]{:S(2)}) collective-permute-start(s16[32,2176]{1,0:T(8,128)(2,1)S(1)} %get-tuple-element.82), channel_id=1, source_target_pairs={{0,8},{1,9},{2,10},{3,11},{4,12},{5,13},{6,14},{7,15},{8,0},{9,1},... | collective-permute-start | bytes 417800 | tf_op jit(solution)/shard_map/ppermute | solution.py:322
  149.7 9.0 %collective-permute-start.31 = (s16[32,2176]{1,0:T(8,128)(2,1)S(1)}, s16[32,2176]{1,0:T(8,128)(2,1)S(1)}, u32[]{:S(2)}, u32[]{:S(2)}) collective-permute-start(s16[32,2176]{1,0:T(8,128)(2,1)S(1)} %get-tuple-element.93), channel_id=1, source_target_pairs={{0,4},{1,5},{2,6},{3,7},{4,8},{5,9},{6,10},{7,11},{8,12},{9,13},{1... | collective-permute-start | bytes 417800 | tf_op jit(solution)/shard_map/ppermute | solution.py:322
  (11 other events, 115.7 us)

commit v4 on v1

--- a/solution.py
+++ b/solution.py
@@ -19,6 +19,8 @@
 CODE_TOP = 32767.0
 SUM_TOP = 32700.0
 BLOCK = 512
+FIRST = 512
+CUTS = (1024, 1792, 2560)
 ROWS = 64
 
 
@@ -157,22 +159,30 @@
     for index, ref in enumerate(codes):
         base = index * rows
         scale[base : base + rows, :] = jnp.broadcast_to(scale_of(ref[:, depth:]), (rows, LANES))
-        for tile in range(depth // LANES):
-            span = slice(tile * LANES, (tile + 1) * LANES)
-            level = ref[:, span].astype(I32).astype(F32)
-            quant = level * jnp.abs(level) * (8.0 / CODE_TOP**2)
-            high = quant.astype(BF16)
-            low = (quant - high.astype(F32)).astype(BF16)
-            lhs[base : base + rows, span] = high
-            lhs[4 * rows + base : 4 * rows + base + rows, span] = low
+    both = None
+    edges = (0, *CUTS, depth)
+    for low, high in zip(edges[:-1], edges[1:]):
+        for index, ref in enumerate(codes):
+            base = index * rows
+            for start in range(low, high, LANES):
+                span = slice(start, start + LANES)
+                level = ref[:, span].astype(I32).astype(F32)
+                quant = level * jnp.abs(level) * (8.0 / CODE_TOP**2)
+                head = quant.astype(BF16)
+                lhs[base : base + rows, span] = head
+                tail = (quant - head.astype(F32)).astype(BF16)
+                lhs[4 * rows + base : 4 * rows + base + rows, span] = tail
+        piece = jnp.dot(lhs[:, low:high], w_ref[low:high, :FIRST], preferred_element_type=F32)
+        both = piece if both is None else both + piece
+    total[:, :FIRST] = (both[: 4 * rows] + both[4 * rows :]) * scale[:, 0:1]
 
     def columns(step, carry):
-        start = pl.multiple_of(step * BLOCK, BLOCK)
+        start = pl.multiple_of(FIRST + step * BLOCK, LANES)
         both = jnp.dot(lhs[...], w_ref[:, pl.ds(start, BLOCK)], preferred_element_type=F32)
         total[:, pl.ds(start, BLOCK)] = (both[: 4 * rows] + both[4 * rows :]) * scale[:, 0:1]
         return carry
 
-    lax.fori_loop(0, width // BLOCK, columns, 0)
+    lax.fori_loop(0, (width - FIRST) // BLOCK, columns, 0)
     for group in range(2):
         chosen = outs if parts == 1 else outs[4 * group : 4 * group + 4]
         span = slice(group * size, (group + 1) * size) if parts == 1 else slice(None)
@@ -330,16 +340,16 @@
     own_0 = halves[:, 0].reshape(ROWS, columns + LANES)
     own_1 = halves[:, 1].reshape(ROWS, columns + LANES)
     below_0, above_0 = along_x(own_0, 1), along_x(own_0, -1)
-    below_1, above_1 = along_x(own_1, 1), along_x(own_1, -1)
     natural, grouped = (ROWS // 2, ROWS), (2 * ROWS, ROWS // 2)
     codes = [(own, 0), (own, 1), (own_c, 0), (own_c, 1)]
     *sends, kept_0 = product(codes, weight, natural)
-    sends, below_0, above_0 = lax.optimization_barrier((sends, below_0, above_0))
+    sends, below_0, above_0, own_1 = lax.optimization_barrier((sends, below_0, above_0, own_1))
+    below_1, above_1 = along_x(own_1, 1), along_x(own_1, -1)
     got_0 = along_y(sends)
-    far_0 = along_x(below_0, 1)
     codes = [above_0, other_core(above_0), below_0, other_core(below_0)]
     *sends, kept_1 = product([(code, 0) for code in codes], weight, grouped)
-    sends, below_1, above_1 = lax.optimization_barrier((sends, below_1, above_1))
+    sends, below_0, below_1, above_1 = lax.optimization_barrier((sends, below_0, below_1, above_1))
+    far_0 = along_x(below_0, 1)
     got_1 = along_y(sends)
     far_1 = along_x(above_1, -1)
     codes = [above_1, other_core(above_1), below_1, other_core(below_1)]

time: 163 us -> 162 us (level)
  waiting for transfers between devices: 44.3 us -> 51 us
  Pallas kernels: 44.9 us -> 40.2 us
  starting transfers between devices: 29.1 us -> 27 us
    ppermute x6, waiting for transfers between devices: 6.8 us -> 11.5 us  [along_x(): lax.ppermute(block, 'seq', [(i, (i + 2 * apart) % 8) for i in range(8)])]
    pallas_call x4, Pallas kernels: 37.3 us -> 32.7 us  [product(): pl.pallas_call(functools.partial(product_kernel, strides, parts), grid=(1...]
    ppermute x15, waiting for transfers between devices: 31.8 us -> 33.8 us  [along_y(): got.append(lax.ppermute(block, 'tensor', route))]
  transfers between devices with their start and end apart: 34 -> 34, of which waited for: 16 -> 16; matrix products, arithmetic and copies ran while one was open for 0% -> 0% of each run, Pallas kernels for 24% -> 21%
where the time goes in v4:
time: 162 us; the launch traced here: 161 us
  waiting for transfers between devices  51 us (31%)
  blocking collectives  40.9 us (25%)
  Pallas kernels  40.2 us (25%)
  starting transfers between devices  27 us (17%)
    ppermute x15, waiting for transfers between devices, along_y(): got.append(lax.ppermute(block, 'tensor', route))  33.8 us
    pallas_call x4, Pallas kernels, product(): pl.pallas_call(functools.partial(product_kernel, strides, parts), grid=(1...  32.7 us
    all_to_all x1, blocking collectives, step(): lax.all_to_all(sent, 'tensor', split_axis=0, concat_axis=0, tiled=True)  23.2 us
    all_to_all x1, blocking collectives, step(): lax.all_to_all(code, 'tensor', split_axis=0, concat_axis=0, tiled=True)  17.7 us
    ppermute x15, starting transfers between devices, along_y(): got.append(lax.ppermute(block, 'tensor', route))  14 us
    ppermute x6, waiting for transfers between devices, along_x(): lax.ppermute(block, 'seq', [(i, (i + 2 * apart) % 8) for i in range(8)])  11.5 us
    ppermute x6, starting transfers between devices, along_x(): lax.ppermute(block, 'seq', [(i, (i + 2 * apart) % 8) for i in range(8)])  6.88 us
    ppermute x6, waiting for transfers between devices, along_z(): lax.ppermute(block, 'tensor', [(i, (i + 4 * apart) % 16) for i in range(1...  5.68 us
  transfers between devices with their start and end apart: 34, of which 16 were waited for; matrix products, arithmetic and copies ran while one was open for 0% of the time, Pallas kernels for 21%

profile of v4, /device:TPU:0, one launch (start us, length us, event | category | flops | bytes accessed | tf_op | source)
XLA Modules:
  0.0 161.5 jit_solution(11529451296093370924)
XLA Ops:
  1.4 23.2 %all_to_all.10 = bf16[16,8,3328]{2,1,0:T(8,128)(2,1)S(1)} all-to-all(bf16[16,8,3328]{2,1,0:T(8,128)(2,1)} %bitcast.16), channel_id=1, replica_groups=mesh['seq'=8,'tensor'=16] {'tensor'}, dimensions={0} | all-to-all | bytes 1703936 | tf_op jit(solution)/shard_map/all_to_all | solution.py:331
  24.6 4.9 %rotate.1 = (s16[128,3456]{1,0:T(8,128)(2,1)S(1)}, bf16[3328,2048]{1,0:T(8,128)(2,1)S(1)}) custom-call(bf16[128,3328]{1,0:T(8,128)(2,1)S(1)} %bitcast.13, bf16[52,52]{1,0:T(8,128)(2,1)S(1)} %convert_element_type.9.had_ref, bf16[3328,2048]{1,0:T(8,128)(2,1)} %w_ref.1), custom_call_target="tpu_custom_call" | custom-call | tf_op jit(solution)/shard_map/rotate/pallas_call | solution.py:135
  29.5 17.7 %all_to_all.11 = s16[16,8,3456]{2,1,0:T(8,128)(2,1)S(1)} all-to-all(s16[16,8,3456]{2,1,0:T(8,128)(2,1)S(1)} %bitcast.14), channel_id=1, replica_groups=mesh['seq'=8,'tensor'=16] {'tensor'}, dimensions={0} | all-to-all | bytes 1769472 | tf_op jit(solution)/shard_map/all_to_all | solution.py:334
  47.3 2.8 %collective-permute-start.2 = (s16[64,3456]{1,0:T(8,128)(2,1)S(1)}, s16[64,3456]{1,0:T(8,128)(2,1)S(1)}, u32[]{:S(2)}, u32[]{:S(2)}) collective-permute-start(s16[64,3456]{1,0:T(8,128)(2,1)S(1)} %bitcast.19), channel_id=1, source_target_pairs={{0,96},{16,112},{32,0},{48,16},{64,32},{80,48},{96,64},{112,80},{1... | collective-permute-start | bytes 1327112 | tf_op jit(solution)/shard_map/ppermute | solution.py:303
  50.1 8.2 %shard_map.59 = (s16[64,2176]{1,0:T(8,128)(2,1)S(1)}, s16[64,2176]{1,0:T(8,128)(2,1)S(1)}, s16[64,2176]{1,0:T(8,128)(2,1)S(1)}, f32[64,2048]{1,0:T(8,128)S(1)}) custom-call(s16[128,3456]{1,0:T(8,128)(2,1)S(1)} %bitcast.10, s16[128,3456]{1,0:T(8,128)(2,1)S(1)} %bitcast.11, s16[128,3456]{1,0:T(8,128)(2,1)S(1)} %collective-permute-done.refs_2_.refs_3_, ...), custom_call_target="tpu_custom_call" | custom-call | flops 6979321856 | bytes 13631488 | tf_op jit(solution)/shard_map/pallas_call | solution.py:208
  58.3 1.9 %collective-permute-done.2.refs_0_ = s16[64,3456]{1,0:T(8,128)(2,1)S(1)} collective-permute-done((s16[64,3456]{1,0:T(8,128)(2,1)S(1)}, s16[64,3456]{1,0:T(8,128)(2,1)S(1)}, u32[]{:S(2)}, u32[]{:S(2)}) %collective-permute-start.2) | collective-permute-done | bytes 442400 | tf_op jit(solution)/shard_map/ppermute | solution.py:303
  60.2 3.4 %collective-permute-done.1.refs_2_ = s16[64,3456]{1,0:T(8,128)(2,1)S(1)} collective-permute-done((s16[64,3456]{1,0:T(8,128)(2,1)S(1)}, s16[64,3456]{1,0:T(8,128)(2,1)S(1)}, u32[]{:S(2)}, u32[]{:S(2)}) %collective-permute-start.1) | collective-permute-done | bytes 442400 | tf_op jit(solution)/shard_map/ppermute | solution.py:303
  64.4 1.7 %collective-permute-start.8 = (s16[64,3456]{1,0:T(8,128)(2,1)S(1)}, s16[64,3456]{1,0:T(8,128)(2,1)S(1)}, u32[]{:S(2)}, u32[]{:S(2)}) collective-permute-start(s16[64,3456]{1,0:T(8,128)(2,1)S(1)} %bitcast.18), channel_id=1, source_target_pairs={{0,32},{16,48},{32,64},{48,80},{64,96},{80,112},{96,0},{112,16},{1... | collective-permute-start | bytes 1327112 | tf_op jit(solution)/shard_map/ppermute | solution.py:303
  66.1 8.2 %shard_map.60 = (s16[64,2176]{1,0:T(8,128)(2,1)S(1)}, s16[64,2176]{1,0:T(8,128)(2,1)S(1)}, s16[64,2176]{1,0:T(8,128)(2,1)S(1)}, f32[64,2048]{1,0:T(8,128)S(1)}) custom-call(s16[64,3456]{1,0:T(8,128)(2,1)S(1)} %collective-permute-done.2.refs_0_, s16[64,3456]{1,0:T(8,128)(2,1)S(1)} %collective-permute-done.6.refs_1_, ...), custom_call_target="tpu_custom_call" | custom-call | flops 6979321856 | bytes 13631488 | tf_op jit(solution)/shard_map/pallas_call | solution.py:208
  74.3 1.9 %collective-permute-done.9.refs_0_ = s16[64,3456]{1,0:T(8,128)(2,1)S(1)} collective-permute-done((s16[64,3456]{1,0:T(8,128)(2,1)S(1)}, s16[64,3456]{1,0:T(8,128)(2,1)S(1)}, u32[]{:S(2)}, u32[]{:S(2)}) %collective-permute-start.9) | collective-permute-done | bytes 442400 | tf_op jit(solution)/shard_map/ppermute | solution.py:303
  78.2 1.7 %collective-permute-start.15 = (s16[64,3456]{1,0:T(8,128)(2,1)S(1)}, s16[64,3456]{1,0:T(8,128)(2,1)S(1)}, u32[]{:S(2)}, u32[]{:S(2)}) collective-permute-start(s16[64,3456]{1,0:T(8,128)(2,1)S(1)} %collective-permute-done.1.refs_2_), channel_id=1, source_target_pairs={{0,32},{16,48},{32,64},{48,80},{64,96},{80,112},{96,0},{112,16},{1... | collective-permute-start | bytes 1327112 | tf_op jit(solution)/shard_map/ppermute | solution.py:303
  79.9 8.2 %shard_map.61 = (s16[64,2176]{1,0:T(8,128)(2,1)S(1)}, s16[64,2176]{1,0:T(8,128)(2,1)S(1)}, s16[64,2176]{1,0:T(8,128)(2,1)S(1)}, f32[64,2048]{1,0:T(8,128)S(1)}) custom-call(s16[64,3456]{1,0:T(8,128)(2,1)S(1)} %collective-permute-done.9.refs_0_, s16[64,3456]{1,0:T(8,128)(2,1)S(1)} %collective-permute-done.13.refs_1_, ...), custom_call_target="tpu_custom_call" | custom-call | flops 6979321856 | bytes 13631488 | tf_op jit(solution)/shard_map/pallas_call | solution.py:208
  88.1 3.1 %collective-permute-done.15.refs_0_ = s16[64,3456]{1,0:T(8,128)(2,1)S(1)} collective-permute-done((s16[64,3456]{1,0:T(8,128)(2,1)S(1)}, s16[64,3456]{1,0:T(8,128)(2,1)S(1)}, u32[]{:S(2)}, u32[]{:S(2)}) %collective-permute-start.15) | collective-permute-done | bytes 442400 | tf_op jit(solution)/shard_map/ppermute | solution.py:303
  95.1 12.4 %collective-permute-done.3.refs_1_ = s16[64,2176]{1,0:T(8,128)(2,1)S(1)} collective-permute-done((s16[64,2176]{1,0:T(8,128)(2,1)S(1)}, s16[64,2176]{1,0:T(8,128)(2,1)S(1)}, u32[]{:S(2)}, u32[]{:S(2)}) %collective-permute-start.3) | collective-permute-done | bytes 278560 | tf_op jit(solution)/shard_map/ppermute | solution.py:321
  108.6 2.3 %collective-permute-start.12 = (s16[64,2176]{1,0:T(8,128)(2,1)S(1)}, s16[64,2176]{1,0:T(8,128)(2,1)S(1)}, u32[]{:S(2)}, u32[]{:S(2)}) collective-permute-start(s16[64,2176]{1,0:T(8,128)(2,1)S(1)} %get-tuple-element.71), channel_id=1, source_target_pairs={{0,3},{1,0},{2,1},{3,2},{4,7},{5,4},{6,5},{7,6},{8,11},{9,8},{10,9... | collective-permute-start | bytes 835592 | tf_op jit(solution)/shard_map/ppermute | solution.py:321
  111.7 2.3 %collective-permute-start.26 = (s16[64,2176]{1,0:T(8,128)(2,1)S(1)}, s16[64,2176]{1,0:T(8,128)(2,1)S(1)}, u32[]{:S(2)}, u32[]{:S(2)}) collective-permute-start(s16[64,2176]{1,0:T(8,128)(2,1)S(1)} %get-tuple-element.90), channel_id=1, source_target_pairs={{0,2},{1,3},{2,0},{3,1},{4,6},{5,7},{6,4},{7,5},{8,10},{9,11},{10,... | collective-permute-start | bytes 835592 | tf_op jit(solution)/shard_map/ppermute | solution.py:321
  114.0 8.2 %shard_map.62 = (s16[32,2176]{1,0:T(8,128)(2,1)S(1)}, s16[32,2176]{1,0:T(8,128)(2,1)S(1)}, s16[32,2176]{1,0:T(8,128)(2,1)S(1)}, f32[32,2048]{1,0:T(8,128)S(1)}, ...) custom-call(s16[64,3456]{1,0:T(8,128)(2,1)S(1)} %collective-permute-, ...), custom_call_target="tpu_custom_call" | custom-call | flops 6979321856 | bytes 13631488 | tf_op jit(solution)/shard_map/pallas_call | solution.py:208
  122.2 2.0 %collective-permute-done.10.refs_5_ = s16[64,2176]{1,0:T(8,128)(2,1)S(1)} collective-permute-done((s16[64,2176]{1,0:T(8,128)(2,1)S(1)}, s16[64,2176]{1,0:T(8,128)(2,1)S(1)}, u32[]{:S(2)}, u32[]{:S(2)}) %collective-permute-start.10) | collective-permute-done | bytes 278560 | tf_op jit(solution)/shard_map/ppermute | solution.py:321
  124.6 1.7 %collective-permute-start.19 = (s16[32,2176]{1,0:T(8,128)(2,1)S(1)}, s16[32,2176]{1,0:T(8,128)(2,1)S(1)}, u32[]{:S(2)}, u32[]{:S(2)}) collective-permute-start(s16[32,2176]{1,0:T(8,128)(2,1)S(1)} %get-tuple-element.81), channel_id=1, source_target_pairs={{0,1},{1,2},{2,3},{3,0},{4,5},{5,6},{6,7},{7,4},{8,9},{9,10},{10,1... | collective-permute-start | bytes 417800 | tf_op jit(solution)/shard_map/ppermute | solution.py:321
  126.3 11.9 %collective-permute-done.25.refs_5_ = s16[64,2176]{1,0:T(8,128)(2,1)S(1)} collective-permute-done((s16[64,2176]{1,0:T(8,128)(2,1)S(1)}, s16[64,2176]{1,0:T(8,128)(2,1)S(1)}, u32[]{:S(2)}, u32[]{:S(2)}) %collective-permute-start.25) | collective-permute-done | bytes 278560 | tf_op jit(solution)/shard_map/ppermute | solution.py:321
  138.2 1.7 %collective-permute-done.19.refs_9_ = s16[32,2176]{1,0:T(8,128)(2,1)S(1)} collective-permute-done((s16[32,2176]{1,0:T(8,128)(2,1)S(1)}, s16[32,2176]{1,0:T(8,128)(2,1)S(1)}, u32[]{:S(2)}, u32[]{:S(2)}) %collective-permute-start.19) | collective-permute-done | bytes 139296 | tf_op jit(solution)/shard_map/ppermute | solution.py:321
  140.9 2.5 %collective-permute-done.21.refs_11_ = s16[32,2176]{1,0:T(8,128)(2,1)S(1)} collective-permute-done((s16[32,2176]{1,0:T(8,128)(2,1)S(1)}, s16[32,2176]{1,0:T(8,128)(2,1)S(1)}, u32[]{:S(2)}, u32[]{:S(2)}) %collective-permute-start.21) | collective-permute-done | bytes 139296 | tf_op jit(solution)/shard_map/ppermute | solution.py:321
  145.8 2.7 %collective-permute-done.28.refs_9_ = s16[32,2176]{1,0:T(8,128)(2,1)S(1)} collective-permute-done((s16[32,2176]{1,0:T(8,128)(2,1)S(1)}, s16[32,2176]{1,0:T(8,128)(2,1)S(1)}, u32[]{:S(2)}, u32[]{:S(2)}) %collective-permute-start.28) | collective-permute-done | bytes 139296 | tf_op jit(solution)/shard_map/ppermute | solution.py:321
  156.3 2.8 %collective-permute-done.31.refs_5_ = s16[32,2176]{1,0:T(8,128)(2,1)S(1)} collective-permute-done((s16[32,2176]{1,0:T(8,128)(2,1)S(1)}, s16[32,2176]{1,0:T(8,128)(2,1)S(1)}, u32[]{:S(2)}, u32[]{:S(2)}) %collective-permute-start.31) | collective-permute-done | bytes 139296 | tf_op jit(solution)/shard_map/ppermute | solution.py:313
  (60 shorter events, 23.3 us)
Async XLA Ops:
  47.3 12.9 %collective-permute-start.2 = (s16[64,3456]{1,0:T(8,128)(2,1)S(1)}, s16[64,3456]{1,0:T(8,128)(2,1)S(1)}, u32[]{:S(2)}, u32[]{:S(2)}) collective-permute-start(s16[64,3456]{1,0:T(8,128)(2,1)S(1)} %bitcast.19), channel_id=1, source_target_pairs={{0,96},{16,112},{32,0},{48,16},{64,32},{80,48},{96,64},{112,80},{1... | collective-permute-start | bytes 1327112 | tf_op jit(solution)/shard_map/ppermute | solution.py:303
  50.1 13.5 %collective-permute-start.1 = (s16[64,3456]{1,0:T(8,128)(2,1)S(1)}, s16[64,3456]{1,0:T(8,128)(2,1)S(1)}, u32[]{:S(2)}, u32[]{:S(2)}) collective-permute-start(s16[64,3456]{1,0:T(8,128)(2,1)S(1)} %bitcast.20), channel_id=1, source_target_pairs={{0,32},{16,48},{32,64},{48,80},{64,96},{80,112},{96,0},{112,16},{1... | collective-permute-start | bytes 1327112 | tf_op jit(solution)/shard_map/ppermute | solution.py:303
  64.1 12.1 %collective-permute-start.9 = (s16[64,3456]{1,0:T(8,128)(2,1)S(1)}, s16[64,3456]{1,0:T(8,128)(2,1)S(1)}, u32[]{:S(2)}, u32[]{:S(2)}) collective-permute-start(s16[64,3456]{1,0:T(8,128)(2,1)S(1)} %bitcast.17), channel_id=1, source_target_pairs={{0,96},{16,112},{32,0},{48,16},{64,32},{80,48},{96,64},{112,80},{1... | collective-permute-start | bytes 1327112 | tf_op jit(solution)/shard_map/ppermute | solution.py:303
  64.4 13.0 %collective-permute-start.8 = (s16[64,3456]{1,0:T(8,128)(2,1)S(1)}, s16[64,3456]{1,0:T(8,128)(2,1)S(1)}, u32[]{:S(2)}, u32[]{:S(2)}) collective-permute-start(s16[64,3456]{1,0:T(8,128)(2,1)S(1)} %bitcast.18), channel_id=1, source_target_pairs={{0,32},{16,48},{32,64},{48,80},{64,96},{80,112},{96,0},{112,16},{1... | collective-permute-start | bytes 1327112 | tf_op jit(solution)/shard_map/ppermute | solution.py:303
  77.9 13.3 %collective-permute-start.16 = (s16[64,3456]{1,0:T(8,128)(2,1)S(1)}, s16[64,3456]{1,0:T(8,128)(2,1)S(1)}, u32[]{:S(2)}, u32[]{:S(2)}) collective-permute-start(s16[64,3456]{1,0:T(8,128)(2,1)S(1)} %collective-permute-done.9.refs_0_), channel_id=1, source_target_pairs={{0,96},{16,112},{32,0},{48,16},{64,32},{80,48},{96,64},{112,80},{1... | collective-permute-start | bytes 1327112 | tf_op jit(solution)/shard_map/ppermute | solution.py:303
  78.2 13.0 %collective-permute-start.15 = (s16[64,3456]{1,0:T(8,128)(2,1)S(1)}, s16[64,3456]{1,0:T(8,128)(2,1)S(1)}, u32[]{:S(2)}, u32[]{:S(2)}) collective-permute-start(s16[64,3456]{1,0:T(8,128)(2,1)S(1)} %collective-permute-done.1.refs_2_), channel_id=1, source_target_pairs={{0,32},{16,48},{32,64},{48,80},{64,96},{80,112},{96,0},{112,16},{1... | collective-permute-start | bytes 1327112 | tf_op jit(solution)/shard_map/ppermute | solution.py:303
  91.2 19.7 %collective-permute-start.17 = (s16[64,3456]{1,0:T(8,128)(2,1)S(1)}, s16[64,3456]{1,0:T(8,128)(2,1)S(1)}, u32[]{:S(2)}, u32[]{:S(2)}) collective-permute-start(s16[64,3456]{1,0:T(8,128)(2,1)S(1)} %collective-permute-done.15.refs_0_), channel_id=1, source_target_pairs={{0,16},{16,0},{32,48},{48,32},{64,80},{80,64},{96,112},{112,96},{1... | collective-permute-start | bytes 1327112 | tf_op jit(solution)/shard_map/ppermute | solution.py:307
  91.2 20.5 %collective-permute-start.18 = (s16[64,3456]{1,0:T(8,128)(2,1)S(1)}, s16[64,3456]{1,0:T(8,128)(2,1)S(1)}, u32[]{:S(2)}, u32[]{:S(2)}) collective-permute-start(s16[64,3456]{1,0:T(8,128)(2,1)S(1)} %collective-permute-done.16.refs_2_), channel_id=1, source_target_pairs={{0,16},{16,0},{32,48},{48,32},{64,80},{80,64},{96,112},{112,96},{1... | collective-permute-start | bytes 1327112 | tf_op jit(solution)/shard_map/ppermute | solution.py:307
  91.7 15.8 %collective-permute-start.3 = (s16[64,2176]{1,0:T(8,128)(2,1)S(1)}, s16[64,2176]{1,0:T(8,128)(2,1)S(1)}, u32[]{:S(2)}, u32[]{:S(2)}) collective-permute-start(s16[64,2176]{1,0:T(8,128)(2,1)S(1)} %get-tuple-element.59), channel_id=1, source_target_pairs={{0,1},{1,2},{2,3},{3,0},{4,5},{5,6},{6,7},{7,4},{8,9},{9,10},{10,1... | collective-permute-start | bytes 835592 | tf_op jit(solution)/shard_map/ppermute | solution.py:321
  92.3 15.2 %collective-permute-start.4 = (s16[64,2176]{1,0:T(8,128)(2,1)S(1)}, s16[64,2176]{1,0:T(8,128)(2,1)S(1)}, u32[]{:S(2)}, u32[]{:S(2)}) collective-permute-start(s16[64,2176]{1,0:T(8,128)(2,1)S(1)} %get-tuple-element.60), channel_id=1, source_target_pairs={{0,2},{1,3},{2,0},{3,1},{4,6},{5,7},{6,4},{7,5},{8,10},{9,11},{10,... | collective-permute-start | bytes 835592 | tf_op jit(solution)/shard_map/ppermute | solution.py:321
  93.7 14.9 %collective-permute-start.5 = (s16[64,2176]{1,0:T(8,128)(2,1)S(1)}, s16[64,2176]{1,0:T(8,128)(2,1)S(1)}, u32[]{:S(2)}, u32[]{:S(2)}) collective-permute-start(s16[64,2176]{1,0:T(8,128)(2,1)S(1)} %get-tuple-element.61), channel_id=1, source_target_pairs={{0,3},{1,0},{2,1},{3,2},{4,7},{5,4},{6,5},{7,6},{8,11},{9,8},{10,9... | collective-permute-start | bytes 835592 | tf_op jit(solution)/shard_map/ppermute | solution.py:321
  107.5 16.7 %collective-permute-start.10 = (s16[64,2176]{1,0:T(8,128)(2,1)S(1)}, s16[64,2176]{1,0:T(8,128)(2,1)S(1)}, u32[]{:S(2)}, u32[]{:S(2)}) collective-permute-start(s16[64,2176]{1,0:T(8,128)(2,1)S(1)} %get-tuple-element.69), channel_id=1, source_target_pairs={{0,1},{1,2},{2,3},{3,0},{4,5},{5,6},{6,7},{7,4},{8,9},{9,10},{10,1... | collective-permute-start | bytes 835592 | tf_op jit(solution)/shard_map/ppermute | solution.py:321
  107.6 17.1 %collective-permute-start.11 = (s16[64,2176]{1,0:T(8,128)(2,1)S(1)}, s16[64,2176]{1,0:T(8,128)(2,1)S(1)}, u32[]{:S(2)}, u32[]{:S(2)}) collective-permute-start(s16[64,2176]{1,0:T(8,128)(2,1)S(1)} %get-tuple-element.70), channel_id=1, source_target_pairs={{0,2},{1,3},{2,0},{3,1},{4,6},{5,7},{6,4},{7,5},{8,10},{9,11},{10,... | collective-permute-start | bytes 835592 | tf_op jit(solution)/shard_map/ppermute | solution.py:321
  108.6 17.7 %collective-permute-start.12 = (s16[64,2176]{1,0:T(8,128)(2,1)S(1)}, s16[64,2176]{1,0:T(8,128)(2,1)S(1)}, u32[]{:S(2)}, u32[]{:S(2)}) collective-permute-start(s16[64,2176]{1,0:T(8,128)(2,1)S(1)} %get-tuple-element.71), channel_id=1, source_target_pairs={{0,3},{1,0},{2,1},{3,2},{4,7},{5,4},{6,5},{7,6},{8,11},{9,8},{10,9... | collective-permute-start | bytes 835592 | tf_op jit(solution)/shard_map/ppermute | solution.py:321
  110.9 27.3 %collective-permute-start.25 = (s16[64,2176]{1,0:T(8,128)(2,1)S(1)}, s16[64,2176]{1,0:T(8,128)(2,1)S(1)}, u32[]{:S(2)}, u32[]{:S(2)}) collective-permute-start(s16[64,2176]{1,0:T(8,128)(2,1)S(1)} %get-tuple-element.89), channel_id=1, source_target_pairs={{0,1},{1,2},{2,3},{3,0},{4,5},{5,6},{6,7},{7,4},{8,9},{9,10},{10,1... | collective-permute-start | bytes 835592 | tf_op jit(solution)/shard_map/ppermute | solution.py:321
  111.7 33.6 %collective-permute-start.26 = (s16[64,2176]{1,0:T(8,128)(2,1)S(1)}, s16[64,2176]{1,0:T(8,128)(2,1)S(1)}, u32[]{:S(2)}, u32[]{:S(2)}) collective-permute-start(s16[64,2176]{1,0:T(8,128)(2,1)S(1)} %get-tuple-element.90), channel_id=1, source_target_pairs={{0,2},{1,3},{2,0},{3,1},{4,6},{5,7},{6,4},{7,5},{8,10},{9,11},{10,... | collective-permute-start | bytes 835592 | tf_op jit(solution)/shard_map/ppermute | solution.py:321
  124.2 21.1 %collective-permute-start.27 = (s16[64,2176]{1,0:T(8,128)(2,1)S(1)}, s16[64,2176]{1,0:T(8,128)(2,1)S(1)}, u32[]{:S(2)}, u32[]{:S(2)}) collective-permute-start(s16[64,2176]{1,0:T(8,128)(2,1)S(1)} %get-tuple-element.91), channel_id=1, source_target_pairs={{0,3},{1,0},{2,1},{3,2},{4,7},{5,4},{6,5},{7,6},{8,11},{9,8},{10,9... | collective-permute-start | bytes 835592 | tf_op jit(solution)/shard_map/ppermute | solution.py:321
  124.6 15.3 %collective-permute-start.19 = (s16[32,2176]{1,0:T(8,128)(2,1)S(1)}, s16[32,2176]{1,0:T(8,128)(2,1)S(1)}, u32[]{:S(2)}, u32[]{:S(2)}) collective-permute-start(s16[32,2176]{1,0:T(8,128)(2,1)S(1)} %get-tuple-element.81), channel_id=1, source_target_pairs={{0,1},{1,2},{2,3},{3,0},{4,5},{5,6},{6,7},{7,4},{8,9},{9,10},{10,1... | collective-permute-start | bytes 417800 | tf_op jit(solution)/shard_map/ppermute | solution.py:321
  126.3 13.9 %collective-permute-start.20 = (s16[32,2176]{1,0:T(8,128)(2,1)S(1)}, s16[32,2176]{1,0:T(8,128)(2,1)S(1)}, u32[]{:S(2)}, u32[]{:S(2)}) collective-permute-start(s16[32,2176]{1,0:T(8,128)(2,1)S(1)} %get-tuple-element.82), channel_id=1, source_target_pairs={{0,2},{1,3},{2,0},{3,1},{4,6},{5,7},{6,4},{7,5},{8,10},{9,11},{10,... | collective-permute-start | bytes 417800 | tf_op jit(solution)/shard_map/ppermute | solution.py:321
  139.9 8.6 %collective-permute-start.28 = (s16[32,2176]{1,0:T(8,128)(2,1)S(1)}, s16[32,2176]{1,0:T(8,128)(2,1)S(1)}, u32[]{:S(2)}, u32[]{:S(2)}) collective-permute-start(s16[32,2176]{1,0:T(8,128)(2,1)S(1)} %get-tuple-element.93), channel_id=1, source_target_pairs={{0,1},{1,2},{2,3},{3,0},{4,5},{5,6},{6,7},{7,4},{8,9},{9,10},{10,1... | collective-permute-start | bytes 417800 | tf_op jit(solution)/shard_map/ppermute | solution.py:321
  140.2 8.5 %collective-permute-start.29 = (s16[32,2176]{1,0:T(8,128)(2,1)S(1)}, s16[32,2176]{1,0:T(8,128)(2,1)S(1)}, u32[]{:S(2)}, u32[]{:S(2)}) collective-permute-start(s16[32,2176]{1,0:T(8,128)(2,1)S(1)} %get-tuple-element.94), channel_id=1, source_target_pairs={{0,2},{1,3},{2,0},{3,1},{4,6},{5,7},{6,4},{7,5},{8,10},{9,11},{10,... | collective-permute-start | bytes 417800 | tf_op jit(solution)/shard_map/ppermute | solution.py:321
  145.3 8.3 %collective-permute-start.22 = (s16[32,2176]{1,0:T(8,128)(2,1)S(1)}, s16[32,2176]{1,0:T(8,128)(2,1)S(1)}, u32[]{:S(2)}, u32[]{:S(2)}) collective-permute-start(s16[32,2176]{1,0:T(8,128)(2,1)S(1)} %get-tuple-element.85), channel_id=1, source_target_pairs={{0,4},{1,5},{2,6},{3,7},{4,8},{5,9},{6,10},{7,11},{8,12},{9,13},{1... | collective-permute-start | bytes 417800 | tf_op jit(solution)/shard_map/ppermute | solution.py:313
  145.4 10.4 %collective-permute-start.23 = (s16[32,2176]{1,0:T(8,128)(2,1)S(1)}, s16[32,2176]{1,0:T(8,128)(2,1)S(1)}, u32[]{:S(2)}, u32[]{:S(2)}) collective-permute-start(s16[32,2176]{1,0:T(8,128)(2,1)S(1)} %get-tuple-element.86), channel_id=1, source_target_pairs={{0,8},{1,9},{2,10},{3,11},{4,12},{5,13},{6,14},{7,15},{8,0},{9,1},... | collective-permute-start | bytes 417800 | tf_op jit(solution)/shard_map/ppermute | solution.py:313
  150.1 9.0 %collective-permute-start.31 = (s16[32,2176]{1,0:T(8,128)(2,1)S(1)}, s16[32,2176]{1,0:T(8,128)(2,1)S(1)}, u32[]{:S(2)}, u32[]{:S(2)}) collective-permute-start(s16[32,2176]{1,0:T(8,128)(2,1)S(1)} %get-tuple-element.97), channel_id=1, source_target_pairs={{0,4},{1,5},{2,6},{3,7},{4,8},{5,9},{6,10},{7,11},{8,12},{9,13},{1... | collective-permute-start | bytes 417800 | tf_op jit(solution)/shard_map/ppermute | solution.py:313
  (11 other events, 115.7 us)
